TPU v7x, 32 devices: a whole 2x2x4 slice. The times are simulated.
32 devices in a mesh: dp: 4 (over z), ctx: 2 (over x), tensor: 4 (over y, core).
Axes of the slice: x: 2, y: 2, z: 4, core: 2. Of those that a mesh axis runs over, the one named last changes fastest.
Arguments:
- hidden_in: bfloat16 [4, 1024, 768], P('dp', ('ctx', 'tensor')), may hold values from -6 to 6
- cotangent: bfloat16 [4, 1024, 768], P('dp', ('ctx', 'tensor')), may hold values from -6 to 6
- segment_ids: int32 [4, 1024], P('dp'), may hold values from 0 to 3, never falling along the last dimension, each value on 1 to 512 neighbouring positions
- attend_gain: bfloat16 [768], P('dp'), may hold values from 0.099609375 to 1.8984375
- attend_shift: bfloat16 [768], P('dp'), may hold values from -3 to 3
- feed_gain: bfloat16 [768], P('dp'), may hold values from 0.099609375 to 1.8984375
- feed_shift: bfloat16 [768], P('dp'), may hold values from -3 to 3
- project_weight: bfloat16 [768, 3, 768], P('dp', None, 'tensor'), may hold values from -4 to 4
- project_bias: bfloat16 [3, 12, 64], P(None, 'tensor', 'dp'), may hold values from -3 to 3
- output_weight: bfloat16 [768, 768], P('tensor', 'dp'), may hold values from -0.875 to 0.875
- output_bias: bfloat16 [768], P('dp'), may hold values from -3 to 3
- upward_weight: bfloat16 [768, 3072], P('dp', 'tensor'), may hold values from -0.21875 to 0.21875
- upward_bias: bfloat16 [4, 768], P('tensor', 'dp'), may hold values from -3 to 3
- downward_weight: bfloat16 [3072, 768], P('tensor', 'dp'), may hold values from -0.109375 to 0.109375
- downward_bias: bfloat16 [768], P('dp'), may hold values from -3 to 3
Outputs:
- hidden_out: bfloat16 [4, 1024, 768], P('dp', ('ctx', 'tensor'))
- hidden_grad: bfloat16 [4, 1024, 768], P('dp', ('ctx', 'tensor'))
- attend_gain_grad: float32 [768], P('dp')
- attend_shift_grad: float32 [768], P('dp')
- feed_gain_grad: float32 [768], P('dp')
- feed_shift_grad: float32 [768], P('dp')
- project_weight_grad: float32 [768, 3, 768], P('dp', None, 'tensor')
- project_bias_grad: float32 [3, 12, 64], P(None, 'tensor', 'dp')
- output_weight_grad: float32 [768, 768], P('tensor', 'dp')
- output_bias_grad: float32 [768], P('dp')
- upward_weight_grad: float32 [768, 3072], P('dp', 'tensor')
- upward_bias_grad: float32 [4, 768], P('tensor', 'dp')
- downward_weight_grad: float32 [3072, 768], P('tensor', 'dp')
- downward_bias_grad: float32 [768], P('dp')
Inputs may be any that keep to these rules, and one draw needn't show every extreme that they name: `segment_ids`: along each sequence the ids never fall; each of the 4 documents spans 1 to 512 tokens and one spans exactly 512.
All inputs are finite; a program needn't handle non-finite values.
Results may differ from a plain program's by a relative error of at most 0.013.
Values may be sent and summed in bfloat16 or wider, within the bound.
No kernel may reach another device: no remote copies, remote signals or barrier semaphores. Data moves between devices by JAX's collectives and lax.ppermute only.
A program may use at most 64 MiB of HBM per device.

v0:
```python
import math

import jax
import jax.numpy as jnp
from jax import lax
from jax.sharding import PartitionSpec as P

D = 768
HD = 64
ROT = 16


epsilon = 1e-05
masked_score = -1e30


def passed_along(block, axis, distance):
    devices = range(lax.axis_size(axis))
    route = [(i - distance, i) for i in devices if i - distance in devices]
    return lax.ppermute(block, axis, route)


def normalize(values):
    average = jnp.mean(values, axis=-1, keepdims=True)
    centred = values - average
    variance = jnp.mean(centred * centred, axis=-1, keepdims=True)
    inverse = lax.rsqrt(variance + epsilon)
    return (centred * inverse, inverse)


def rotary_tables(positions):
    half_rot = ROT // 2
    frequency = 10000.0 ** (-2.0 * jnp.arange(half_rot, dtype=jnp.float32) / ROT)
    angles = positions.astype(jnp.float32)[:, None] * frequency[None, :]
    return (jnp.cos(angles), jnp.sin(angles))


def rotate(tensor, cosine, sine_table, direction):
    half_rot = ROT // 2
    first_half = tensor[..., :half_rot]
    second_half = tensor[..., half_rot:ROT]
    cosine_wide = cosine[:, None, :]
    sine_wide = direction * sine_table[:, None, :]
    return jnp.concatenate(
        [
            first_half * cosine_wide - second_half * sine_wide,
            second_half * cosine_wide + first_half * sine_wide,
            tensor[..., ROT:],
        ],
        axis=-1,
    )


def gelu_pair(preact):
    cumulative = 0.5 * (1.0 + jax.scipy.special.erf(preact * 0.7071067811865476))
    density = jnp.exp(-0.5 * preact * preact) * 0.3989422804014327
    return (preact * cumulative, cumulative + preact * density)


def masked_scores(queries, keys_all, allowed, score_scale):
    scores = (
        jnp.einsum("qhd,khd->hqk", queries, keys_all, preferred_element_type=jnp.float32)
        * score_scale
    )
    return jnp.where(allowed[None], scores, masked_score)


def attend_forward(queries, keys_all, values_all, allowed, score_scale):
    scores = masked_scores(queries, keys_all, allowed, score_scale)
    highest = jnp.max(scores, axis=-1, keepdims=True)
    exponent = jnp.exp(scores - highest)
    row_sum = jnp.sum(exponent, axis=-1, keepdims=True)
    log_total = highest + jnp.log(row_sum)
    weights = (exponent / row_sum).astype(jnp.bfloat16)
    attended = jnp.einsum("hqk,khd->qhd", weights, values_all, preferred_element_type=jnp.float32)
    return (attended, log_total)


def attend_backward(
    queries, keys_all, values_all, allowed, log_total, grad_att, row_delta, score_scale
):
    scores = masked_scores(queries, keys_all, allowed, score_scale)
    probabilities = jnp.exp(scores - log_total)
    probs_b = probabilities.astype(jnp.bfloat16)
    grad_values = jnp.einsum("hqk,qhd->khd", probs_b, grad_att, preferred_element_type=jnp.float32)
    grad_probs = jnp.einsum(
        "qhd,khd->hqk", grad_att, values_all, preferred_element_type=jnp.float32
    )
    grad_scores = (probabilities * (grad_probs - row_delta)).astype(jnp.bfloat16)
    grad_queries = (
        jnp.einsum("hqk,khd->qhd", grad_scores, keys_all, preferred_element_type=jnp.float32)
        * score_scale
    )
    grad_keys = (
        jnp.einsum("hqk,qhd->khd", grad_scores, queries, preferred_element_type=jnp.float32)
        * score_scale
    )
    return (grad_queries, grad_keys, grad_values)


def body(
    hidden_in,
    cotangent,
    segment_ids,
    attend_gain,
    attend_shift,
    feed_gain,
    feed_shift,
    project_weight,
    project_bias,
    output_weight,
    output_bias,
    upward_weight,
    upward_bias,
    downward_weight,
    downward_bias,
):
    gathered = (
        lax.all_gather(attend_gain, "dp", axis=0, tiled=True),
        lax.all_gather(attend_shift, "dp", axis=0, tiled=True),
        lax.all_gather(feed_gain, "dp", axis=0, tiled=True),
        lax.all_gather(feed_shift, "dp", axis=0, tiled=True),
        lax.all_gather(project_weight, "dp", axis=0, tiled=True),
        lax.all_gather(project_bias, "dp", axis=2, tiled=True),
        lax.all_gather(output_weight, "dp", axis=1, tiled=True),
        lax.all_gather(output_bias, "dp", axis=0, tiled=True),
        lax.all_gather(upward_weight, "dp", axis=0, tiled=True),
        lax.all_gather(upward_bias, "dp", axis=1, tiled=True),
        lax.all_gather(downward_weight, "dp", axis=1, tiled=True),
        lax.all_gather(downward_bias, "dp", axis=0, tiled=True),
    )
    (
        gain_one,
        shift_one,
        gain_two,
        shift_two,
        weight_project,
        bias_project,
        weight_output,
        bias_output,
        weight_upward,
        bias_upward,
        weight_downward,
        bias_downward,
    ) = gathered
    score_scale = 1.0 / math.sqrt(HD)
    local_width = weight_project.shape[2]
    local_heads = local_width // HD
    gain_first = gain_one.astype(jnp.float32)
    gain_second = gain_two.astype(jnp.float32)
    source = hidden_in[0].astype(jnp.float32)
    normed, inverse = normalize(source)
    first_in = (normed * gain_first + shift_one.astype(jnp.float32)).astype(jnp.bfloat16)
    second_in = (normed * gain_second + shift_two.astype(jnp.float32)).astype(jnp.bfloat16)
    first_all, second_all = (
        lax.all_gather(first_in, "tensor", axis=0, tiled=True),
        lax.all_gather(second_in, "tensor", axis=0, tiled=True),
    )
    span_len = first_all.shape[0]
    project_flat = weight_project.reshape(D, 3 * local_width)
    projected = jnp.dot(first_all, project_flat, preferred_element_type=jnp.float32).reshape(
        span_len, 3, local_heads, HD
    )
    bias_proj = bias_project.astype(jnp.float32)
    ctx_index = lax.axis_index("ctx")
    positions = ctx_index * span_len + jnp.arange(span_len, dtype=jnp.int32)
    cosine, sine_table = rotary_tables(positions)
    queries = rotate(projected[:, 0] + bias_proj[0], cosine, sine_table, 1.0).astype(jnp.bfloat16)
    keys_own = rotate(projected[:, 1] + bias_proj[1], cosine, sine_table, 1.0).astype(jnp.bfloat16)
    values_own = (projected[:, 2] + bias_proj[2]).astype(jnp.bfloat16)
    keys_prior, values_prior = passed_along((keys_own, values_own), "ctx", 1)
    sequence_ids = segment_ids[0]
    own_start = ctx_index * span_len
    prior_start = jnp.maximum(own_start - span_len, 0)
    own_segments = lax.dynamic_slice_in_dim(sequence_ids, own_start, span_len)
    prior_segments = lax.dynamic_slice_in_dim(sequence_ids, prior_start, span_len)
    allow_own = (positions[None, :] <= positions[:, None]) & (
        own_segments[:, None] == own_segments[None, :]
    )
    allow_prior = (ctx_index > 0) & (own_segments[:, None] == prior_segments[None, :])
    keys_both = jnp.concatenate([keys_prior, keys_own], axis=0)
    values_both = jnp.concatenate([values_prior, values_own], axis=0)
    allow_both = jnp.concatenate([allow_prior, allow_own], axis=1)
    attended, log_total = attend_forward(queries, keys_both, values_both, allow_both, score_scale)
    attended_b = attended.astype(jnp.bfloat16)
    attended_flat = attended_b.reshape(span_len, local_width)
    preact = jnp.dot(
        second_all, weight_upward, preferred_element_type=jnp.float32
    ) + bias_upward.reshape(-1).astype(jnp.float32)
    activated, slope = gelu_pair(preact)
    hidden_act = activated.astype(jnp.bfloat16)
    mixed = lax.psum_scatter(
        jnp.dot(attended_flat, weight_output, preferred_element_type=jnp.float32)
        + jnp.dot(hidden_act, weight_downward, preferred_element_type=jnp.float32),
        "tensor",
        scatter_dimension=0,
        tiled=True,
    )
    bias_sum = bias_output.astype(jnp.float32) + bias_downward.astype(jnp.float32)
    hidden_out = (source + mixed + bias_sum).astype(jnp.bfloat16)[None]
    grad_rows = cotangent[0]
    grad_all = lax.all_gather(grad_rows, "tensor", axis=0, tiled=True)
    bias_grad = jnp.sum(grad_rows.astype(jnp.float32), axis=0)
    grad_down = jnp.dot(hidden_act.T, grad_all, preferred_element_type=jnp.float32)
    grad_outw = jnp.dot(attended_flat.T, grad_all, preferred_element_type=jnp.float32)
    grad_pre = jnp.dot(grad_all, weight_downward.T, preferred_element_type=jnp.float32) * slope
    grad_pre_b = grad_pre.astype(jnp.bfloat16)
    grad_up = jnp.dot(second_all.T, grad_pre_b, preferred_element_type=jnp.float32)
    grad_upbias = jnp.sum(grad_pre, axis=0)
    grad_att = (
        jnp.dot(grad_all, weight_output.T, preferred_element_type=jnp.float32)
        .astype(jnp.bfloat16)
        .reshape(span_len, local_heads, HD)
    )
    row_delta = jnp.sum(grad_att.astype(jnp.float32) * attended_b.astype(jnp.float32), axis=-1).T[
        :, :, None
    ]
    grad_queries, grad_keys, grad_values = attend_backward(
        queries, keys_both, values_both, allow_both, log_total, grad_att, row_delta, score_scale
    )
    grad_queries, keys_back, values_back, keys_local, values_local = (
        grad_queries,
        grad_keys[:span_len],
        grad_values[:span_len],
        grad_keys[span_len:],
        grad_values[span_len:],
    )
    keys_later, values_later = passed_along((keys_back, values_back), "ctx", -1)
    grad_keys = rotate(keys_local + keys_later, cosine, sine_table, -1.0)
    grad_values = values_local + values_later
    grad_queries = rotate(grad_queries, cosine, sine_table, -1.0)
    grad_proj = (
        jnp.stack([grad_queries, grad_keys, grad_values], axis=1)
        .astype(jnp.bfloat16)
        .reshape(span_len, 3 * local_width)
    )
    grad_pbias = jnp.stack(
        [jnp.sum(grad_queries, axis=0), jnp.sum(grad_keys, axis=0), jnp.sum(grad_values, axis=0)]
    )
    grad_project = jnp.dot(first_all.T, grad_proj, preferred_element_type=jnp.float32).reshape(
        D, 3, local_width
    )
    first_part = jnp.dot(grad_proj, project_flat.T, preferred_element_type=jnp.float32)
    second_part = jnp.dot(grad_pre_b, weight_upward.T, preferred_element_type=jnp.float32)
    both_grads = lax.psum_scatter(
        jnp.concatenate([first_part, second_part], axis=1),
        "tensor",
        scatter_dimension=0,
        tiled=True,
    )
    grad_first = both_grads[:, :D]
    grad_second = both_grads[:, D:]
    small_grads = lax.psum(
        (
            jnp.sum(grad_first * normed, axis=0),
            jnp.sum(grad_first, axis=0),
            jnp.sum(grad_second * normed, axis=0),
            jnp.sum(grad_second, axis=0),
            bias_grad,
        ),
        ("ctx", "tensor"),
    )
    grad_normed = grad_first * gain_first + grad_second * gain_second
    grad_inner = inverse * (
        grad_normed
        - jnp.mean(grad_normed, axis=-1, keepdims=True)
        - normed * jnp.mean(grad_normed * normed, axis=-1, keepdims=True)
    )
    hidden_grad = (grad_rows.astype(jnp.float32) + grad_inner).astype(jnp.bfloat16)[None]
    upbias_row = grad_upbias[None]
    large_grads = lax.psum(
        (grad_project, grad_pbias, grad_outw, grad_up, upbias_row, grad_down), "ctx"
    )
    shares = (
        lax.psum_scatter(large_grads[0], "dp", scatter_dimension=0, tiled=True),
        lax.psum_scatter(large_grads[1], "dp", scatter_dimension=2, tiled=True),
        lax.psum_scatter(large_grads[2], "dp", scatter_dimension=1, tiled=True),
        lax.psum_scatter(large_grads[3], "dp", scatter_dimension=0, tiled=True),
        lax.psum_scatter(large_grads[4], "dp", scatter_dimension=1, tiled=True),
        lax.psum_scatter(large_grads[5], "dp", scatter_dimension=1, tiled=True),
        lax.psum_scatter(small_grads[0], "dp", scatter_dimension=0, tiled=True),
        lax.psum_scatter(small_grads[1], "dp", scatter_dimension=0, tiled=True),
        lax.psum_scatter(small_grads[2], "dp", scatter_dimension=0, tiled=True),
        lax.psum_scatter(small_grads[3], "dp", scatter_dimension=0, tiled=True),
        lax.psum_scatter(small_grads[4], "dp", scatter_dimension=0, tiled=True),
    )
    return (
        hidden_out,
        hidden_grad,
        shares[6],
        shares[7],
        shares[8],
        shares[9],
        shares[0],
        shares[1],
        shares[2],
        shares[10],
        shares[3],
        shares[4],
        shares[5],
        shares[10],
    )


def solution(mesh):
    in_specs = (
        P("dp", ("ctx", "tensor"), None),
        P("dp", ("ctx", "tensor"), None),
        P("dp", None),
        P("dp"),
        P("dp"),
        P("dp"),
        P("dp"),
        P("dp", None, "tensor"),
        P(None, "tensor", "dp"),
        P("tensor", "dp"),
        P("dp"),
        P("dp", "tensor"),
        P("tensor", "dp"),
        P("tensor", "dp"),
        P("dp"),
    )
    out_specs = (
        P("dp", ("ctx", "tensor"), None),
        P("dp", ("ctx", "tensor"), None),
        P("dp"),
        P("dp"),
        P("dp"),
        P("dp"),
        P("dp", None, "tensor"),
        P(None, "tensor", "dp"),
        P("tensor", "dp"),
        P("dp"),
        P("dp", "tensor"),
        P("tensor", "dp"),
        P("tensor", "dp"),
        P("dp"),
    )
    return jax.shard_map(body, mesh=mesh, in_specs=in_specs, out_specs=out_specs, check_vma=False)
```

profile of v0, /device:TPU:0, one launch (start us, length us, event | category | flops | bytes accessed | tf_op | source)
XLA Modules:
  0.0 517.5 jit_solution(9668535946721957956)
XLA Ops:
  15.9 21.6 %all-reduce.16 = (bf16[768]{0:T(1024)(128)(2,1)S(1)}, bf16[768]{0:T(1024)(128)(2,1)S(1)}, bf16[768]{0:T(1024)(128)(2,1)S(1)}, bf16[768]{0:T(1024)(128)(2,1)S(1)}...) all-reduce(bf16[768]{0:T(1024)(128)(2,1)S(1)} %dynamic-update-slice, ...), channel_id=1, replica_groups=mesh['dp'=4,'ctx'=2,'tensor'=4] {'dp'}, use_global_device_ids=true, to_apply=%add.1 | all-reduce | flops 5376 | bytes 21504
  41.0 27.5 %all_gather.48 = bf16[768,3,192]{2,1,0:T(4,128)(2,1)S(1)} all-gather(bf16[192,3,192]{2,1,0:T(4,128)(2,1)S(1)} %copy.32), channel_id=1, replica_groups=mesh['dp'=4,'ctx'=2,'tensor'=4] {'dp'}, dimensions={0}, use_global_device_ids=true | all-gather | bytes 1105920 | tf_op jit(solution)/shard_map/all_gather | solution.py:123
  69.5 13.1 %all_gather.49 = bf16[3,3,64]{1,0,2:T(4,128)(2,1)S(1)} all-gather(bf16[3,3,16]{1,0,2:T(4,128)(2,1)S(1)} %copy.34), channel_id=1, replica_groups=mesh['dp'=4,'ctx'=2,'tensor'=4] {'dp'}, dimensions={2}, use_global_device_ids=true | all-gather | bytes 1440 | tf_op jit(solution)/shard_map/all_gather | solution.py:124
  83.8 8.6 %all_gather.47 = bf16[512,768]{1,0:T(8,128)(2,1)S(1)} all-gather(bf16[128,768]{1,0:T(8,128)(2,1)S(1)} %get-tuple-element.61), channel_id=1, replica_groups=mesh['dp'=4,'ctx'=2,'tensor'=4] {'tensor'}, dimensions={0}, use_global_device_ids=true | all-gather | bytes 983040 | tf_op jit(solution)/shard_map/all_gather | solution.py:156
  96.0 4.1 collective-permute-start.1
  102.2 8.4 %all-gather = bf16[1,512,768]{2,1,0:T(8,128)(2,1)S(1)} all-gather(bf16[1,128,768]{2,1,0:T(8,128)(2,1)S(1)} %copy-done.9), channel_id=2, replica_groups=mesh['dp'=4,'ctx'=2,'tensor'=4] {'tensor'}, dimensions={1}, use_global_device_ids=true | all-gather | bytes 983040 | tf_op jit(solution)/shard_map/all_gather | solution.py:202
  110.7 18.0 %all_gather.50 = bf16[192,768]{0,1:T(8,128)(2,1)S(1)} all-gather(bf16[192,192]{0,1:T(8,128)(2,1)S(1)} %copy.38), channel_id=1, replica_groups=mesh['dp'=4,'ctx'=2,'tensor'=4] {'dp'}, dimensions={1}, use_global_device_ids=true | all-gather | bytes 368640 | tf_op jit(solution)/shard_map/all_gather | solution.py:125
  135.4 3.2 multiply_reduce_fusion
  138.6 3.7 multiply_convert_fusion
  159.0 5.7 %collective-permute-done.3 = f32[512,3,64]{0,2,1:T(8,128)} collective-permute-done((f32[512,3,64]{0,2,1:T(8,128)}, f32[512,3,64]{0,2,1:T(8,128)}, u32[]{:S(2)}, u32[]{:S(2)}) %collective-permute-start.3) | collective-permute-done | bytes 393248 | tf_op jit(solution)/shard_map/ppermute | solution.py:20
  169.9 7.8 %all_gather.53 = bf16[512,768]{1,0:T(8,128)(2,1)S(1)} all-gather(bf16[128,768]{1,0:T(8,128)(2,1)S(1)} %copy-done.15), channel_id=1, replica_groups=mesh['dp'=4,'ctx'=2,'tensor'=4] {'tensor'}, dimensions={0}, use_global_device_ids=true | all-gather | bytes 983040 | tf_op jit(solution)/shard_map/all_gather | solution.py:157
  177.7 3.3 multiply_convert_fusion.1
  198.1 3.2 convolution_add_fusion
  208.2 19.9 %reduce-scatter.19.cloned.1.call-done = f32[192,3,192]{2,0,1:T(8,128)} async-done(((f32[768,3,192]{2,0,1:T(8,128)}), f32[192,3,192]{2,0,1:T(8,128)}) %reduce-scatter.19.cloned.1.call-update) | async-done | bytes 442384 | tf_op jit(solution)/shard_map/reduce_scatter | solution.py:275
  228.1 49.7 %reduce-scatter.21.cloned.1.call-done = f32[192,768]{1,0:T(8,128)} async-done(((f32[768,768]{1,0:T(8,128)}), f32[192,768]{1,0:T(8,128)}) %reduce-scatter.21.cloned.1.call-update) | async-done | bytes 589840 | tf_op jit(solution)/shard_map/reduce_scatter | solution.py:278
  277.9 49.7 %reduce-scatter.23.cloned.1.call-done = f32[768,192]{0,1:T(8,128)} async-done(((f32[768,768]{0,1:T(8,128)}), f32[768,192]{0,1:T(8,128)}) %reduce-scatter.23.cloned.1.call-update) | async-done | bytes 589840 | tf_op jit(solution)/shard_map/reduce_scatter | solution.py:280
  328.3 20.5 %reduce-scatter.25.cloned.1.call-done = f32[16,9]{1,0:T(8,128)} async-done(((f32[64,9]{1,0:T(8,128)}), f32[16,9]{1,0:T(8,128)}) %reduce-scatter.25.cloned.1.call-update) | async-done | bytes 592
  349.7 20.8 %reduce-scatter.29.cloned.1.call-done = f32[192,1]{1,0:T(8,128)} async-done(((f32[768,1]{1,0:T(8,128)}), f32[192,1]{1,0:T(8,128)}) %reduce-scatter.29.cloned.1.call-update) | async-done | bytes 784
  371.5 5.6 %all-reduce.14 = (f32[3,3,16]{2,1,0:T(4,128)}, f32[1,192]{1,0:T(1,128)}) all-reduce(f32[3,3,16]{2,1,0:T(4,128)S(1)} %copy.44, f32[1,192]{1,0:T(1,128)S(1)} %copy.48), channel_id=1, replica_groups=mesh['dp'=4,'ctx'=2,'tensor'=4] {'ctx'}, use_global_device_ids=true, to_apply=%region_26.27 | all-reduce | flops 336 | bytes 2688 | tf_op jit(solution)/shard_map/psum | solution.py:271
  377.0 22.5 %reduce-scatter.15.cloned.1.call-done = f32[128,768]{1,0:T(8,128)} async-done(((f32[512,768]{1,0:T(8,128)}), f32[128,768]{1,0:T(8,128)}) %reduce-scatter.15.cloned.1.call-update) | async-done | bytes 393232 | tf_op jit(solution)/shard_map/reduce_scatter | solution.py:192
  399.5 40.6 %reduce-scatter.17.cloned.1.call-done = f32[128,1536]{1,0:T(8,128)} async-done(((f32[512,1536]{1,0:T(8,128)}), f32[128,1536]{1,0:T(8,128)}) %reduce-scatter.17.cloned.1.call-update) | async-done | bytes 786448 | tf_op jit(solution)/shard_map/reduce_scatter | solution.py:245
  442.3 18.9 %all-reduce.13 = (f32[768]{0:T(1024)S(1)}, f32[768]{0:T(1024)S(1)}, f32[768]{0:T(1024)S(1)}, f32[768]{0:T(1024)S(1)}, f32[768]{0:T(1024)S(1)}) all-reduce(f32[768]{0:T(1024)S(1)} %get-tuple-element.18, f32[768]{0:T(1024)S(1)} %get-tuple-element.17, ...), channel_id=5, replica_groups=mesh['dp'=4,'ctx'=2,'tensor'=4] {'dp'}, use_global_device_ids=true, to_apply=%region_11.12.clone | all-reduce | flops 3840 | bytes 30720
  461.6 13.0 %all-reduce.12 = (f32[192]{0:T(256)}, f32[192]{0:T(256)}, f32[192]{0:T(256)}, f32[192]{0:T(256)}, f32[192]{0:T(256)S(1)}) all-reduce(f32[192]{0:T(256)S(1)} %dynamic-slice.10, f32[192]{0:T(256)S(1)} %dynamic-slice.12, f32[192]{0:T(256)S(1)} %dynamic-slice.14, ...), channel_id=1, replica_groups=mesh['dp'=4,'ctx'=2,'tensor'=4] {'ctx','tensor'}, use_global_device_ids=true, to_apply=%region_10.11 | all-reduce | flops 960 | bytes 7680 | tf_op jit(solution)/shard_map/psum | solution.py:253
  475.5 28.6 %all-reduce.19.cloned.1.call-done = (f32[192,3,192]{2,0,1:T(8,128)}, f32[192,192]{1,0:T(8,128)}, f32[192,768]{1,0:T(8,128)}, f32[768,192]{0,1:T(8,128)}) async-done(((f32[192,3,192]{2,0,1:T(8,128)}, f32[192,192]{1,0:T(8,128)}, f32[192,768]{1,0:T(8,128)}, f32[768,192]{0,1:T(8,128)}), (f32[192,3,192]{2,0,1:T(8,128)}, f32[192,192]{1,0:T(8,128)}, f32[192,768]{1,0:T(8,128)}, ...) | async-done | bytes 1769488 | tf_op jit(solution)/shard_map/psum | solution.py:271
  (206 shorter events, 83.6 us)
Async XLA Ops:
  7.2 170.5 %all-gather.4.cloned.1.call-start = ((), (), s32[]{:S(2)}) async-start(), calls=%async_computation.8 | async-start | bytes 1474560 | tf_op jit(solution)/shard_map/all_gather | solution.py:127
  7.9 173.0 %all-gather.6.cloned.1.call-start = ((), (), s32[]{:S(2)}) async-start(), calls=%async_computation.9 | async-start | bytes 1474560 | tf_op jit(solution)/shard_map/all_gather | solution.py:129
  37.5 45.4 %copy-start.24 = (f32[768]{0:T(1024)}, f32[768]{0:T(1024)S(1)}, u32[]{:S(2)}) copy-start(f32[768]{0:T(1024)S(1)} %convert_element_type.103) | copy-start | bytes 9220
  37.5 45.4 %copy-start.26 = (f32[768]{0:T(1024)}, f32[768]{0:T(1024)S(1)}, u32[]{:S(2)}) copy-start(f32[768]{0:T(1024)S(1)} %convert_element_type.112) | copy-start | bytes 9220
  96.0 35.2 %collective-permute-start.1 = (bf16[512,3,64]{0,2,1:T(8,128)(2,1)}, bf16[512,3,64]{0,2,1:T(8,128)(2,1)}, u32[]{:S(2)}, u32[]{:S(2)}) collective-permute-start(bf16[512,3,64]{0,2,1:T(8,128)(2,1)} %pad_maximum_fusion.7), channel_id=1, source_target_pairs={{0,4},{1,5},{2,6},{3,7},{8,12},{9,13},{10,14},{11,15},{16,20},{17,... | collective-permute-start | bytes 589832 | tf_op jit(solution)/shard_map/ppermute | solution.py:20
  100.1 35.3 %collective-permute-start = (bf16[512,3,64]{0,2,1:T(8,128)(2,1)}, bf16[512,3,64]{0,2,1:T(8,128)(2,1)}, u32[]{:S(2)}, u32[]{:S(2)}) collective-permute-start(bf16[512,3,64]{0,2,1:T(8,128)(2,1)} %get-tuple-element.46), channel_id=1, source_target_pairs={{0,4},{1,5},{2,6},{3,7},{8,12},{9,13},{10,14},{11,15},{16,20},{17,... | collective-permute-start | bytes 589832 | tf_op jit(solution)/shard_map/ppermute | solution.py:20
  102.1 104.4 %reduce-scatter.27.cloned.1.call-start = ((), (), s32[]{:S(2)}) async-start(), calls=%async_computation.16 | async-start | bytes 983040
  143.8 13.1 %collective-permute-start.2 = (f32[512,3,64]{0,2,1:T(8,128)}, f32[512,3,64]{0,2,1:T(8,128)}, u32[]{:S(2)}, u32[]{:S(2)}) collective-permute-start(f32[512,3,64]{0,2,1:T(8,128)} %slice.114), channel_id=1, source_target_pairs={{4,0},{5,1},{6,2},{7,3},{12,8},{13,9},{14,10},{15,11},{20,16},{21,... | collective-permute-start | bytes 1179656 | tf_op jit(solution)/shard_map/ppermute | solution.py:20
  151.1 13.6 %collective-permute-start.3 = (f32[512,3,64]{0,2,1:T(8,128)}, f32[512,3,64]{0,2,1:T(8,128)}, u32[]{:S(2)}, u32[]{:S(2)}) collective-permute-start(f32[512,3,64]{0,2,1:T(8,128)} %slice.119), channel_id=1, source_target_pairs={{4,0},{5,1},{6,2},{7,3},{12,8},{13,9},{14,10},{15,11},{20,16},{21,... | collective-permute-start | bytes 1179656 | tf_op jit(solution)/shard_map/ppermute | solution.py:20
  153.8 74.3 %reduce-scatter.19.cloned.1.call-start = ((), (), s32[]{:S(2)}) async-start(), calls=%async_computation.12 | async-start | bytes 2949120 | tf_op jit(solution)/shard_map/reduce_scatter | solution.py:275
  169.0 108.9 %reduce-scatter.21.cloned.1.call-start = ((), (), s32[]{:S(2)}) async-start(), calls=%async_computation.13 | async-start | bytes 2949120 | tf_op jit(solution)/shard_map/reduce_scatter | solution.py:278
  187.2 140.4 %reduce-scatter.23.cloned.1.call-start = ((), (), s32[]{:S(2)}) async-start(), calls=%async_computation.14 | async-start | bytes 2949120 | tf_op jit(solution)/shard_map/reduce_scatter | solution.py:280
  189.6 159.2 %reduce-scatter.25.cloned.1.call-start = ((), (), s32[]{:S(2)}) async-start(), calls=%async_computation.15 | async-start | bytes 40960
  197.1 173.5 %reduce-scatter.29.cloned.1.call-start = ((), (), s32[]{:S(2)}) async-start(), calls=%async_computation.17 | async-start | bytes 491520
  198.1 201.5 %reduce-scatter.15.cloned.1.call-start = ((), (), s32[]{:S(2)}) async-start(), calls=%async_computation.10 | async-start | bytes 1966080 | tf_op jit(solution)/shard_map/reduce_scatter | solution.py:192
  201.4 238.7 %reduce-scatter.17.cloned.1.call-start = ((), (), s32[]{:S(2)}) async-start(), calls=%async_computation.11 | async-start | bytes 3932160 | tf_op jit(solution)/shard_map/reduce_scatter | solution.py:245
  206.3 122.0 %copy-start.10 = (bf16[1,128,768]{2,1,0:T(8,128)(2,1)S(1)}, bf16[1,128,768]{2,1,0:T(8,128)(2,1)}, u32[]{:S(2)}) copy-start(bf16[1,128,768]{2,1,0:T(8,128)(2,1)} %param.16) | copy-start | bytes 589828
  206.3 122.0 %copy-start.34 = (bf16[768]{0:T(1024)(128)(2,1)S(1)}, bf16[768]{0:T(1024)(128)(2,1)}, u32[]{:S(2)}) copy-start(bf16[768]{0:T(1024)(128)(2,1)} %get-tuple-element.43) | copy-start | bytes 4612
  206.3 122.0 %copy-start.35 = (bf16[768]{0:T(1024)(128)(2,1)S(1)}, bf16[768]{0:T(1024)(128)(2,1)}, u32[]{:S(2)}) copy-start(bf16[768]{0:T(1024)(128)(2,1)} %get-tuple-element.44) | copy-start | bytes 4612
  206.3 233.8 %copy-start.25 = (f32[768]{0:T(1024)S(1)}, f32[768]{0:T(1024)}, u32[]{:S(2)}) copy-start(f32[768]{0:T(1024)} %copy-done.24) | copy-start | bytes 9220
  206.3 233.8 %copy-start.27 = (f32[768]{0:T(1024)S(1)}, f32[768]{0:T(1024)}, u32[]{:S(2)}) copy-start(f32[768]{0:T(1024)} %copy-done.26) | copy-start | bytes 9220
  206.3 233.8 %copy-start.29 = (f32[128]{0:T(128)S(1)}, f32[128]{0:T(128)}, u32[]{:S(2)}) copy-start(f32[128]{0:T(128)} %copy-done.28) | copy-start | bytes 1540
  206.3 233.8 %copy-start.31 = (f32[128]{0:T(128)S(1)}, f32[128]{0:T(128)}, u32[]{:S(2)}) copy-start(f32[128]{0:T(128)} %copy-done.30) | copy-start | bytes 1540
  206.4 297.7 %all-reduce.19.cloned.1.call-start = ((), (), s32[]{:S(2)}) async-start(), calls=%async_computation.18 | async-start | bytes 3932160 | tf_op jit(solution)/shard_map/psum | solution.py:271
  (29 other events, 394.6 us)
Sparse Core Ops, SparseCore 0:
  9.6 36.2 all-gather.3
  102.2 33.7 all-gather.5
  154.0 24.6 reduce-scatter.26
  180.8 47.2 reduce-scatter.18
  230.3 47.5 reduce-scatter.20
  280.0 47.5 reduce-scatter.22
  330.4 18.3 reduce-scatter.24
  351.8 18.6 reduce-scatter.28
  373.1 26.4 reduce-scatter.14
  402.1 37.9 reduce-scatter.16
  443.1 60.9 all-reduce.18
where the time goes:
time: 519 us; the launch traced here: 517 us
  waiting for transfers between devices  262 us (50%)
  blocking collectives  142 us (27%)
  matrix products  37.3 us (7%)
  local copies, waits for them, and re-layouts  29.2 us (6%)
  other arithmetic  21.5 us (4%)
  between operations  15.9 us (3%)
  starting transfers between devices  9.34 us (2%)
    reduce_scatter x1, waiting for transfers between devices, body(): lax.psum_scatter(large_grads[3], 'dp', scatter_dimension=0, tiled=True)  49.7 us
    reduce_scatter x1, waiting for transfers between devices, body(): lax.psum_scatter(large_grads[5], 'dp', scatter_dimension=1, tiled=True)  49.7 us
    unnamed x14, waiting for transfers between devices  42.2 us
    unnamed x2, blocking collectives  40.6 us
    reduce_scatter x1, waiting for transfers between devices, body(): lax.psum_scatter(jnp.concatenate([first_part, second_part], axis=1), 'ten...  40.6 us
    psum x1, waiting for transfers between devices, body(): lax.psum((grad_project, grad_pbias, grad_outw, grad_up, upbias_row, grad_...  28.6 us
    all_gather x1, blocking collectives, body(): lax.all_gather(project_weight, 'dp', axis=0, tiled=True)  27.5 us
    unnamed x111, local copies, waits for them, and re-layouts  24.8 us
  transfers between devices with their start and end apart: 15, of which 10 were waited for; matrix products, arithmetic and copies ran while one was open for 15% of the time, Pallas kernels for 0%

commit v1 on v0

v1 whole, which is shorter than its diff:
```python
import jax
import jax.numpy as jnp
from jax import lax
from jax.experimental import pallas as pl
from jax.experimental.pallas import tpu as pltpu
from jax.sharding import PartitionSpec as P

HD = 64
ROT = 16
HALF = ROT // 2
DOC_MAX = 512
ROWS = 256

epsilon = 1e-05
masked_score = -1e30
f32 = jnp.float32
bf16 = jnp.bfloat16


def flipped(block, axis, bit):
    return lax.ppermute(block, axis, [(i, i ^ bit) for i in range(lax.axis_size(axis))])


def ordered(own, other, second, dim):
    return jnp.where(
        second, jnp.stack([other, own], axis=dim), jnp.stack([own, other], axis=dim)
    )


def gather_tokens(rows):
    block = rows
    dims = 0
    for axis in ("ctx", "tensor"):
        index = lax.axis_index(axis)
        bit = lax.axis_size(axis) // 2
        while bit:
            block = ordered(block, flipped(block, axis, bit), (index & bit) > 0, dims)
            bit //= 2
            dims += 1
    return block.reshape(-1, rows.shape[-1])


def gather_dp(block):
    count = lax.axis_size("dp")
    return lax.all_to_all(jnp.broadcast_to(block[None], (count,) + block.shape), "dp", 0, 0)


def scatter_rows(partial):
    count = lax.axis_size("ctx") * lax.axis_size("tensor")
    blocks = partial.reshape(count, partial.shape[0] // count, partial.shape[1])
    return lax.all_to_all(blocks, ("ctx", "tensor"), 0, 0)


def high_low(values):
    high = lax.reduce_precision(values, 8, 7)
    return jnp.stack([high, values - high]).astype(bf16)


def pad_rows(block, rows):
    return jnp.pad(block, ((0, rows - block.shape[0]), (0, 0)))


def gelu_pair(preact):
    cumulative = 0.5 * (1.0 + jax.scipy.special.erf(preact * 0.7071067811865476))
    density = jnp.exp(-0.5 * preact * preact) * 0.3989422804014327
    return (preact * cumulative, cumulative + preact * density)


def dot(left, right, dims):
    return lax.dot_general(left, right, (dims, ((), ())), preferred_element_type=f32)


def attention_kernel(
    qkv_ref, bias_ref, cos_ref, sin_ref, seg_row_ref, seg_col_ref, grad_ref,
    att_ref, grad_proj_ref, bias_grad_ref, dq_ref, dk_ref, dv_ref,
):
    width, tokens = grad_ref.shape
    cosine = cos_ref[...]
    sine = sin_ref[...]
    scale = HD**-0.5

    def rotate(block, direction):
        first, second = block[:HALF], block[HALF:ROT]
        return jnp.concatenate(
            [
                first * cosine - second * (direction * sine),
                second * cosine + first * (direction * sine),
                block[ROT:],
            ],
            axis=0,
        )

    def head(index, carry):
        start = pl.multiple_of(index * HD, HD)

        def rows(part):
            return pl.ds(part * width + start, HD)

        queries = rotate(qkv_ref[rows(0), :] + bias_ref[rows(0), :], 1.0).astype(bf16)
        keys = rotate(qkv_ref[rows(1), :] + bias_ref[rows(1), :], 1.0).astype(bf16)
        values = (qkv_ref[rows(2), :] + bias_ref[rows(2), :]).astype(bf16)
        queries = queries * jnp.asarray(scale, bf16)
        grads = grad_ref[pl.ds(start, HD), :]
        key_rows = keys.T
        value_rows = values.T
        dk_ref[...] = jnp.zeros(dk_ref.shape, f32)
        dv_ref[...] = jnp.zeros(dv_ref.shape, f32)
        for block in range(tokens // ROWS):
            begin, end = block * ROWS, (block + 1) * ROWS
            low = max(0, (begin - DOC_MAX + 1) // ROWS * ROWS)
            query = queries[:, begin:end]
            grad = grads[:, begin:end]
            scores = dot(key_rows[low:end], query, ((1,), (0,)))
            key_at = lax.broadcasted_iota(jnp.int32, scores.shape, 0) + low
            query_at = lax.broadcasted_iota(jnp.int32, scores.shape, 1) + begin
            allowed = (seg_col_ref[low:end, :] == seg_row_ref[:, begin:end]) & (
                key_at <= query_at
            )
            scores = jnp.where(allowed, scores, masked_score)
            highest = jnp.max(scores, axis=0, keepdims=True)
            exponent = jnp.exp(scores - highest)
            probs = exponent * (1.0 / jnp.sum(exponent, axis=0, keepdims=True))
            probs_b = probs.astype(bf16)
            attended = dot(values[:, low:end], probs_b, ((1,), (0,))).astype(bf16)
            att_ref[pl.ds(start, HD), begin:end] = attended
            delta = jnp.sum(
                grad.astype(f32) * attended.astype(f32), axis=0, keepdims=True
            )
            grad_probs = dot(value_rows[low:end], grad, ((1,), (0,)))
            grad_scores = (probs * (grad_probs - delta)).astype(bf16)
            dq_ref[:, begin:end] = dot(keys[:, low:end], grad_scores, ((1,), (0,))) * scale
            dk_ref[:, low:end] += dot(query, grad_scores, ((1,), (1,)))
            dv_ref[:, low:end] += dot(grad, probs_b, ((1,), (1,)))
        for part, result in enumerate(
            (rotate(dq_ref[...], -1.0), rotate(dk_ref[...], -1.0), dv_ref[...])
        ):
            grad_proj_ref[rows(part), :] = result.astype(bf16)
            bias_grad_ref[rows(part), :] = jnp.sum(result, axis=1, keepdims=True)
        return carry

    lax.fori_loop(0, width // HD, head, 0)


def attention(qkv, bias, cosine, sine, segments, grad):
    width, tokens = grad.shape
    whole = pl.BlockSpec(memory_space=pltpu.VMEM)
    pairs = tokens * (DOC_MAX + ROWS) * (width // HD)
    return pl.pallas_call(
        attention_kernel,
        out_shape=(
            jax.ShapeDtypeStruct((width, tokens), bf16),
            jax.ShapeDtypeStruct((3 * width, tokens), bf16),
            jax.ShapeDtypeStruct((3 * width, 1), f32),
        ),
        in_specs=[whole] * 7,
        out_specs=(whole, whole, whole),
        scratch_shapes=[pltpu.VMEM((HD, tokens), f32)] * 3,
        cost_estimate=pl.CostEstimate(
            flops=pairs * HD * 10, transcendentals=pairs, bytes_accessed=tokens * width * 24
        ),
        name="attention",
    )(qkv, bias, cosine, sine, segments[None, :], segments[:, None], grad)


def body(
    hidden_in, cotangent, segment_ids, attend_gain, attend_shift, feed_gain, feed_shift,
    project_weight, project_bias, output_weight, output_bias,
    upward_weight, upward_bias, downward_weight, downward_bias,
):
    n_dp, n_ctx, n_tensor = (lax.axis_size(a) for a in ("dp", "ctx", "tensor"))
    dp_index, ctx_index = lax.axis_index("dp"), lax.axis_index("ctx")
    second = ctx_index > 0
    share, _, width = project_weight.shape
    model = share * n_dp
    units = upward_weight.shape[1]
    half_units = units // n_ctx
    half_share = share // n_ctx
    heads = width // HD

    def own_half(block, size, axis):
        return lax.dynamic_slice_in_dim(block, ctx_index * size, size, axis)

    packed = jnp.concatenate(
        [
            own_half(project_weight, half_share, 0).reshape(half_share, 3 * width),
            own_half(output_weight, half_share, 1).T,
        ],
        axis=1,
    )
    small = jnp.concatenate(
        [
            attend_gain, attend_shift, feed_gain, feed_shift, output_bias, downward_bias,
            upward_bias[0], project_bias.reshape(-1),
        ]
    )
    columns = 4 * width
    small_rows = -(-small.shape[0] // (8 * columns)) * 8
    small_block = jnp.pad(small, (0, small_rows * columns - small.shape[0]))
    packed = jnp.concatenate([packed, small_block.reshape(small_rows, columns)], axis=0)
    attention_all = gather_dp(packed)
    feed_all = gather_dp(
        jnp.concatenate(
            [own_half(upward_weight, half_units, 1), own_half(downward_weight, half_units, 0).T],
            axis=0,
        )
    )
    hidden_rows = hidden_in[0]
    grad_rows = cotangent[0]
    hidden_all = gather_tokens(hidden_rows)
    grad_all = gather_tokens(grad_rows)
    tokens = hidden_all.shape[0]

    attention_half = attention_all[:, :half_share]
    weights = ordered(attention_half, flipped(attention_half, "ctx", 1), second, 1)
    weights = weights.reshape(model, columns)
    weight_project, weight_output = weights[:, : 3 * width], weights[:, 3 * width :]
    params = attention_all[:, half_share:].reshape(n_dp, -1)[:, : small.shape[0]].astype(f32)
    vectors = params[:, : 6 * share].reshape(n_dp, 6, share).transpose(1, 0, 2).reshape(6, model)
    gain_one, shift_one, gain_two, shift_two, bias_output, bias_downward = (
        vectors[i] for i in range(6)
    )
    unit_share = units // n_dp
    bias_upward = own_half(
        params[:, 6 * share : 6 * share + unit_share].reshape(units), half_units, 0
    )
    bias_project = (
        params[:, 6 * share + unit_share :]
        .reshape(n_dp, 3, heads, HD // n_dp)
        .transpose(1, 2, 0, 3)
        .reshape(3 * width, 1)
    )
    weight_up = feed_all[:, :share].reshape(model, half_units)
    weight_down = feed_all[:, share:].reshape(model, half_units)

    source = hidden_all.astype(f32)
    centred = source - jnp.mean(source, axis=-1, keepdims=True)
    inverse = lax.rsqrt(jnp.mean(centred * centred, axis=-1, keepdims=True) + epsilon)
    normed = centred * inverse
    first_in = (normed * gain_one + shift_one).astype(bf16)
    second_in = (normed * gain_two + shift_two).astype(bf16)

    frequency = 10000.0 ** (-2.0 * jnp.arange(HALF, dtype=f32) / ROT)
    angles = frequency[:, None] * jnp.arange(tokens, dtype=f32)[None, :]
    qkv = dot(weight_project, first_in, ((0,), (1,)))
    grad_att = dot(weight_output, grad_all, ((0,), (1,))).astype(bf16)
    attended, grad_proj, bias_grad = attention(
        qkv, bias_project, jnp.cos(angles), jnp.sin(angles), segment_ids[0], grad_att
    )

    grad_weights = jnp.concatenate(
        [dot(first_in, grad_proj, ((0,), (1,))), dot(grad_all, attended, ((0,), (1,)))], axis=1
    ).astype(bf16)
    grad_half = lax.dynamic_index_in_dim(
        grad_weights.reshape(n_dp, n_ctx, half_share, columns), ctx_index, 1, keepdims=False
    )
    bias_block = pad_rows(
        jnp.pad(high_low(bias_grad[:, 0]), ((0, 0), (0, columns - 3 * width))), 8
    )
    attention_parts = lax.all_to_all(
        jnp.concatenate(
            [grad_half, jnp.broadcast_to(bias_block[None], (n_dp, 8, columns))], axis=1
        ),
        "dp", 0, 0,
    )

    preact = dot(second_in, weight_up, ((1,), (0,))) + bias_upward
    activated, slope = gelu_pair(preact)
    hidden_act = activated.astype(bf16)
    grad_pre = dot(grad_all, weight_down, ((1,), (0,))) * slope
    grad_pre_b = grad_pre.astype(bf16)
    grad_feed = jnp.concatenate(
        [
            dot(second_in, grad_pre_b, ((0,), (0,))).reshape(n_dp, share, half_units),
            dot(grad_all, hidden_act, ((0,), (0,))).reshape(n_dp, share, half_units),
        ],
        axis=1,
    ).astype(bf16)
    unit_block = pad_rows(high_low(jnp.sum(grad_pre, axis=0)), 8)
    feed_parts = lax.all_to_all(
        jnp.concatenate(
            [grad_feed, jnp.broadcast_to(unit_block[None], (n_dp, 8, half_units))], axis=1
        ),
        "dp", 0, 0,
    )

    part = 1.0 / n_ctx
    mixed = dot(hidden_act, weight_down, ((1,), (1,))) + part * dot(
        attended, weight_output, ((0,), (1,))
    )
    mixed_parts = scatter_rows(mixed.astype(bf16))
    grad_first = part * dot(grad_proj, weight_project, ((0,), (1,)))
    grad_second = dot(grad_pre_b, weight_up, ((1,), (1,)))
    normed_parts = scatter_rows((grad_first * gain_one + grad_second * gain_two).astype(bf16))
    sums = jnp.stack(
        [
            jnp.sum(grad_first * normed, axis=0),
            jnp.sum(grad_first, axis=0),
            jnp.sum(grad_second * normed, axis=0),
            jnp.sum(grad_second, axis=0),
            jnp.sum(grad_rows.astype(f32), axis=0),
        ]
    )
    sums = sums.reshape(5, n_dp, share).transpose(1, 0, 2)
    sums = jnp.broadcast_to(sums[:, None], (n_dp, n_ctx * n_tensor, 5, share))
    sums = lax.all_to_all(
        sums.reshape(-1, 5, share), ("dp", "ctx", "tensor"), 0, 0
    ).sum(axis=0)

    own_source = hidden_rows.astype(f32)
    hidden_out = own_source + jnp.sum(mixed_parts.astype(f32), axis=0)
    hidden_out = (hidden_out + (bias_output + bias_downward)).astype(bf16)[None]

    own_centred = own_source - jnp.mean(own_source, axis=-1, keepdims=True)
    own_inverse = lax.rsqrt(jnp.mean(own_centred * own_centred, axis=-1, keepdims=True) + epsilon)
    own_normed = own_centred * own_inverse
    grad_normed = jnp.sum(normed_parts.astype(f32), axis=0)
    grad_inner = own_inverse * (
        grad_normed
        - jnp.mean(grad_normed, axis=-1, keepdims=True)
        - own_normed * jnp.mean(grad_normed * own_normed, axis=-1, keepdims=True)
    )
    hidden_grad = (grad_rows.astype(f32) + grad_inner).astype(bf16)[None]

    attention_sum = jnp.sum(attention_parts.astype(f32), axis=0)
    attention_own = lax.reduce_precision(attention_sum[:half_share], 8, 7).astype(bf16)
    attention_both = ordered(attention_own, flipped(attention_own, "ctx", 1), second, 0)
    attention_both = attention_both.reshape(share, columns).astype(f32)
    project_bias_sum = (attention_sum[half_share] + attention_sum[half_share + 1])[: 3 * width]
    bias_share = HD // n_dp
    project_bias_grad = lax.dynamic_slice_in_dim(
        project_bias_sum.reshape(3, heads, HD), dp_index * bias_share, bias_share, 2
    )

    feed_sum = jnp.sum(feed_parts.astype(f32), axis=0)
    unit_sum = feed_sum[2 * share] + feed_sum[2 * share + 1]
    feed_own = jnp.concatenate(
        [
            lax.reduce_precision(feed_sum[: 2 * share], 8, 7).astype(bf16),
            pad_rows(high_low(unit_sum), 8),
        ],
        axis=0,
    )
    feed_both = ordered(feed_own, flipped(feed_own, "ctx", 1), second, 0).astype(f32)
    upward_grad = feed_both[:, :share].transpose(1, 0, 2).reshape(share, units)
    downward_grad = feed_both[:, share : 2 * share].transpose(0, 2, 1).reshape(units, share)
    unit_both = (feed_both[:, 2 * share] + feed_both[:, 2 * share + 1]).reshape(units)
    upward_bias_grad = lax.dynamic_slice_in_dim(unit_both, dp_index * unit_share, unit_share)[None]

    return (
        hidden_out,
        hidden_grad,
        sums[0],
        sums[1],
        sums[2],
        sums[3],
        attention_both[:, : 3 * width].reshape(share, 3, width),
        project_bias_grad,
        attention_both[:, 3 * width :].T,
        sums[4],
        upward_grad,
        upward_bias_grad,
        downward_grad,
        sums[4],
    )


def solution(mesh):
    rows = P("dp", ("ctx", "tensor"), None)
    in_specs = (
        rows, rows, P("dp", None), P("dp"), P("dp"), P("dp"), P("dp"),
        P("dp", None, "tensor"), P(None, "tensor", "dp"), P("tensor", "dp"), P("dp"),
        P("dp", "tensor"), P("tensor", "dp"), P("tensor", "dp"), P("dp"),
    )
    out_specs = (
        rows, rows, P("dp"), P("dp"), P("dp"), P("dp"),
        P("dp", None, "tensor"), P(None, "tensor", "dp"), P("tensor", "dp"), P("dp"),
        P("dp", "tensor"), P("tensor", "dp"), P("tensor", "dp"), P("dp"),
    )
    return jax.shard_map(body, mesh=mesh, in_specs=in_specs, out_specs=out_specs, check_vma=False)
```

time: 519 us -> 238 us (0.46)
  waiting for transfers between devices: 262 us -> 78 us
  blocking collectives: 142 us -> 0 us
  starting transfers between devices: 9.34 us -> 41.6 us
  Pallas kernels: 0 us -> 14.8 us
  between operations: 15.9 us -> 1.35 us
  local copies, waits for them, and re-layouts: 29.2 us -> 41.4 us
  other arithmetic: 21.5 us -> 30.9 us
  matrix products: 37.3 us -> 28.7 us
    reduce_scatter x5 -> x0, waiting for transfers between devices: 182 us -> none  [the longest x1 49.7 us: body(): lax.psum_scatter(large_grads[3], 'dp', scatter_dimension=0, tiled=True)]
    all_gather x6 -> x0, blocking collectives: 83.4 us -> none  [the longest x1 27.5 us: body(): lax.all_gather(project_weight, 'dp', axis=0, tiled=True)]
    all_to_all x0 -> x7, waiting for transfers between devices: none -> 56.1 us  [the longest x2 27.3 us: scatter_rows(): return lax.all_to_all(blocks, ('ctx', 'tensor'), 0, 0)]
    unnamed x14 -> x0, waiting for transfers between devices: 42.2 us -> none
    unnamed x2 -> x0, blocking collectives: 40.6 us -> none
    all_to_all x0 -> x7, starting transfers between devices: none -> 30 us  [the longest x2 9.68 us: gather_dp(): lax.all_to_all(jnp.broadcast_to(block[None], (count,) + block.shape), 'dp...]
    psum x1 -> x0, waiting for transfers between devices: 28.6 us -> none  [body(): lax.psum((grad_project, grad_pbias, grad_outw, grad_up, upbias_row, grad_...]
    psum x2 -> x0, blocking collectives: 18.6 us -> none  [the longest x1 13 us: body(): lax.psum((jnp.sum(grad_first * normed, axis=0), jnp.sum(grad_first, axis=...]
  transfers between devices with their start and end apart: 15 -> 16, of which waited for: 10 -> 9; matrix products, arithmetic and copies ran while one was open for 15% -> 35% of each run, Pallas kernels for 0% -> 6%
where the time goes in v1:
time: 238 us; the launch traced here: 237 us
  waiting for transfers between devices  78 us (33%)
  starting transfers between devices  41.6 us (17%)
  local copies, waits for them, and re-layouts  41.4 us (17%)
  other arithmetic  30.9 us (13%)
  matrix products  28.7 us (12%)
  Pallas kernels  14.8 us (6%)
    dot_general x12, matrix products, dot(): lax.dot_general(left, right, (dims, ((), ())), preferred_element_type=f32)  28.7 us
    all_to_all x2, waiting for transfers between devices, scatter_rows(): return lax.all_to_all(blocks, ('ctx', 'tensor'), 0, 0)  27.3 us
    ppermute x9, waiting for transfers between devices, flipped(): lax.ppermute(block, axis, [(i, i ^ bit) for i in range(lax.axis_size(axis...  22 us
    pallas_call x1, Pallas kernels, attention(): pl.pallas_call(attention_kernel, out_shape=(jax.ShapeDtypeStruct((width,...  14.8 us
    all_to_all x1, waiting for transfers between devices, body(): lax.all_to_all(jnp.concatenate([grad_half, jnp.broadcast_to(bias_block[No...  12.3 us
    ppermute x9, starting transfers between devices, flipped(): lax.ppermute(block, axis, [(i, i ^ bit) for i in range(lax.axis_size(axis...  11.6 us
    all_to_all x1, waiting for transfers between devices, body(): lax.all_to_all(jnp.concatenate([grad_feed, jnp.broadcast_to(unit_block[No...  10.3 us
    all_to_all x2, starting transfers between devices, gather_dp(): lax.all_to_all(jnp.broadcast_to(block[None], (count,) + block.shape), 'dp...  9.68 us
  transfers between devices with their start and end apart: 16, of which 9 were waited for; matrix products, arithmetic and copies ran while one was open for 35% of the time, Pallas kernels for 6%

profile of v1, /device:TPU:0, one launch (start us, length us, event | category | flops | bytes accessed | tf_op | source)
XLA Modules:
  0.0 236.7 jit_solution(12835011657486246436)
XLA Ops:
  0.7 3.0 %collective-permute-start = (bf16[128,768]{1,0:T(8,128)(2,1)}, bf16[128,768]{1,0:T(8,128)(2,1)S(1)}, u32[]{:S(2)}, u32[]{:S(2)}) collective-permute-start(bf16[128,768]{1,0:T(8,128)(2,1)} %bitcast.155), channel_id=1, source_target_pairs={{0,4},{4,0},{1,5},{5,1},{2,6},{6,2},{3,7},{7,3},{8,12},{12,8},{9,1... | collective-permute-start | bytes 589832 | tf_op jit(solution)/shard_map/ppermute | solution.py:21
  7.2 4.1 %concatenate.123 = bf16[1488]{0:T(1024)(128)(2,1)S(1)} concatenate(bf16[192]{0:T(256)(128)(2,1)} %param.18, bf16[192]{0:T(256)(128)(2,1)} %param.19, bf16[192]{0:T(256)(128)(2,1)} %param.20, bf16[192]{0:T(256)(128)(2,1)} %param.21, bf16[192]{0:T(256)(128)(2,1)} %param.25, bf16[192]{0:T(256)(128)(2,1)} %param.29, bf16[192]{0:T(256)(128)(2,1)S(1)} %reduce.3, ...), dimensions={0} | concatenate | bytes 5952 | tf_op jit(solution)/shard_map/concatenate | solution.py:190
  12.7 4.9 %all-to-all-start = ((bf16[4,104,768]{2,1,0:T(8,128)(2,1)}), bf16[4,104,768]{2,1,0:T(8,128)(2,1)S(1)}, u32[]{:S(2)}, u32[]{:S(2)}) async-start(bf16[4,104,768]{2,1,0:T(8,128)(2,1)} %broadcast_in_dim.12), calls=%async_computation | async-start | bytes 1277952 | tf_op jit(solution)/shard_map/all_to_all | solution.py:45
  25.5 8.8 %collective-permute-done.1 = bf16[2,128,768]{2,1,0:T(8,128)(2,1)S(1)} collective-permute-done((bf16[2,128,768]{2,1,0:T(8,128)(2,1)S(1)}, bf16[2,128,768]{2,1,0:T(8,128)(2,1)S(1)}, u32[]{:S(2)}, u32[]{:S(2)}) %collective-permute-start.1) | collective-permute-done | bytes 393248 | tf_op jit(solution)/shard_map/ppermute | solution.py:21
  35.4 5.4 %collective-permute-done.5 = bf16[2,128,768]{2,1,0:T(8,128)(2,1)S(1)} collective-permute-done((bf16[2,128,768]{2,1,0:T(8,128)(2,1)S(1)}, bf16[2,128,768]{2,1,0:T(8,128)(2,1)S(1)}, u32[]{:S(2)}, u32[]{:S(2)}) %collective-permute-start.5) | collective-permute-done | bytes 393248 | tf_op jit(solution)/shard_map/ppermute | solution.py:21
  44.1 4.8 %all-to-all-start.1 = ((bf16[4,384,384]{2,1,0:T(8,128)(2,1)}), bf16[4,384,384]{2,1,0:T(8,128)(2,1)}, u32[]{:S(2)}, u32[]{:S(2)}) async-start(bf16[4,384,384]{2,1,0:T(8,128)(2,1)} %broadcast_in_dim.13), calls=%async_computation.1 | async-start | bytes 2359296 | tf_op jit(solution)/shard_map/all_to_all | solution.py:45
  61.3 3.1 %add_convert_fusion = (bf16[1024,768]{1,0:T(8,128)(2,1)}, bf16[1024,768]{1,0:T(8,128)(2,1)}) fusion(f32[768]{0:T(1024)S(1)} %add.154, f32[768]{0:T(1024)S(1)} %mul.195, f32[1024]{0:T(1024)S(1)} %bitcast.198, f32[1024]{0:T(1024)S(1)} %bitcast.196, bf16[2,2,1,128,768]{4,3,2,1,0:T(8,128)(2,1)S(1)} %bitcast.149, ...), kind=kLoop, calls=%fused_computation.4 | loop fusion | flops 9437184 | bytes 4739073 | tf_op jit(solution)/shard_map/convert_element_type | solution.py:240
  74.9 14.8 %attention.1 = (bf16[192,1024]{1,0:T(8,128)(2,1)}, bf16[576,1024]{1,0:T(8,128)(2,1)}, f32[576,1]{1,0:T(8,128)}) custom-call(f32[576,1024]{1,0:T(8,128)} %fusion.9.qkv_ref, f32[576,1]{1,0:T(8,128)} %reshape.790.bias_ref, f32[8,1024]{1,0:T(8,128)} %get-tuple-element.116.cos_ref, f32[8,1024]{1,0:T(8,128)} %get-tuple-element.115.sin_ref, s32[1,1024]{1,0:T(1,128)} %seg_row_ref.1, ...), custom_call_target="tpu_custom_call" | custom-call | flops 1509949440 | bytes 4718592 | tf_op jit(solution)/shard_map/attention/pallas_call | solution.py:148
  90.9 2.9 %convolution_convert_fusion.3 = bf16[4,2,96,192]{3,2,1,0:T(8,128)(2,1)} fusion(bf16[4,2,96,1024]{3,2,1,0:T(8,128)(2,1)} %bitcast.178, bf16[192,1024]{1,0:T(8,128)(2,1)} %get-tuple-element.17), kind=kOutput, calls=%fused_computation.31 | convolution fusion | flops 302137344 | bytes 2260992 | tf_op jit(solution)/shard_map/dot_general | solution.py:70
  93.8 3.7 %convolution_convert_fusion = bf16[4,2,96,576]{3,2,1,0:T(8,128)(2,1)} fusion(bf16[4,2,96,1024]{3,2,1,0:T(8,128)(2,1)S(1)} %bitcast.181, bf16[576,1024]{1,0:T(8,128)(2,1)} %get-tuple-element.18), kind=kOutput, calls=%fused_computation.27 | convolution fusion | flops 906412032 | bytes 3637248 | tf_op jit(solution)/shard_map/dot_general | solution.py:70
  105.7 3.7 %fusion.56 = (f32[768]{0:T(1024)S(1)}, f32[768]{0:T(1024)S(1)}, bf16[1024,768]{1,0:T(8,128)(2,1)}, f32[768]{0:T(1024)S(1)}, f32[768]{0:T(1024)S(1)}) fusion(f32[1024,768]{1,0:T(8,128)S(1)} %fusion.33, f32[1024]{0:T(1024)S(1)} %bitcast.199, f32[1024]{0:T(1024)S(1)} %bitcast.197, bf16[2,2,1,128,768]{4,3,2,1,0:T(8,128)(2,1)S(1)} %bitcast.151, ...), kind=kOutput, calls=%fused_computation.148 | convolution fusion | flops 919335936 | bytes 8482817 | tf_op jit(solution)/shard_map/dot_general | solution.py:70
  110.7 5.2 %all-to-all-start.4 = ((f32[32,1,960]{2,1,0:T(1,128)}), f32[32,1,960]{2,1,0:T(1,128)S(1)}, u32[]{:S(2)}, u32[]{:S(2)}) async-start(f32[32,1,960]{2,1,0:T(1,128)} %reshape.800), calls=%async_computation.4 | async-start | bytes 262144 | tf_op jit(solution)/shard_map/all_to_all | solution.py:305
  117.9 6.2 %all-to-all-done.4 = f32[32,1,960]{2,1,0:T(1,128)S(1)} async-done(((f32[32,1,960]{2,1,0:T(1,128)}), f32[32,1,960]{2,1,0:T(1,128)S(1)}, u32[]{:S(2)}, u32[]{:S(2)}) %all-to-all-start.4) | async-done | bytes 122912 | tf_op jit(solution)/shard_map/all_to_all | solution.py:305
  124.2 4.2 %all-to-all-start.5 = ((bf16[4,104,768]{2,1,0:T(8,128)(2,1)}), bf16[4,104,768]{2,1,0:T(8,128)(2,1)}, u32[]{:S(2)}, u32[]{:S(2)}) async-start(bf16[4,104,768]{2,1,0:T(8,128)(2,1)} %pad_maximum_fusion.1), calls=%async_computation.5 | async-start | bytes 1277952 | tf_op jit(solution)/shard_map/all_to_all | solution.py:259
  130.3 3.4 %convolution_convert_fusion.2 = bf16[4,192,384]{2,1,0:T(8,128)(2,1)} fusion(bf16[4,192,1024]{2,1,0:T(8,128)(2,1)} %bitcast.182, bf16[1024,384]{1,0:T(8,128)(2,1)} %copy-done.16), kind=kOutput, calls=%fused_computation.29 | convolution fusion | flops 604274688 | bytes 2949120 | tf_op jit(solution)/shard_map/dot_general | solution.py:70
  133.7 12.3 %all-to-all-done.5 = bf16[4,104,768]{2,1,0:T(8,128)(2,1)} async-done(((bf16[4,104,768]{2,1,0:T(8,128)(2,1)}), bf16[4,104,768]{2,1,0:T(8,128)(2,1)}, u32[]{:S(2)}, u32[]{:S(2)}) %all-to-all-start.5) | async-done | bytes 639008 | tf_op jit(solution)/shard_map/all_to_all | solution.py:259
  146.0 3.6 %all-to-all-start.3 = ((bf16[8,128,768]{2,1,0:T(8,128)(2,1)}), bf16[8,128,768]{2,1,0:T(8,128)(2,1)S(1)}, u32[]{:S(2)}, u32[]{:S(2)}) async-start(bf16[8,128,768]{2,1,0:T(8,128)(2,1)} %bitcast.180), calls=%async_computation.3 | async-start | bytes 3145728 | tf_op jit(solution)/shard_map/all_to_all | solution.py:51
  159.2 10.4 %all-to-all-done.3 = bf16[8,128,768]{2,1,0:T(8,128)(2,1)S(1)} async-done(((bf16[8,128,768]{2,1,0:T(8,128)(2,1)}), bf16[8,128,768]{2,1,0:T(8,128)(2,1)S(1)}, u32[]{:S(2)}, u32[]{:S(2)}) %all-to-all-start.3) | async-done | bytes 1572896 | tf_op jit(solution)/shard_map/all_to_all | solution.py:51
  169.6 3.8 %all-to-all-start.6 = ((bf16[4,392,384]{2,1,0:T(8,128)(2,1)}), bf16[4,392,384]{2,1,0:T(8,128)(2,1)S(1)}, u32[]{:S(2)}, u32[]{:S(2)}) async-start(bf16[4,392,384]{2,1,0:T(8,128)(2,1)} %pad_maximum_fusion), calls=%async_computation.6 | async-start | bytes 2408448 | tf_op jit(solution)/shard_map/all_to_all | solution.py:279
  178.2 2.8 %collective-permute-done.7 = bf16[96,768]{1,0:T(8,128)(2,1)} collective-permute-done((bf16[96,768]{1,0:T(8,128)(2,1)}, bf16[96,768]{1,0:T(8,128)(2,1)}, u32[]{:S(2)}, u32[]{:S(2)}) %collective-permute-start.7) | collective-permute-done | bytes 147488 | tf_op jit(solution)/shard_map/ppermute | solution.py:21
  192.0 10.3 %all-to-all-done.6 = bf16[4,392,384]{2,1,0:T(8,128)(2,1)S(1)} async-done(((bf16[4,392,384]{2,1,0:T(8,128)(2,1)}), bf16[4,392,384]{2,1,0:T(8,128)(2,1)S(1)}, u32[]{:S(2)}, u32[]{:S(2)}) %all-to-all-start.6) | async-done | bytes 1204256 | tf_op jit(solution)/shard_map/all_to_all | solution.py:279
  202.3 3.6 %all-to-all-start.2 = ((bf16[8,128,768]{2,1,0:T(8,128)(2,1)}), bf16[8,128,768]{2,1,0:T(8,128)(2,1)S(1)}, u32[]{:S(2)}, u32[]{:S(2)}) async-start(bf16[8,128,768]{2,1,0:T(8,128)(2,1)} %bitcast.34), calls=%async_computation.2 | async-start | bytes 3145728 | tf_op jit(solution)/shard_map/all_to_all | solution.py:51
  209.4 16.9 %all-to-all-done.2 = bf16[8,128,768]{2,1,0:T(8,128)(2,1)S(1)} async-done(((bf16[8,128,768]{2,1,0:T(8,128)(2,1)}), bf16[8,128,768]{2,1,0:T(8,128)(2,1)S(1)}, u32[]{:S(2)}, u32[]{:S(2)}) %all-to-all-start.2) | async-done | bytes 1572896 | tf_op jit(solution)/shard_map/all_to_all | solution.py:51
  227.4 5.0 %collective-permute-done.8 = bf16[392,384]{1,0:T(8,128)(2,1)} collective-permute-done((bf16[392,384]{1,0:T(8,128)(2,1)S(1)}, bf16[392,384]{1,0:T(8,128)(2,1)}, u32[]{:S(2)}, u32[]{:S(2)}) %collective-permute-start.8) | collective-permute-done | bytes 301088 | tf_op jit(solution)/shard_map/ppermute | solution.py:21
  (214 shorter events, 88.6 us)
Async XLA Ops:
  0.6 20.7 %copy-start = (bf16[192,768]{1,0:T(8,128)(2,1)S(1)}, bf16[192,768]{1,0:T(8,128)(2,1)}, u32[]{:S(2)}) copy-start(bf16[192,768]{1,0:T(8,128)(2,1)} %param.26) | copy-start | bytes 884740
  0.7 21.5 %collective-permute-start = (bf16[128,768]{1,0:T(8,128)(2,1)}, bf16[128,768]{1,0:T(8,128)(2,1)S(1)}, u32[]{:S(2)}, u32[]{:S(2)}) collective-permute-start(bf16[128,768]{1,0:T(8,128)(2,1)} %bitcast.155), channel_id=1, source_target_pairs={{0,4},{4,0},{1,5},{5,1},{2,6},{6,2},{3,7},{7,3},{8,12},{12,8},{9,1... | collective-permute-start | bytes 589832 | tf_op jit(solution)/shard_map/ppermute | solution.py:21
  11.8 9.5 %copy-start.19 = (bf16[768,192]{0,1:T(8,128)(2,1)S(1)}, bf16[768,192]{0,1:T(8,128)(2,1)}, u32[]{:S(2)}) copy-start(bf16[768,192]{0,1:T(8,128)(2,1)} %param.28) | copy-start | bytes 884740
  12.7 29.3 %all-to-all-start = ((bf16[4,104,768]{2,1,0:T(8,128)(2,1)}), bf16[4,104,768]{2,1,0:T(8,128)(2,1)S(1)}, u32[]{:S(2)}, u32[]{:S(2)}) async-start(bf16[4,104,768]{2,1,0:T(8,128)(2,1)} %broadcast_in_dim.12), calls=%async_computation | async-start | bytes 1277952 | tf_op jit(solution)/shard_map/all_to_all | solution.py:45
  17.6 6.2 %collective-permute-start.4 = (bf16[128,768]{1,0:T(8,128)(2,1)S(1)}, bf16[128,768]{1,0:T(8,128)(2,1)S(1)}, u32[]{:S(2)}, u32[]{:S(2)}) collective-permute-start(bf16[128,768]{1,0:T(8,128)(2,1)S(1)} %bitcast.160), channel_id=1, source_target_pairs={{0,4},{4,0},{1,5},{5,1},{2,6},{6,2},{3,7},{7,3},{8,12},{12,8},{9,1... | collective-permute-start | bytes 589832 | tf_op jit(solution)/shard_map/ppermute | solution.py:21
  22.2 12.1 %collective-permute-start.1 = (bf16[2,128,768]{2,1,0:T(8,128)(2,1)S(1)}, bf16[2,128,768]{2,1,0:T(8,128)(2,1)S(1)}, u32[]{:S(2)}, u32[]{:S(2)}) collective-permute-start(bf16[2,128,768]{2,1,0:T(8,128)(2,1)S(1)} %maximum_select_fusion.8), channel_id=1, source_target_pairs={{0,2},{1,3},{2,0},{3,1},{4,6},{5,7},{6,4},{7,5},{8,10},{9,11},{10,... | collective-permute-start | bytes 1179656 | tf_op jit(solution)/shard_map/ppermute | solution.py:21
  23.9 16.9 %collective-permute-start.5 = (bf16[2,128,768]{2,1,0:T(8,128)(2,1)S(1)}, bf16[2,128,768]{2,1,0:T(8,128)(2,1)S(1)}, u32[]{:S(2)}, u32[]{:S(2)}) collective-permute-start(bf16[2,128,768]{2,1,0:T(8,128)(2,1)S(1)} %maximum_select_fusion.9), channel_id=1, source_target_pairs={{0,2},{1,3},{2,0},{3,1},{4,6},{5,7},{6,4},{7,5},{8,10},{9,11},{10,... | collective-permute-start | bytes 1179656 | tf_op jit(solution)/shard_map/ppermute | solution.py:21
  35.3 20.2 %collective-permute-start.2 = (bf16[2,2,128,768]{3,2,0,1:T(8,128)(2,1)}, bf16[2,2,128,768]{3,2,0,1:T(8,128)(2,1)}, u32[]{:S(2)}, u32[]{:S(2)}) collective-permute-start(bf16[2,2,128,768]{3,2,0,1:T(8,128)(2,1)} %maximum_select_fusion.3), channel_id=1, source_target_pairs={{0,1},{1,0},{2,3},{3,2},{4,5},{5,4},{6,7},{7,6},{8,9},{9,8},{10,11... | collective-permute-start | bytes 2359304 | tf_op jit(solution)/shard_map/ppermute | solution.py:21
  41.7 16.2 %collective-permute-start.6 = (bf16[2,2,128,768]{3,2,0,1:T(8,128)(2,1)}, bf16[2,2,128,768]{3,2,0,1:T(8,128)(2,1)}, u32[]{:S(2)}, u32[]{:S(2)}) collective-permute-start(bf16[2,2,128,768]{3,2,0,1:T(8,128)(2,1)} %maximum_select_fusion.5), channel_id=1, source_target_pairs={{0,1},{1,0},{2,3},{3,2},{4,5},{5,4},{6,7},{7,6},{8,9},{9,8},{10,11... | collective-permute-start | bytes 2359304 | tf_op jit(solution)/shard_map/ppermute | solution.py:21
  44.1 53.4 %all-to-all-start.1 = ((bf16[4,384,384]{2,1,0:T(8,128)(2,1)}), bf16[4,384,384]{2,1,0:T(8,128)(2,1)}, u32[]{:S(2)}, u32[]{:S(2)}) async-start(bf16[4,384,384]{2,1,0:T(8,128)(2,1)} %broadcast_in_dim.13), calls=%async_computation.1 | async-start | bytes 2359296 | tf_op jit(solution)/shard_map/all_to_all | solution.py:45
  49.8 17.2 %copy-start.20 = (f32[768]{0:T(1024)}, f32[768]{0:T(1024)S(1)}, u32[]{:S(2)}) copy-start(f32[768]{0:T(1024)S(1)} %mul.195) | copy-start | bytes 9220
  52.5 16.3 %collective-permute-start.3 = (bf16[4,96,768]{2,1,0:T(8,128)(2,1)}, bf16[4,96,768]{2,1,0:T(8,128)(2,1)}, u32[]{:S(2)}, u32[]{:S(2)}) collective-permute-start(bf16[4,96,768]{2,1,0:T(8,128)(2,1)} %get-tuple-element.98), channel_id=1, source_target_pairs={{0,4},{4,0},{1,5},{5,1},{2,6},{6,2},{3,7},{7,3},{8,12},{12,8},{9,1... | collective-permute-start | bytes 1769480 | tf_op jit(solution)/shard_map/ppermute | solution.py:21
  110.7 13.5 %all-to-all-start.4 = ((f32[32,1,960]{2,1,0:T(1,128)}), f32[32,1,960]{2,1,0:T(1,128)S(1)}, u32[]{:S(2)}, u32[]{:S(2)}) async-start(f32[32,1,960]{2,1,0:T(1,128)} %reshape.800), calls=%async_computation.4 | async-start | bytes 262144 | tf_op jit(solution)/shard_map/all_to_all | solution.py:305
  117.0 11.3 %copy-start.32 = (f32[128]{0:T(128)S(1)}, f32[128]{0:T(128)}, u32[]{:S(2)}) copy-start(f32[128]{0:T(128)} %convert_reduce_fusion.6) | copy-start | bytes 1540
  117.0 11.5 %copy-start.26 = (f32[4,192]{1,0:T(4,128)S(1)}, f32[4,192]{1,0:T(4,128)}, u32[]{:S(2)}) copy-start(f32[4,192]{1,0:T(4,128)} %get-tuple-element.82) | copy-start | bytes 9220
  117.0 11.6 %copy-start.3 = (bf16[1024,768]{1,0:T(8,128)(2,1)S(1)}, bf16[1024,768]{1,0:T(8,128)(2,1)}, u32[]{:S(2)}) copy-start(bf16[1024,768]{1,0:T(8,128)(2,1)} %get-tuple-element.92) | copy-start | bytes 4718596
  124.2 21.8 %all-to-all-start.5 = ((bf16[4,104,768]{2,1,0:T(8,128)(2,1)}), bf16[4,104,768]{2,1,0:T(8,128)(2,1)}, u32[]{:S(2)}, u32[]{:S(2)}) async-start(bf16[4,104,768]{2,1,0:T(8,128)(2,1)} %pad_maximum_fusion.1), calls=%async_computation.5 | async-start | bytes 1277952 | tf_op jit(solution)/shard_map/all_to_all | solution.py:259
  146.0 23.6 %all-to-all-start.3 = ((bf16[8,128,768]{2,1,0:T(8,128)(2,1)}), bf16[8,128,768]{2,1,0:T(8,128)(2,1)S(1)}, u32[]{:S(2)}, u32[]{:S(2)}) async-start(bf16[8,128,768]{2,1,0:T(8,128)(2,1)} %bitcast.180), calls=%async_computation.3 | async-start | bytes 3145728 | tf_op jit(solution)/shard_map/all_to_all | solution.py:51
  159.2 76.9 %copy-start.28 = (f32[1,192]{1,0:T(1,128)}, f32[1,192]{1,0:T(1,128)S(1)}, u32[]{:S(2)}) copy-start(f32[1,192]{1,0:T(1,128)S(1)} %get-tuple-element.106) | copy-start | bytes 2308
  169.6 32.6 %all-to-all-start.6 = ((bf16[4,392,384]{2,1,0:T(8,128)(2,1)}), bf16[4,392,384]{2,1,0:T(8,128)(2,1)S(1)}, u32[]{:S(2)}, u32[]{:S(2)}) async-start(bf16[4,392,384]{2,1,0:T(8,128)(2,1)} %pad_maximum_fusion), calls=%async_computation.6 | async-start | bytes 2408448 | tf_op jit(solution)/shard_map/all_to_all | solution.py:279
  175.2 5.7 %collective-permute-start.7 = (bf16[96,768]{1,0:T(8,128)(2,1)}, bf16[96,768]{1,0:T(8,128)(2,1)}, u32[]{:S(2)}, u32[]{:S(2)}) collective-permute-start(bf16[96,768]{1,0:T(8,128)(2,1)} %fusion.37), channel_id=1, source_target_pairs={{0,4},{4,0},{1,5},{5,1},{2,6},{6,2},{3,7},{7,3},{8,12},{12,8},{9,1... | collective-permute-start | bytes 442376 | tf_op jit(solution)/shard_map/ppermute | solution.py:21
  202.3 24.1 %all-to-all-start.2 = ((bf16[8,128,768]{2,1,0:T(8,128)(2,1)}), bf16[8,128,768]{2,1,0:T(8,128)(2,1)S(1)}, u32[]{:S(2)}, u32[]{:S(2)}) async-start(bf16[8,128,768]{2,1,0:T(8,128)(2,1)} %bitcast.34), calls=%async_computation.2 | async-start | bytes 3145728 | tf_op jit(solution)/shard_map/all_to_all | solution.py:51
  207.3 19.2 %copy-start.6 = (f32[128,768]{1,0:T(8,128)S(1)}, f32[128,768]{1,0:T(8,128)}, u32[]{:S(2)}) copy-start(f32[128,768]{1,0:T(8,128)} %get-tuple-element.81) | copy-start | bytes 1179652
  207.4 25.0 %collective-permute-start.8 = (bf16[392,384]{1,0:T(8,128)(2,1)S(1)}, bf16[392,384]{1,0:T(8,128)(2,1)}, u32[]{:S(2)}, u32[]{:S(2)}) collective-permute-start(bf16[392,384]{1,0:T(8,128)(2,1)S(1)} %get-tuple-element.102), channel_id=1, source_target_pairs={{0,4},{4,0},{1,5},{5,1},{2,6},{6,2},{3,7},{7,3},{8,12},{12,8},{9,1... | collective-permute-start | bytes 903176 | tf_op jit(solution)/shard_map/ppermute | solution.py:21
  (26 other events, 83.3 us)

commit v2 on v1

v2 whole, which is shorter than its diff:
```python
import jax
import jax.numpy as jnp
from jax import lax
from jax.experimental import pallas as pl
from jax.experimental.pallas import tpu as pltpu
from jax.sharding import PartitionSpec as P

HD = 64
ROT = 16
HALF = ROT // 2
DOC_MAX = 512
ROWS = 256

epsilon = 1e-05
masked_score = -1e30
f32 = jnp.float32
bf16 = jnp.bfloat16


def flipped(block, axis, bit):
    return lax.ppermute(block, axis, [(i, i ^ bit) for i in range(lax.axis_size(axis))])


def ordered(own, other, second, dim):
    return jnp.where(
        second, jnp.stack([other, own], axis=dim), jnp.stack([own, other], axis=dim)
    )


def joined(own, other, second):
    return jnp.where(
        second, jnp.concatenate([other, own], axis=1), jnp.concatenate([own, other], axis=1)
    )


def gather_tokens(rows):
    block = rows
    dims = 0
    first = None
    for axis in ("ctx", "tensor"):
        index = lax.axis_index(axis)
        bit = lax.axis_size(axis) // 2
        while bit:
            other = flipped(block, axis, bit)
            first = other if first is None else first
            block = ordered(block, other, (index & bit) > 0, dims)
            bit //= 2
            dims += 1
    return block.reshape(-1, rows.shape[-1]), first


def gather_dp(block):
    count = lax.axis_size("dp")
    return lax.all_to_all(jnp.broadcast_to(block[None], (count,) + block.shape), "dp", 0, 0)


def exchange_dp(blocks):
    return lax.all_to_all(blocks, "dp", 0, 0)


def total_over(values, axes):
    for axis in axes:
        bit = 1
        while bit < lax.axis_size(axis):
            values = values + flipped(values, axis, bit)
            bit *= 2
    return values


def halve_rows(partial):
    rows = partial.astype(bf16)
    for axis in ("tensor", "ctx"):
        index, size, bit = lax.axis_index(axis), lax.axis_size(axis), 1
        outer = lax.axis_size("ctx") if axis == "tensor" else 1
        while bit < size:
            view = rows.reshape(outer * (size // bit // 2), 2, -1, rows.shape[-1])
            mine = (index // bit) % 2
            away = lax.dynamic_index_in_dim(view, 1 - mine, 1, keepdims=False)
            kept = lax.dynamic_index_in_dim(view, mine, 1, keepdims=False).astype(f32)
            rows = kept + flipped(away, axis, bit).astype(f32)
            last = axis == "ctx" and bit * 2 == size
            rows = rows.astype(f32 if last else bf16).reshape(-1, rows.shape[-1])
            bit *= 2
    return rows


def gelu_pair(preact):
    cumulative = 0.5 * (1.0 + jax.scipy.special.erf(preact * 0.7071067811865476))
    density = jnp.exp(-0.5 * preact * preact) * 0.3989422804014327
    return (preact * cumulative, cumulative + preact * density)


def dot(left, right, dims):
    return lax.dot_general(left, right, (dims, ((), ())), preferred_element_type=f32)


def attention_kernel(
    ctx_ref, all_ref, normed_ref, cot_ref, cos_ref, sin_ref, seg_row_ref, seg_col_ref,
    vectors_ref, mixed_ref, grad_normed_ref, grad_weights_ref, sums_ref, bias_grad_ref,
    weights_ref, first_ref, qkv_ref, grad_ref, feature_ref, dq_ref, dk_ref, dv_ref,
):
    tokens, model = normed_ref.shape
    shares, share = all_ref.shape[0], all_ref.shape[1] - 8
    width = grad_ref.shape[0]
    scale = HD**-0.5
    for s in range(shares):
        weights_ref[s * share : (s + 1) * share, :] = all_ref[s, :share, :]
    small = [all_ref[s, share:, :].astype(f32) for s in range(shares)]
    vectors = jnp.concatenate([piece[:, :share] for piece in small], axis=1)
    vectors_ref[...] = vectors
    bias = sum(piece[7:8, : 3 * width] for piece in small)
    gain, shift = vectors[0:1], vectors[1:2]
    project = weights_ref[:, : 3 * width]
    output = weights_ref[:, 3 * width :]
    chunks = [slice(i, i + ROWS) for i in range(0, tokens, ROWS)]
    for rows in chunks:
        first = (normed_ref[rows, :] * gain + shift).astype(bf16)
        first_ref[rows, :] = first
        qkv_ref[:, rows] = (dot(first, project, ((1,), (0,))) + bias).T
        grad_ref[:, rows] = dot(cot_ref[rows, :], output, ((1,), (0,))).astype(bf16).T
    cosine = cos_ref[...]
    sine = sin_ref[...]
    ones = jnp.ones((8, tokens), bf16)

    def rotate(block, direction):
        first, second = block[:HALF], block[HALF:ROT]
        return jnp.concatenate(
            [
                first * cosine - second * (direction * sine),
                second * cosine + first * (direction * sine),
                block[ROT:],
            ],
            axis=0,
        )

    def head(index, carry):
        start = pl.multiple_of(index * HD, HD)

        def rows(part):
            return pl.ds(part * width + start, HD)

        queries = rotate(qkv_ref[rows(0), :], 1.0).astype(bf16)
        keys = rotate(qkv_ref[rows(1), :], 1.0).astype(bf16)
        values = qkv_ref[rows(2), :].astype(bf16)
        queries = queries * jnp.asarray(scale, bf16)
        grads = grad_ref[pl.ds(start, HD), :]
        key_rows = keys.T
        value_rows = values.T
        dk_ref[...] = jnp.zeros(dk_ref.shape, f32)
        dv_ref[...] = jnp.zeros(dv_ref.shape, f32)
        for block in range(tokens // ROWS):
            begin, end = block * ROWS, (block + 1) * ROWS
            low = max(0, (begin - DOC_MAX + 1) // ROWS * ROWS)
            query = queries[:, begin:end]
            grad = grads[:, begin:end]
            scores = dot(key_rows[low:end], query, ((1,), (0,)))
            key_at = lax.broadcasted_iota(jnp.int32, scores.shape, 0) + low
            query_at = lax.broadcasted_iota(jnp.int32, scores.shape, 1) + begin
            allowed = (seg_col_ref[low:end, :] == seg_row_ref[:, begin:end]) & (
                key_at <= query_at
            )
            scores = jnp.where(allowed, scores, masked_score)
            highest = jnp.max(scores, axis=0, keepdims=True)
            exponent = jnp.exp(scores - highest)
            probs = exponent * (1.0 / jnp.sum(exponent, axis=0, keepdims=True))
            probs_b = probs.astype(bf16)
            attended = dot(values[:, low:end], probs_b, ((1,), (0,))).astype(bf16)
            feature_ref[rows(3), begin:end] = attended
            delta = jnp.sum(
                grad.astype(f32) * attended.astype(f32), axis=0, keepdims=True
            )
            grad_probs = dot(value_rows[low:end], grad, ((1,), (0,)))
            grad_scores = (probs * (grad_probs - delta)).astype(bf16)
            dq_ref[:, begin:end] = dot(keys[:, low:end], grad_scores, ((1,), (0,))) * scale
            dk_ref[:, low:end] += dot(query, grad_scores, ((1,), (1,)))
            dv_ref[:, low:end] += dot(grad, probs_b, ((1,), (1,)))
        for part, result in enumerate(
            (rotate(dq_ref[...], -1.0), rotate(dk_ref[...], -1.0), dv_ref[...])
        ):
            high = result.astype(bf16)
            feature_ref[rows(part), :] = high
            rest = (result - high.astype(f32)).astype(bf16)
            total = dot(ones, high, ((1,), (1,))) + dot(ones, rest, ((1,), (1,)))
            bias_grad_ref[pl.ds(part * (width // HD) + index, 1), :] = total[0:1]
        return carry

    bias_grad_ref[...] = jnp.zeros(bias_grad_ref.shape, f32)
    lax.fori_loop(0, width // HD, head, 0)

    begin = pl.multiple_of(ctx_ref[0] * (2 * width), 2 * width)
    part_one = dot(feature_ref[pl.ds(begin, width), :], first_ref[...], ((1,), (0,)))
    grad_weights_ref[:, :width] = part_one.astype(bf16).T

    @pl.when(ctx_ref[0] == 0)
    def _():
        keys_part = dot(feature_ref[width : 2 * width, :], first_ref[...], ((1,), (0,)))
        grad_weights_ref[:, width:] = keys_part.astype(bf16).T

    @pl.when(ctx_ref[0] != 0)
    def _():
        output_part = dot(feature_ref[3 * width :, :], cot_ref[...], ((1,), (0,)))
        grad_weights_ref[:, width:] = output_part.astype(bf16).T

    total_one = jnp.zeros((1, model), f32)
    total_two = jnp.zeros((1, model), f32)
    for rows in chunks:
        attended = feature_ref[3 * width :, rows].T
        mixed_ref[rows, :] = (0.5 * dot(attended, output, ((1,), (1,)))).astype(bf16)
        grad_first = 0.5 * dot(feature_ref[: 3 * width, rows].T, project, ((1,), (1,)))
        total_one += jnp.sum(grad_first * normed_ref[rows, :], axis=0, keepdims=True)
        total_two += jnp.sum(grad_first, axis=0, keepdims=True)
        grad_normed_ref[rows, :] = (grad_first * gain).astype(bf16)
    sums_ref[0:1, :] = total_one
    sums_ref[1:2, :] = total_two


def feed_kernel(
    ctx_ref, all_ref, normed_ref, cot_ref, vectors_ref, mixed_in_ref, grad_in_ref,
    mixed_ref, grad_normed_ref, grad_weights_ref, sums_ref, bias_grad_ref,
    up_ref, down_ref, second_ref, act_ref, pre_ref,
):
    tokens, model = normed_ref.shape
    shares, share, units = all_ref.shape[0], all_ref.shape[1] // 2, all_ref.shape[2]
    for s in range(shares):
        up_ref[s * share : (s + 1) * share, :] = all_ref[s, :share, :]
        down_ref[s * share : (s + 1) * share, :] = all_ref[s, share:, :]
    gain, shift = vectors_ref[2:3, :], vectors_ref[3:4, :]
    bias = jnp.where(
        ctx_ref[0] > 0, vectors_ref[6:7, units : 2 * units], vectors_ref[6:7, :units]
    )
    up, down = up_ref[...], down_ref[...]
    total_one = jnp.zeros((1, model), f32)
    total_two = jnp.zeros((1, model), f32)
    total_bias = jnp.zeros((1, units), f32)
    for i in range(0, tokens, ROWS):
        rows = slice(i, i + ROWS)
        second = (normed_ref[rows, :] * gain + shift).astype(bf16)
        second_ref[rows, :] = second
        preact = dot(second, up, ((1,), (0,))) + bias
        activated, slope = gelu_pair(preact)
        act = activated.astype(bf16)
        act_ref[:, rows] = act.T
        grad_pre = dot(cot_ref[rows, :], down, ((1,), (0,))) * slope
        total_bias += jnp.sum(grad_pre, axis=0, keepdims=True)
        pre = grad_pre.astype(bf16)
        pre_ref[:, rows] = pre.T
        mixed = dot(act, down, ((1,), (1,))) + mixed_in_ref[rows, :].astype(f32)
        mixed_ref[rows, :] = mixed.astype(bf16)
        grad_second = dot(pre, up, ((1,), (1,)))
        total_one += jnp.sum(grad_second * normed_ref[rows, :], axis=0, keepdims=True)
        total_two += jnp.sum(grad_second, axis=0, keepdims=True)
        grad_normed_ref[rows, :] = (
            grad_second * gain + grad_in_ref[rows, :].astype(f32)
        ).astype(bf16)
    sums_ref[0:1, :] = total_one
    sums_ref[1:2, :] = total_two
    bias_grad_ref[...] = total_bias
    up_part = dot(pre_ref[...], second_ref[...], ((1,), (0,))).astype(bf16).T
    down_part = dot(act_ref[...], cot_ref[...], ((1,), (0,))).astype(bf16).T
    for s in range(shares):
        grad_weights_ref[s, :share, :] = up_part[s * share : (s + 1) * share]
        grad_weights_ref[s, share:, :] = down_part[s * share : (s + 1) * share]


def call(kernel, out_shape, scratch, flops, name, *args):
    whole = pl.BlockSpec(memory_space=pltpu.VMEM)
    scalar = pl.BlockSpec(memory_space=pltpu.SMEM)
    moved = sum(a.size * a.dtype.itemsize for a in args)
    return pl.pallas_call(
        kernel,
        out_shape=[jax.ShapeDtypeStruct(shape, dtype) for shape, dtype in out_shape],
        in_specs=[scalar] + [whole] * (len(args) - 1),
        out_specs=[whole] * len(out_shape),
        scratch_shapes=[pltpu.VMEM(shape, dtype) for shape, dtype in scratch],
        cost_estimate=pl.CostEstimate(flops=flops, transcendentals=0, bytes_accessed=moved),
        name=name,
    )(*args)


def body(
    hidden_in, cotangent, segment_ids, attend_gain, attend_shift, feed_gain, feed_shift,
    project_weight, project_bias, output_weight, output_bias,
    upward_weight, upward_bias, downward_weight, downward_bias,
):
    n_dp, n_ctx, n_tensor = (lax.axis_size(a) for a in ("dp", "ctx", "tensor"))
    dp_index, ctx_index = lax.axis_index("dp"), lax.axis_index("ctx")
    second = ctx_index > 0
    share, _, width = project_weight.shape
    model = share * n_dp
    units = upward_weight.shape[1]
    half_units = units // n_ctx
    heads = width // HD

    def own_half(block, size, axis):
        return lax.dynamic_slice_in_dim(block, ctx_index * size, size, axis)

    hidden_all, hidden_first = gather_tokens(hidden_in[0])
    columns = 4 * width
    vectors = [
        attend_gain, attend_shift, feed_gain, feed_shift, output_bias, downward_bias,
        upward_bias[0],
    ]
    bias_share = HD // n_dp
    bias_wide = lax.dynamic_update_slice_in_dim(
        jnp.zeros((3, heads, HD), bf16), project_bias, dp_index * bias_share, 2
    )
    row = lax.broadcasted_iota(jnp.int32, (8, columns), 0)
    small = jnp.where(row == 7, jnp.pad(bias_wide.reshape(1, -1), ((0, 0), (0, width))), 0)
    for i, vector in enumerate(vectors):
        small = jnp.where(row == i, jnp.pad(vector, (0, columns - share))[None, :], small)
    attention_all = gather_dp(
        jnp.concatenate(
            [
                jnp.concatenate(
                    [project_weight.reshape(share, 3 * width), output_weight.T], axis=1
                ),
                small,
            ],
            axis=0,
        )
    )
    feed_all = gather_dp(
        jnp.concatenate(
            [own_half(upward_weight, half_units, 1), own_half(downward_weight, half_units, 0).T],
            axis=0,
        )
    )
    if share % 32:
        tail = attention_all[:, share:]
        tail = jnp.concatenate(
            [
                tail[:, :7, :share].transpose(1, 0, 2).reshape(7, model),
                jnp.sum(tail[:, 7], axis=0, keepdims=True),
            ],
            axis=0,
        )
        attention_all = jnp.concatenate(
            [attention_all[:, :share].reshape(model, columns), tail], axis=0
        )[None]
        feed_all = feed_all.reshape(n_dp, 2, share, half_units).transpose(1, 0, 2, 3)
        feed_all = feed_all.reshape(1, 2 * model, half_units)

    hidden_rows = hidden_in[0]
    grad_rows = cotangent[0]
    grad_source, _ = lax.optimization_barrier((grad_rows, hidden_first))
    grad_all, _ = gather_tokens(grad_source)
    tokens = hidden_all.shape[0]

    source = hidden_all.astype(f32)
    centred = source - jnp.mean(source, axis=-1, keepdims=True)
    inverse = lax.rsqrt(jnp.mean(centred * centred, axis=-1, keepdims=True) + epsilon)
    normed = centred * inverse

    frequency = 10000.0 ** (-2.0 * jnp.arange(HALF, dtype=f32) / ROT)
    angles = frequency[:, None] * jnp.arange(tokens, dtype=f32)[None, :]
    ctx_scalar = ctx_index.reshape(1).astype(jnp.int32)
    segments = segment_ids[0]
    vectors, mixed, grad_normed, grad_attention, attention_sums, project_bias_grad = call(
        attention_kernel,
        [
            ((8, model), f32), ((tokens, model), bf16), ((tokens, model), bf16),
            ((model, 2 * width), bf16), ((2, model), f32), ((16, HD), f32),
        ],
        [
            ((model, columns), bf16), ((tokens, model), bf16), ((3 * width, tokens), f32),
            ((width, tokens), bf16), ((columns, tokens), bf16),
            ((HD, tokens), f32), ((HD, tokens), f32), ((HD, tokens), f32),
        ],
        tokens * model * columns * 8,
        "attention_part",
        ctx_scalar, attention_all, normed, grad_all, jnp.cos(angles), jnp.sin(angles),
        segments[None, :], segments[:, None],
    )
    attention_parts = exchange_dp(grad_attention.reshape(n_dp, share, 2 * width))

    mixed, grad_normed, grad_feed, feed_sums, upward_bias_grad = call(
        feed_kernel,
        [
            ((tokens, model), bf16), ((tokens, model), bf16), (feed_all.shape, bf16),
            ((2, model), f32), ((1, half_units), f32),
        ],
        [
            ((model, half_units), bf16), ((model, half_units), bf16), ((tokens, model), bf16),
            ((half_units, tokens), bf16), ((half_units, tokens), bf16),
        ],
        tokens * model * half_units * 12,
        "feed_part",
        ctx_scalar, feed_all, normed, grad_all, vectors, mixed, grad_normed,
    )
    if share % 32:
        grad_feed = grad_feed.reshape(2, n_dp, share, half_units).transpose(1, 0, 2, 3)
        grad_feed = grad_feed.reshape(n_dp, 2 * share, half_units)
    grad_feed, attention_parts = lax.optimization_barrier((grad_feed, attention_parts))
    feed_parts = exchange_dp(grad_feed)

    mixed = halve_rows(mixed)
    grad_normed = halve_rows(grad_normed)

    tensor_index = lax.axis_index("tensor")
    project_row = 0.5 * project_bias_grad[: 3 * heads].reshape(1, 3 * width)
    project_row = jnp.pad(project_row, ((0, 0), (0, model - 3 * width)))
    unit_row = jnp.where(
        second,
        jnp.pad(upward_bias_grad, ((0, 0), (half_units, 0))),
        jnp.pad(upward_bias_grad, ((0, 0), (0, half_units))),
    )
    slot = lax.broadcasted_iota(jnp.int32, (n_tensor, 1), 0) == tensor_index
    sums = jnp.concatenate(
        [
            attention_sums,
            feed_sums,
            jnp.sum(grad_rows.astype(f32), axis=0, keepdims=True),
            jnp.where(slot, project_row, 0.0),
            jnp.where(slot, unit_row, 0.0),
        ],
        axis=0,
    )
    sums = total_over(sums, ("tensor", "ctx", "dp"))
    shared = lax.dynamic_slice_in_dim(sums[:5], dp_index * share, share, 1)
    project_sum = lax.dynamic_index_in_dim(sums, 5 + tensor_index, 0, keepdims=False)
    project_bias_grad = lax.dynamic_slice_in_dim(
        project_sum[: 3 * width].reshape(3, heads, HD), dp_index * bias_share, bias_share, 2
    )
    upward_bias_grad = lax.dynamic_slice(
        sums, (5 + n_tensor + tensor_index, dp_index * (units // n_dp)), (1, units // n_dp)
    )

    own_source = hidden_rows.astype(f32)
    hidden_out = own_source + mixed
    hidden_out = (hidden_out + (vectors[4] + vectors[5])).astype(bf16)[None]

    own_centred = own_source - jnp.mean(own_source, axis=-1, keepdims=True)
    own_inverse = lax.rsqrt(jnp.mean(own_centred * own_centred, axis=-1, keepdims=True) + epsilon)
    own_normed = own_centred * own_inverse
    grad_inner = own_inverse * (
        grad_normed
        - jnp.mean(grad_normed, axis=-1, keepdims=True)
        - own_normed * jnp.mean(grad_normed * own_normed, axis=-1, keepdims=True)
    )
    hidden_grad = (grad_rows.astype(f32) + grad_inner).astype(bf16)[None]

    attention_sum = jnp.sum(attention_parts.astype(f32), axis=0)
    attention_own = lax.reduce_precision(attention_sum, 8, 7).astype(bf16)
    attention_both = joined(attention_own, flipped(attention_own, "ctx", 1), second).astype(f32)

    feed_sum = jnp.sum(feed_parts.astype(f32), axis=0)
    feed_own = lax.reduce_precision(feed_sum, 8, 7).astype(bf16)
    feed_both = joined(feed_own, flipped(feed_own, "ctx", 1), second).astype(f32)

    return (
        hidden_out,
        hidden_grad,
        shared[0],
        shared[1],
        shared[2],
        shared[3],
        attention_both[:, : 3 * width].reshape(share, 3, width),
        project_bias_grad,
        attention_both[:, 3 * width :].T,
        shared[4],
        feed_both[:share],
        upward_bias_grad,
        feed_both[share:].T,
        shared[4],
    )


def solution(mesh):
    rows = P("dp", ("ctx", "tensor"), None)
    in_specs = (
        rows, rows, P("dp", None), P("dp"), P("dp"), P("dp"), P("dp"),
        P("dp", None, "tensor"), P(None, "tensor", "dp"), P("tensor", "dp"), P("dp"),
        P("dp", "tensor"), P("tensor", "dp"), P("tensor", "dp"), P("dp"),
    )
    out_specs = (
        rows, rows, P("dp"), P("dp"), P("dp"), P("dp"),
        P("dp", None, "tensor"), P(None, "tensor", "dp"), P("tensor", "dp"), P("dp"),
        P("dp", "tensor"), P("tensor", "dp"), P("tensor", "dp"), P("dp"),
    )
    return jax.shard_map(body, mesh=mesh, in_specs=in_specs, out_specs=out_specs, check_vma=False)
```

time: 238 us -> 168 us (0.71)
  waiting for transfers between devices: 78 us -> 45.7 us
  matrix products: 28.7 us -> 0 us
  Pallas kernels: 14.8 us -> 31 us
  local copies, waits for them, and re-layouts: 41.4 us -> 25.3 us
  other arithmetic: 30.9 us -> 25.1 us
  starting transfers between devices: 41.6 us -> 39.2 us
    all_to_all x5 -> x2, waiting for transfers between devices: 56.1 us -> 10.3 us  [exchange_dp(): return lax.all_to_all(blocks, 'dp', 0, 0)]
    dot_general x12 -> x0, matrix products: 28.7 us -> none  [dot(): lax.dot_general(left, right, (dims, ((), ())), preferred_element_type=f32)]
    pallas_call x1 -> x2, Pallas kernels: 14.8 us -> 31 us  [call(): pl.pallas_call(kernel, out_shape=[jax.ShapeDtypeStruct(shape, dtype) for...]
    all_to_all x5 -> x2, starting transfers between devices: 20.3 us -> 7.79 us  [exchange_dp(): return lax.all_to_all(blocks, 'dp', 0, 0)]
    ppermute x9 -> x19, waiting for transfers between devices: 22 us -> 34.1 us  [flipped(): lax.ppermute(block, axis, [(i, i ^ bit) for i in range(lax.axis_size(axis...]
    ppermute x9 -> x19, starting transfers between devices: 11.6 us -> 21.6 us  [flipped(): lax.ppermute(block, axis, [(i, i ^ bit) for i in range(lax.axis_size(axis...]
    dot_general x3 -> x0, local copies, waits for them, and re-layouts: 5.9 us -> none  [dot(): lax.dot_general(left, right, (dims, ((), ())), preferred_element_type=f32)]
    squeeze x0 -> x6, local copies, waits for them, and re-layouts: none -> 4.76 us  [halve_rows(): away = lax.dynamic_index_in_dim(view, 1 - mine, 1, keepdims=False)]
  transfers between devices with their start and end apart: 16 -> 23, of which waited for: 9 -> 11; matrix products, arithmetic and copies ran while one was open for 35% -> 27% of each run, Pallas kernels for 6% -> 13%
where the time goes in v2:
time: 168 us; the launch traced here: 167 us
  waiting for transfers between devices  45.7 us (27%)
  starting transfers between devices  39.2 us (23%)
  Pallas kernels  31 us (18%)
  local copies, waits for them, and re-layouts  25.3 us (15%)
  other arithmetic  25.1 us (15%)
    ppermute x19, waiting for transfers between devices, flipped(): lax.ppermute(block, axis, [(i, i ^ bit) for i in range(lax.axis_size(axis...  34.1 us
    pallas_call x2, Pallas kernels, call(): pl.pallas_call(kernel, out_shape=[jax.ShapeDtypeStruct(shape, dtype) for...  31 us
    ppermute x19, starting transfers between devices, flipped(): lax.ppermute(block, axis, [(i, i ^ bit) for i in range(lax.axis_size(axis...  21.6 us
    all_to_all x2, waiting for transfers between devices, exchange_dp(): return lax.all_to_all(blocks, 'dp', 0, 0)  10.3 us
    all_to_all x2, starting transfers between devices, gather_dp(): lax.all_to_all(jnp.broadcast_to(block[None], (count,) + block.shape), 'dp...  9.88 us
    all_to_all x2, starting transfers between devices, exchange_dp(): return lax.all_to_all(blocks, 'dp', 0, 0)  7.79 us
    select_n x9, other arithmetic, ordered(): jnp.where(second, jnp.stack([other, own], axis=dim), jnp.stack([own, othe...  7.16 us
    convert_element_type x4, other arithmetic, halve_rows(): rows = rows.astype(f32 if last else bf16).reshape(-1, rows.shape[-1])  5.41 us
  transfers between devices with their start and end apart: 23, of which 11 were waited for; matrix products, arithmetic and copies ran while one was open for 27% of the time, Pallas kernels for 13%

profile of v2, /device:TPU:0, one launch (start us, length us, event | category | flops | bytes accessed | tf_op | source)
XLA Modules:
  0.0 167.4 jit_solution(16417794585392433701)
XLA Ops:
  0.7 3.0 %collective-permute-start = (bf16[128,768]{1,0:T(8,128)(2,1)}, bf16[128,768]{1,0:T(8,128)(2,1)S(1)}, u32[]{:S(2)}, u32[]{:S(2)}) collective-permute-start(bf16[128,768]{1,0:T(8,128)(2,1)} %bitcast.90), channel_id=1, source_target_pairs={{0,4},{4,0},{1,5},{5,1},{2,6},{6,2},{3,7},{7,3},{8,12},{12,8},{9,1... | collective-permute-start | bytes 589832 | tf_op jit(solution)/shard_map/ppermute | solution.py:21
  13.9 5.4 %all-to-all-start.1 = ((bf16[4,200,768]{2,1,0:T(8,128)(2,1)}), bf16[4,200,768]{2,1,0:T(8,128)(2,1)}, u32[]{:S(2)}, u32[]{:S(2)}) async-start(bf16[4,200,768]{2,1,0:T(8,128)(2,1)} %broadcast_in_dim.133), calls=%async_computation.1 | async-start | bytes 2457600 | tf_op jit(solution)/shard_map/all_to_all | solution.py:54
  20.3 1.6 collective-permute-start.1
  23.4 7.3 %collective-permute-done.1 = bf16[2,128,768]{2,1,0:T(8,128)(2,1)S(1)} collective-permute-done((bf16[2,128,768]{2,1,0:T(8,128)(2,1)S(1)}, bf16[2,128,768]{2,1,0:T(8,128)(2,1)S(1)}, u32[]{:S(2)}, u32[]{:S(2)}) %collective-permute-start.1) | collective-permute-done | bytes 393248 | tf_op jit(solution)/shard_map/ppermute | solution.py:21
  35.4 9.0 %collective-permute-done.4 = bf16[2,128,768]{2,1,0:T(8,128)(2,1)} collective-permute-done((bf16[2,128,768]{2,1,0:T(8,128)(2,1)}, bf16[2,128,768]{2,1,0:T(8,128)(2,1)}, u32[]{:S(2)}, u32[]{:S(2)}) %collective-permute-start.4) | collective-permute-done | bytes 393248 | tf_op jit(solution)/shard_map/ppermute | solution.py:21
  44.4 2.1 %maximum_select_fusion.4 = bf16[2,2,128,768]{3,2,0,1:T(8,128)(2,1)} fusion(bf16[2,1,128,768]{3,2,0,1:T(8,128)(2,1)S(1)} %maximum_select_fusion.9, bf16[2,1,128,768]{3,2,0,1:T(8,128)(2,1)} %bitcast.18, pred[]{:T(512)S(6)} %gt.16), kind=kLoop, calls=%fused_computation.14 | loop fusion | flops 1179648 | bytes 1572865 | tf_op jit(solution)/shard_map/jit(_where)/select_n | solution.py:25
  49.8 4.5 %all-to-all-start = ((bf16[4,384,384]{2,1,0:T(8,128)(2,1)}), bf16[4,384,384]{2,1,0:T(8,128)(2,1)}, u32[]{:S(2)}, u32[]{:S(2)}) async-start(bf16[4,384,384]{2,1,0:T(8,128)(2,1)} %broadcast_in_dim.121), calls=%async_computation | async-start | bytes 2359296 | tf_op jit(solution)/shard_map/all_to_all | solution.py:54
  55.5 2.0 %fusion.normed_ref = f32[1024,768]{1,0:T(8,128)} fusion(f32[2,2,2,128,768]{4,3,2,1,0:T(8,128)S(1)} %copy.51, f32[1024]{0:T(1024)S(1)} %bitcast.116, f32[1024]{0:T(1024)S(1)} %bitcast.115), kind=kLoop, calls=%fused_computation.1 | loop fusion | flops 1572864 | bytes 6299648 | tf_op jit(solution)/shard_map/mul | solution.py:352
  57.5 1.6 maximum_select_fusion.1
  60.4 21.4 %attention_part.1 = (f32[8,768]{1,0:T(8,128)}, bf16[1024,768]{1,0:T(8,128)(2,1)}, bf16[1024,768]{1,0:T(8,128)(2,1)}, bf16[768,384]{1,0:T(8,128)(2,1)}, f32[2,768]{1,0:T(2,128)}, /*index=5*/f32[16,64]{1,0:T(8,128)}) custom-call(s32[1]{0:T(128)} %bitcast.ctx_ref, bf16[4,200,768]{2,1,0:T(8,128)(2,1)} %all-to-all-done.1.all_ref, f32[1024,768]{1,0:T(8,128)} %fusion.normed_ref, ...), custom_call_target="tpu_custom_call" | custom-call | flops 4831838208 | bytes 6021124 | tf_op jit(solution)/shard_map/attention_part/pallas_call | solution.py:269
  83.6 9.6 %feed_part.1 = (bf16[1024,768]{1,0:T(8,128)(2,1)}, bf16[1024,768]{1,0:T(8,128)(2,1)}, bf16[4,384,384]{2,1,0:T(8,128)(2,1)}, f32[2,768]{1,0:T(2,128)}, f32[1,384]{1,0:T(1,128)}) custom-call(s32[1]{0:T(128)} %bitcast.ctx_ref, bf16[4,384,384]{2,1,0:T(8,128)(2,1)} %all-to-all-done.all_ref, f32[1024,768]{1,0:T(8,128)} %fusion.normed_ref, ...), custom_call_target="tpu_custom_call" | custom-call | flops 3623878656 | bytes 9068548 | tf_op jit(solution)/shard_map/feed_part/pallas_call | solution.py:269
  95.0 2.2 %dynamic-slice_bitcast_fusion = bf16[4,128,768]{2,1,0:T(8,128)(2,1)} fusion(bf16[4,2,128,768]{3,2,1,0:T(8,128)(2,1)} %bitcast.105, s32[]{:T(128)S(6)} %select_n.263), kind=kLoop, calls=%fused_computation.20 | loop fusion | bytes 1572868 | tf_op jit(solution)/shard_map/jit(dynamic_index_in_dim)/squeeze | solution.py:78
  97.7 1.6 collective-permute-start.13
  99.4 4.2 %all-to-all-start.2 = ((bf16[4,192,384]{2,1,0:T(8,128)(2,1)}), bf16[4,192,384]{2,1,0:T(8,128)(2,1)S(1)}, u32[]{:S(2)}, u32[]{:S(2)}) async-start(bf16[4,192,384]{2,1,0:T(8,128)(2,1)} %bitcast.45), calls=%async_computation.2 | async-start | bytes 1179648 | tf_op jit(solution)/shard_map/all_to_all | solution.py:58
  104.2 3.5 %collective-permute-done.14 = f32[13,768]{1,0:T(8,128)S(1)} collective-permute-done((f32[13,768]{1,0:T(8,128)S(1)}, f32[13,768]{1,0:T(8,128)S(1)}, u32[]{:S(2)}, u32[]{:S(2)}) %collective-permute-start.14) | collective-permute-done | bytes 39968 | tf_op jit(solution)/shard_map/ppermute | solution.py:21
  107.8 2.1 %collective-permute-start.15 = (f32[13,768]{1,0:T(8,128)S(1)}, f32[13,768]{1,0:T(8,128)S(1)}, u32[]{:S(2)}, u32[]{:S(2)}) collective-permute-start(f32[13,768]{1,0:T(8,128)S(1)} %add.202), channel_id=1, source_target_pairs={{0,8},{8,0},{16,24},{24,16},{1,9},{9,1},{17,25},{25,17},{2,10},{10... | collective-permute-start | bytes 119816 | tf_op jit(solution)/shard_map/ppermute | solution.py:21
  110.8 3.4 %collective-permute-done.15 = f32[13,768]{1,0:T(8,128)S(1)} collective-permute-done((f32[13,768]{1,0:T(8,128)S(1)}, f32[13,768]{1,0:T(8,128)S(1)}, u32[]{:S(2)}, u32[]{:S(2)}) %collective-permute-start.15) | collective-permute-done | bytes 39968 | tf_op jit(solution)/shard_map/ppermute | solution.py:21
  114.3 4.6 %collective-permute-start.16 = (f32[13,768]{1,0:T(8,128)S(1)}, f32[13,768]{1,0:T(8,128)S(1)}, u32[]{:S(2)}, u32[]{:S(2)}) collective-permute-start(f32[13,768]{1,0:T(8,128)S(1)} %add.203), channel_id=1, source_target_pairs={{0,16},{8,24},{16,0},{24,8},{1,17},{9,25},{17,1},{25,9},{2,18},{10... | collective-permute-start | bytes 119816 | tf_op jit(solution)/shard_map/ppermute | solution.py:21
  119.8 1.7 %collective-permute-done.16 = f32[13,768]{1,0:T(8,128)S(1)} collective-permute-done((f32[13,768]{1,0:T(8,128)S(1)}, f32[13,768]{1,0:T(8,128)S(1)}, u32[]{:S(2)}, u32[]{:S(2)}) %collective-permute-start.16) | collective-permute-done | bytes 39968 | tf_op jit(solution)/shard_map/ppermute | solution.py:21
  123.6 1.6 fusion.2
  126.5 3.6 %all-to-all-start.3 = ((bf16[4,384,384]{2,1,0:T(8,128)(2,1)}), bf16[4,384,384]{2,1,0:T(8,128)(2,1)S(1)}, u32[]{:S(2)}, u32[]{:S(2)}) async-start(bf16[4,384,384]{2,1,0:T(8,128)(2,1)} %get-tuple-element.41), calls=%async_computation.3 | async-start | bytes 2359296 | tf_op jit(solution)/shard_map/all_to_all | solution.py:58
  142.4 2.1 %collective-permute-done.7 = bf16[2,128,768]{2,1,0:T(8,128)(2,1)} collective-permute-done((bf16[2,128,768]{2,1,0:T(8,128)(2,1)}, bf16[2,128,768]{2,1,0:T(8,128)(2,1)}, u32[]{:S(2)}, u32[]{:S(2)}) %collective-permute-start.7) | collective-permute-done | bytes 393248 | tf_op jit(solution)/shard_map/ppermute | solution.py:21
  147.1 10.3 %all-to-all-done.3 = bf16[4,384,384]{2,1,0:T(8,128)(2,1)S(1)} async-done(((bf16[4,384,384]{2,1,0:T(8,128)(2,1)}), bf16[4,384,384]{2,1,0:T(8,128)(2,1)S(1)}, u32[]{:S(2)}, u32[]{:S(2)}) %all-to-all-start.3) | async-done | bytes 1179680 | tf_op jit(solution)/shard_map/all_to_all | solution.py:58
  159.2 6.5 %collective-permute-done.18 = bf16[384,384]{1,0:T(8,128)(2,1)S(1)} collective-permute-done((bf16[384,384]{1,0:T(8,128)(2,1)S(1)}, bf16[384,384]{1,0:T(8,128)(2,1)S(1)}, u32[]{:S(2)}, u32[]{:S(2)}) %collective-permute-start.18) | collective-permute-done | bytes 294944 | tf_op jit(solution)/shard_map/ppermute | solution.py:21
  (145 shorter events, 51.3 us)
Async XLA Ops:
  0.7 19.6 %collective-permute-start = (bf16[128,768]{1,0:T(8,128)(2,1)}, bf16[128,768]{1,0:T(8,128)(2,1)S(1)}, u32[]{:S(2)}, u32[]{:S(2)}) collective-permute-start(bf16[128,768]{1,0:T(8,128)(2,1)} %bitcast.90), channel_id=1, source_target_pairs={{0,4},{4,0},{1,5},{5,1},{2,6},{6,2},{3,7},{7,3},{8,12},{12,8},{9,1... | collective-permute-start | bytes 589832 | tf_op jit(solution)/shard_map/ppermute | solution.py:21
  13.9 34.8 %all-to-all-start.1 = ((bf16[4,200,768]{2,1,0:T(8,128)(2,1)}), bf16[4,200,768]{2,1,0:T(8,128)(2,1)}, u32[]{:S(2)}, u32[]{:S(2)}) async-start(bf16[4,200,768]{2,1,0:T(8,128)(2,1)} %broadcast_in_dim.133), calls=%async_computation.1 | async-start | bytes 2457600 | tf_op jit(solution)/shard_map/all_to_all | solution.py:54
  20.3 10.4 %collective-permute-start.1 = (bf16[2,128,768]{2,1,0:T(8,128)(2,1)S(1)}, bf16[2,128,768]{2,1,0:T(8,128)(2,1)S(1)}, u32[]{:S(2)}, u32[]{:S(2)}) collective-permute-start(bf16[2,128,768]{2,1,0:T(8,128)(2,1)S(1)} %maximum_select_fusion.7), channel_id=1, source_target_pairs={{0,2},{1,3},{2,0},{3,1},{4,6},{5,7},{6,4},{7,5},{8,10},{9,11},{10,... | collective-permute-start | bytes 1179656 | tf_op jit(solution)/shard_map/ppermute | solution.py:21
  22.8 9.0 %collective-permute-start.3 = (bf16[128,768]{1,0:T(8,128)(2,1)S(1)}, bf16[128,768]{1,0:T(8,128)(2,1)S(1)}, u32[]{:S(2)}, u32[]{:S(2)}) collective-permute-start(bf16[128,768]{1,0:T(8,128)(2,1)S(1)} %bitcast.92), channel_id=1, source_target_pairs={{0,4},{4,0},{1,5},{5,1},{2,6},{6,2},{3,7},{7,3},{8,12},{12,8},{9,1... | collective-permute-start | bytes 589832 | tf_op jit(solution)/shard_map/ppermute | solution.py:21
  31.7 16.1 %collective-permute-start.2 = (bf16[2,2,128,768]{3,2,0,1:T(8,128)(2,1)}, bf16[2,2,128,768]{3,2,0,1:T(8,128)(2,1)S(1)}, u32[]{:S(2)}, u32[]{:S(2)}) collective-permute-start(bf16[2,2,128,768]{3,2,0,1:T(8,128)(2,1)} %maximum_select_fusion.2), channel_id=1, source_target_pairs={{0,1},{1,0},{2,3},{3,2},{4,5},{5,4},{6,7},{7,6},{8,9},{9,8},{10,11... | collective-permute-start | bytes 2359304 | tf_op jit(solution)/shard_map/ppermute | solution.py:21
  32.5 11.8 %collective-permute-start.4 = (bf16[2,128,768]{2,1,0:T(8,128)(2,1)}, bf16[2,128,768]{2,1,0:T(8,128)(2,1)}, u32[]{:S(2)}, u32[]{:S(2)}) collective-permute-start(bf16[2,128,768]{2,1,0:T(8,128)(2,1)} %maximum_select_fusion.8), channel_id=1, source_target_pairs={{0,2},{1,3},{2,0},{3,1},{4,6},{5,7},{6,4},{7,5},{8,10},{9,11},{10,... | collective-permute-start | bytes 1179656 | tf_op jit(solution)/shard_map/ppermute | solution.py:21
  46.5 11.0 %collective-permute-start.5 = (bf16[2,2,128,768]{3,2,0,1:T(8,128)(2,1)}, bf16[2,2,128,768]{3,2,0,1:T(8,128)(2,1)}, u32[]{:S(2)}, u32[]{:S(2)}) collective-permute-start(bf16[2,2,128,768]{3,2,0,1:T(8,128)(2,1)} %maximum_select_fusion.4), channel_id=1, source_target_pairs={{0,1},{1,0},{2,3},{3,2},{4,5},{5,4},{6,7},{7,6},{8,9},{9,8},{10,11... | collective-permute-start | bytes 2359304 | tf_op jit(solution)/shard_map/ppermute | solution.py:21
  49.8 33.8 %all-to-all-start = ((bf16[4,384,384]{2,1,0:T(8,128)(2,1)}), bf16[4,384,384]{2,1,0:T(8,128)(2,1)}, u32[]{:S(2)}, u32[]{:S(2)}) async-start(bf16[4,384,384]{2,1,0:T(8,128)(2,1)} %broadcast_in_dim.121), calls=%async_computation | async-start | bytes 2359296 | tf_op jit(solution)/shard_map/all_to_all | solution.py:54
  94.9 2.8 %collective-permute-start.12 = (f32[13,768]{1,0:T(8,128)S(1)}, f32[13,768]{1,0:T(8,128)S(1)}, u32[]{:S(2)}, u32[]{:S(2)}) collective-permute-start(f32[13,768]{1,0:T(8,128)S(1)} %concatenate.119), channel_id=1, source_target_pairs={{0,1},{1,0},{2,3},{3,2},{4,5},{5,4},{6,7},{7,6},{8,9},{9,8},{10,11... | collective-permute-start | bytes 119816 | tf_op jit(solution)/shard_map/ppermute | solution.py:21
  97.2 26.4 %collective-permute-start.9 = (bf16[4,128,768]{2,1,0:T(8,128)(2,1)}, bf16[4,128,768]{2,1,0:T(8,128)(2,1)}, u32[]{:S(2)}, u32[]{:S(2)}) collective-permute-start(bf16[4,128,768]{2,1,0:T(8,128)(2,1)} %dynamic-slice_bitcast_fusion), channel_id=1, source_target_pairs={{0,1},{1,0},{2,3},{3,2},{4,5},{5,4},{6,7},{7,6},{8,9},{9,8},{10,11... | collective-permute-start | bytes 2359304 | tf_op jit(solution)/shard_map/ppermute | solution.py:21
  97.7 6.0 %collective-permute-start.13 = (f32[13,768]{1,0:T(8,128)S(1)}, f32[13,768]{1,0:T(8,128)S(1)}, u32[]{:S(2)}, u32[]{:S(2)}) collective-permute-start(f32[13,768]{1,0:T(8,128)S(1)} %add.200), channel_id=1, source_target_pairs={{0,2},{1,3},{2,0},{3,1},{4,6},{5,7},{6,4},{7,5},{8,10},{9,11},{10,... | collective-permute-start | bytes 119816 | tf_op jit(solution)/shard_map/ppermute | solution.py:21
  99.4 27.0 %all-to-all-start.2 = ((bf16[4,192,384]{2,1,0:T(8,128)(2,1)}), bf16[4,192,384]{2,1,0:T(8,128)(2,1)S(1)}, u32[]{:S(2)}, u32[]{:S(2)}) async-start(bf16[4,192,384]{2,1,0:T(8,128)(2,1)} %bitcast.45), calls=%async_computation.2 | async-start | bytes 1179648 | tf_op jit(solution)/shard_map/all_to_all | solution.py:58
  103.6 4.2 %collective-permute-start.14 = (f32[13,768]{1,0:T(8,128)S(1)}, f32[13,768]{1,0:T(8,128)S(1)}, u32[]{:S(2)}, u32[]{:S(2)}) collective-permute-start(f32[13,768]{1,0:T(8,128)S(1)} %add.201), channel_id=1, source_target_pairs={{0,4},{4,0},{1,5},{5,1},{2,6},{6,2},{3,7},{7,3},{8,12},{12,8},{9,1... | collective-permute-start | bytes 119816 | tf_op jit(solution)/shard_map/ppermute | solution.py:21
  107.8 6.5 %collective-permute-start.15 = (f32[13,768]{1,0:T(8,128)S(1)}, f32[13,768]{1,0:T(8,128)S(1)}, u32[]{:S(2)}, u32[]{:S(2)}) collective-permute-start(f32[13,768]{1,0:T(8,128)S(1)} %add.202), channel_id=1, source_target_pairs={{0,8},{8,0},{16,24},{24,16},{1,9},{9,1},{17,25},{25,17},{2,10},{10... | collective-permute-start | bytes 119816 | tf_op jit(solution)/shard_map/ppermute | solution.py:21
  114.3 7.3 %collective-permute-start.16 = (f32[13,768]{1,0:T(8,128)S(1)}, f32[13,768]{1,0:T(8,128)S(1)}, u32[]{:S(2)}, u32[]{:S(2)}) collective-permute-start(f32[13,768]{1,0:T(8,128)S(1)} %add.203), channel_id=1, source_target_pairs={{0,16},{8,24},{16,0},{24,8},{1,17},{9,25},{17,1},{25,9},{2,18},{10... | collective-permute-start | bytes 119816 | tf_op jit(solution)/shard_map/ppermute | solution.py:21
  119.7 11.1 %collective-permute-start.6 = (bf16[4,128,768]{2,1,0:T(8,128)(2,1)}, bf16[4,128,768]{2,1,0:T(8,128)(2,1)}, u32[]{:S(2)}, u32[]{:S(2)}) collective-permute-start(bf16[4,128,768]{2,1,0:T(8,128)(2,1)} %dynamic-slice_bitcast_fusion.1), channel_id=1, source_target_pairs={{0,1},{1,0},{2,3},{3,2},{4,5},{5,4},{6,7},{7,6},{8,9},{9,8},{10,11... | collective-permute-start | bytes 2359304 | tf_op jit(solution)/shard_map/ppermute | solution.py:21
  123.0 43.9 %copy-start.9 = (f32[1,192]{1,0:T(1,128)}, f32[1,192]{1,0:T(1,128)S(1)}, u32[]{:S(2)}) copy-start(f32[1,192]{1,0:T(1,128)S(1)} %get-tuple-element.76) | copy-start | bytes 2308
  125.9 13.7 %collective-permute-start.10 = (bf16[2,128,768]{2,1,0:T(8,128)(2,1)}, bf16[2,128,768]{2,1,0:T(8,128)(2,1)}, u32[]{:S(2)}, u32[]{:S(2)}) collective-permute-start(bf16[2,128,768]{2,1,0:T(8,128)(2,1)} %dynamic-slice_bitcast_fusion.2), channel_id=1, source_target_pairs={{0,2},{1,3},{2,0},{3,1},{4,6},{5,7},{6,4},{7,5},{8,10},{9,11},{10,... | collective-permute-start | bytes 1179656 | tf_op jit(solution)/shard_map/ppermute | solution.py:21
  126.5 31.0 %all-to-all-start.3 = ((bf16[4,384,384]{2,1,0:T(8,128)(2,1)}), bf16[4,384,384]{2,1,0:T(8,128)(2,1)S(1)}, u32[]{:S(2)}, u32[]{:S(2)}) async-start(bf16[4,384,384]{2,1,0:T(8,128)(2,1)} %get-tuple-element.41), calls=%async_computation.3 | async-start | bytes 2359296 | tf_op jit(solution)/shard_map/all_to_all | solution.py:58
  130.2 5.4 %collective-permute-start.17 = (bf16[192,384]{1,0:T(8,128)(2,1)S(1)}, bf16[192,384]{1,0:T(8,128)(2,1)S(1)}, u32[]{:S(2)}, u32[]{:S(2)}) collective-permute-start(bf16[192,384]{1,0:T(8,128)(2,1)S(1)} %reduce-precision_convert_fusion.1), channel_id=1, source_target_pairs={{0,4},{4,0},{1,5},{5,1},{2,6},{6,2},{3,7},{7,3},{8,12},{12,8},{9,1... | collective-permute-start | bytes 442376 | tf_op jit(solution)/shard_map/ppermute | solution.py:21
  134.0 10.5 %collective-permute-start.7 = (bf16[2,128,768]{2,1,0:T(8,128)(2,1)}, bf16[2,128,768]{2,1,0:T(8,128)(2,1)}, u32[]{:S(2)}, u32[]{:S(2)}) collective-permute-start(bf16[2,128,768]{2,1,0:T(8,128)(2,1)} %dynamic-slice_bitcast_fusion.3), channel_id=1, source_target_pairs={{0,2},{1,3},{2,0},{3,1},{4,6},{5,7},{6,4},{7,5},{8,10},{9,11},{10,... | collective-permute-start | bytes 1179656 | tf_op jit(solution)/shard_map/ppermute | solution.py:21
  140.8 5.9 %collective-permute-start.11 = (bf16[1,128,768]{2,1,0:T(8,128)(2,1)S(1)}, bf16[1,128,768]{2,1,0:T(8,128)(2,1)S(1)}, u32[]{:S(2)}, u32[]{:S(2)}) collective-permute-start(bf16[1,128,768]{2,1,0:T(8,128)(2,1)S(1)} %constant_dynamic-slice_fusion.3), channel_id=1, source_target_pairs={{0,4},{4,0},{1,5},{5,1},{2,6},{6,2},{3,7},{7,3},{8,12},{12,8},{9,1... | collective-permute-start | bytes 589832 | tf_op jit(solution)/shard_map/ppermute | solution.py:21
  145.7 12.5 %collective-permute-start.8 = (bf16[1,128,768]{2,1,0:T(8,128)(2,1)S(1)}, bf16[1,128,768]{2,1,0:T(8,128)(2,1)S(1)}, u32[]{:S(2)}, u32[]{:S(2)}) collective-permute-start(bf16[1,128,768]{2,1,0:T(8,128)(2,1)S(1)} %constant_dynamic-slice_fusion.4), channel_id=1, source_target_pairs={{0,4},{4,0},{1,5},{5,1},{2,6},{6,2},{3,7},{7,3},{8,12},{12,8},{9,1... | collective-permute-start | bytes 589832 | tf_op jit(solution)/shard_map/ppermute | solution.py:21
  157.6 8.0 %collective-permute-start.18 = (bf16[384,384]{1,0:T(8,128)(2,1)S(1)}, bf16[384,384]{1,0:T(8,128)(2,1)S(1)}, u32[]{:S(2)}, u32[]{:S(2)}) collective-permute-start(bf16[384,384]{1,0:T(8,128)(2,1)S(1)} %reduce-precision_convert_fusion), channel_id=1, source_target_pairs={{0,4},{4,0},{1,5},{5,1},{2,6},{6,2},{3,7},{7,3},{8,12},{12,8},{9,1... | collective-permute-start | bytes 884744 | tf_op jit(solution)/shard_map/ppermute | solution.py:21
  (9 other events, 74.5 us)

commit v3 on v2

--- a/solution.py
+++ b/solution.py
@@ -1,3 +1,5 @@
+import functools
+
 import jax
 import jax.numpy as jnp
 from jax import lax
@@ -33,55 +35,22 @@
     )
 
 
-def gather_tokens(rows):
+def gather_tokens(rows, ctx_first):
+    steps = [("ctx", 1, 0), ("tensor", 2, 1)] if ctx_first else [("tensor", 2, 0), ("ctx", 1, 0)]
     block = rows
-    dims = 0
-    first = None
-    for axis in ("ctx", "tensor"):
-        index = lax.axis_index(axis)
-        bit = lax.axis_size(axis) // 2
-        while bit:
-            other = flipped(block, axis, bit)
-            first = other if first is None else first
-            block = ordered(block, other, (index & bit) > 0, dims)
-            bit //= 2
-            dims += 1
-    return block.reshape(-1, rows.shape[-1]), first
-
-
-def gather_dp(block):
+    for axis, bit, dim in steps + [("tensor", 1, 2)]:
+        upper = (lax.axis_index(axis) & bit) > 0
+        block = ordered(block, flipped(block, axis, bit), upper, dim)
+    return block.reshape(-1, rows.shape[-1])
+
+
+def shifted(block, distance):
     count = lax.axis_size("dp")
-    return lax.all_to_all(jnp.broadcast_to(block[None], (count,) + block.shape), "dp", 0, 0)
+    return lax.ppermute(block, "dp", [(i, (i + distance) % count) for i in range(count)])
 
 
 def exchange_dp(blocks):
     return lax.all_to_all(blocks, "dp", 0, 0)
-
-
-def total_over(values, axes):
-    for axis in axes:
-        bit = 1
-        while bit < lax.axis_size(axis):
-            values = values + flipped(values, axis, bit)
-            bit *= 2
-    return values
-
-
-def halve_rows(partial):
-    rows = partial.astype(bf16)
-    for axis in ("tensor", "ctx"):
-        index, size, bit = lax.axis_index(axis), lax.axis_size(axis), 1
-        outer = lax.axis_size("ctx") if axis == "tensor" else 1
-        while bit < size:
-            view = rows.reshape(outer * (size // bit // 2), 2, -1, rows.shape[-1])
-            mine = (index // bit) % 2
-            away = lax.dynamic_index_in_dim(view, 1 - mine, 1, keepdims=False)
-            kept = lax.dynamic_index_in_dim(view, mine, 1, keepdims=False).astype(f32)
-            rows = kept + flipped(away, axis, bit).astype(f32)
-            last = axis == "ctx" and bit * 2 == size
-            rows = rows.astype(f32 if last else bf16).reshape(-1, rows.shape[-1])
-            bit *= 2
-    return rows
 
 
 def gelu_pair(preact):
@@ -94,18 +63,95 @@
     return lax.dot_general(left, right, (dims, ((), ())), preferred_element_type=f32)
 
 
-def attention_kernel(
-    ctx_ref, all_ref, normed_ref, cot_ref, cos_ref, sin_ref, seg_row_ref, seg_col_ref,
-    vectors_ref, mixed_ref, grad_normed_ref, grad_weights_ref, sums_ref, bias_grad_ref,
-    weights_ref, first_ref, qkv_ref, grad_ref, feature_ref, dq_ref, dk_ref, dv_ref,
+def pack_kernel(dp_ref, project_ref, output_ref, bias_ref, *refs):
+    vector_refs, packed_ref = refs[:-1], refs[-1]
+    _, share, width = project_ref.shape
+    _, heads, part = bias_ref.shape
+    for i in range(3):
+        packed_ref[:share, i * width : (i + 1) * width] = project_ref[i]
+    packed_ref[:share, 3 * width :] = output_ref[...].T
+    rest = jnp.zeros((1, 4 * width - share), f32)
+    rows = [
+        jnp.concatenate([ref[...].astype(f32).reshape(1, share), rest], axis=1)
+        for ref in vector_refs
+    ]
+    lane = lax.broadcasted_iota(jnp.int32, (1, HD), 1)
+    own = (lane >= dp_ref[0] * part) & (lane < (dp_ref[0] + 1) * part)
+    pieces = []
+    for kind in range(3):
+        for head in range(heads):
+            piece = bias_ref[kind, head : head + 1, :].astype(f32)
+            pieces.append(jnp.where(own, jnp.concatenate([piece] * (HD // part), axis=1), 0.0))
+    rows.append(jnp.concatenate(pieces + [jnp.zeros((1, width), f32)], axis=1))
+    packed_ref[share:, :] = jnp.concatenate(rows, axis=0).astype(bf16)
+
+
+def pack_feed_kernel(ctx_ref, up_ref, down_ref, packed_ref):
+    share, units = up_ref.shape
+    for half in range(2):
+
+        @pl.when(ctx_ref[0] == half)
+        def _():
+            lanes = slice(half * (units // 2), (half + 1) * (units // 2))
+            for copy in range(packed_ref.shape[0]):
+                packed_ref[copy, :share, :] = up_ref[:, lanes]
+                packed_ref[copy, share:, :] = down_ref[:, lanes]
+
+
+def rows_at(index, size):
+    return pl.ds(pl.multiple_of(index * size, size), size)
+
+
+def split_kernel(
+    bits_ref, kept_ref, got_ref, mixed_kept_ref, mixed_away_ref, grad_kept_ref, grad_away_ref
 ):
+    size = kept_ref.shape[1] // 4
+    high, ctx = bits_ref[0], bits_ref[1]
+
+    def total(which, c, h):
+        rows = rows_at(c * 2 + h, size)
+        both = kept_ref[which, rows, :].astype(f32) + got_ref[which, rows, :].astype(f32)
+        return both.astype(bf16)
+
+    for i in range(2):
+        rows = slice(i * size, (i + 1) * size)
+        mixed_kept_ref[rows, :] = total(0, i, high)
+        mixed_away_ref[rows, :] = total(0, i, 1 - high)
+        grad_kept_ref[rows, :] = total(1, ctx, i)
+        grad_away_ref[rows, :] = total(1, 1 - ctx, i)
+
+
+def halve_kernel(bit_ref, kept_ref, got_ref, kept_out_ref, away_out_ref):
+    size = kept_ref.shape[0] // 2
+
+    def total(half):
+        rows = rows_at(half, size)
+        return kept_ref[rows, :].astype(f32) + got_ref[rows, :].astype(f32)
+
+    kept_out_ref[...] = total(bit_ref[0])
+    away_out_ref[...] = total(1 - bit_ref[0]).astype(bf16)
+
+
+def attention_kernel(shares, place_ref, *refs):
+    piece_refs, refs = refs[:shares], refs[shares:]
+    normed_ref, cot_ref, cos_ref, sin_ref, seg_row_ref, seg_col_ref = refs[:6]
+    refs = refs[6:]
+    vectors_ref, mixed_ref, grad_normed_ref, sums_ref, bias_grad_ref = refs[:5]
+    part_refs, refs = refs[5 : 5 + shares], refs[5 + shares :]
+    (
+        weights_ref, small_ref, first_ref, qkv_ref, grad_ref, feature_ref, grad_weights_ref,
+        dq_ref, dk_ref, dv_ref,
+    ) = refs
     tokens, model = normed_ref.shape
-    shares, share = all_ref.shape[0], all_ref.shape[1] - 8
+    share = piece_refs[0].shape[0] - 8
     width = grad_ref.shape[0]
     scale = HD**-0.5
-    for s in range(shares):
-        weights_ref[s * share : (s + 1) * share, :] = all_ref[s, :share, :]
-    small = [all_ref[s, share:, :].astype(f32) for s in range(shares)]
+    ctx, dp = place_ref[0], place_ref[1]
+    for d, ref in enumerate(piece_refs):
+        source = lax.rem(dp + (shares - d), shares)
+        weights_ref[rows_at(source, share), :] = ref[:share, :]
+        small_ref[source] = ref[share:, :].astype(f32)
+    small = [small_ref[i] for i in range(shares)]
     vectors = jnp.concatenate([piece[:, :share] for piece in small], axis=1)
     vectors_ref[...] = vectors
     bias = sum(piece[7:8, : 3 * width] for piece in small)
@@ -187,19 +233,22 @@
     bias_grad_ref[...] = jnp.zeros(bias_grad_ref.shape, f32)
     lax.fori_loop(0, width // HD, head, 0)
 
-    begin = pl.multiple_of(ctx_ref[0] * (2 * width), 2 * width)
+    begin = pl.multiple_of(ctx * (2 * width), 2 * width)
     part_one = dot(feature_ref[pl.ds(begin, width), :], first_ref[...], ((1,), (0,)))
     grad_weights_ref[:, :width] = part_one.astype(bf16).T
 
-    @pl.when(ctx_ref[0] == 0)
+    @pl.when(ctx == 0)
     def _():
         keys_part = dot(feature_ref[width : 2 * width, :], first_ref[...], ((1,), (0,)))
         grad_weights_ref[:, width:] = keys_part.astype(bf16).T
 
-    @pl.when(ctx_ref[0] != 0)
+    @pl.when(ctx != 0)
     def _():
         output_part = dot(feature_ref[3 * width :, :], cot_ref[...], ((1,), (0,)))
         grad_weights_ref[:, width:] = output_part.astype(bf16).T
+
+    for d, ref in enumerate(part_refs):
+        ref[...] = grad_weights_ref[rows_at(lax.rem(dp + d, shares), share), :]
 
     total_one = jnp.zeros((1, model), f32)
     total_two = jnp.zeros((1, model), f32)
@@ -216,7 +265,7 @@
 
 def feed_kernel(
     ctx_ref, all_ref, normed_ref, cot_ref, vectors_ref, mixed_in_ref, grad_in_ref,
-    mixed_ref, grad_normed_ref, grad_weights_ref, sums_ref, bias_grad_ref,
+    kept_ref, away_ref, grad_weights_ref, sums_ref, bias_grad_ref,
     up_ref, down_ref, second_ref, act_ref, pre_ref,
 ):
     tokens, model = normed_ref.shape
@@ -229,6 +278,14 @@
         ctx_ref[0] > 0, vectors_ref[6:7, units : 2 * units], vectors_ref[6:7, :units]
     )
     up, down = up_ref[...], down_ref[...]
+    low = ctx_ref[1] > 0
+
+    def divide(which, start, block):
+        first, last = block[: ROWS // 2], block[ROWS // 2 :]
+        rows = slice(start // 2, start // 2 + ROWS // 2)
+        kept_ref[which, rows, :] = jnp.where(low, last, first)
+        away_ref[which, rows, :] = jnp.where(low, first, last)
+
     total_one = jnp.zeros((1, model), f32)
     total_two = jnp.zeros((1, model), f32)
     total_bias = jnp.zeros((1, units), f32)
@@ -245,13 +302,12 @@
         pre = grad_pre.astype(bf16)
         pre_ref[:, rows] = pre.T
         mixed = dot(act, down, ((1,), (1,))) + mixed_in_ref[rows, :].astype(f32)
-        mixed_ref[rows, :] = mixed.astype(bf16)
+        divide(0, i, mixed.astype(bf16))
         grad_second = dot(pre, up, ((1,), (1,)))
         total_one += jnp.sum(grad_second * normed_ref[rows, :], axis=0, keepdims=True)
         total_two += jnp.sum(grad_second, axis=0, keepdims=True)
-        grad_normed_ref[rows, :] = (
-            grad_second * gain + grad_in_ref[rows, :].astype(f32)
-        ).astype(bf16)
+        grad_normed = grad_second * gain + grad_in_ref[rows, :].astype(f32)
+        divide(1, i, grad_normed.astype(bf16))
     sums_ref[0:1, :] = total_one
     sums_ref[1:2, :] = total_two
     bias_grad_ref[...] = total_bias
@@ -291,42 +347,30 @@
     half_units = units // n_ctx
     heads = width // HD
 
-    def own_half(block, size, axis):
-        return lax.dynamic_slice_in_dim(block, ctx_index * size, size, axis)
-
-    hidden_all, hidden_first = gather_tokens(hidden_in[0])
+    hidden_all = gather_tokens(hidden_in[0], True)
     columns = 4 * width
-    vectors = [
+    bias_share = HD // n_dp
+    tensor_index = lax.axis_index("tensor")
+
+    def scalars(*values):
+        return jnp.stack([jnp.asarray(v, jnp.int32) for v in values])
+
+    (packed,) = call(
+        pack_kernel, [((share + 8, columns), bf16)], [], 0, "pack_attention",
+        scalars(dp_index), project_weight.transpose(1, 0, 2), output_weight, project_bias,
         attend_gain, attend_shift, feed_gain, feed_shift, output_bias, downward_bias,
         upward_bias[0],
-    ]
-    bias_share = HD // n_dp
-    bias_wide = lax.dynamic_update_slice_in_dim(
-        jnp.zeros((3, heads, HD), bf16), project_bias, dp_index * bias_share, 2
-    )
-    row = lax.broadcasted_iota(jnp.int32, (8, columns), 0)
-    small = jnp.where(row == 7, jnp.pad(bias_wide.reshape(1, -1), ((0, 0), (0, width))), 0)
-    for i, vector in enumerate(vectors):
-        small = jnp.where(row == i, jnp.pad(vector, (0, columns - share))[None, :], small)
-    attention_all = gather_dp(
-        jnp.concatenate(
-            [
-                jnp.concatenate(
-                    [project_weight.reshape(share, 3 * width), output_weight.T], axis=1
-                ),
-                small,
-            ],
-            axis=0,
-        )
-    )
-    feed_all = gather_dp(
-        jnp.concatenate(
-            [own_half(upward_weight, half_units, 1), own_half(downward_weight, half_units, 0).T],
-            axis=0,
-        )
-    )
-    if share % 32:
-        tail = attention_all[:, share:]
+    )
+    (feed_block,) = call(
+        pack_feed_kernel, [((n_dp, 2 * share, half_units), bf16)], [], 0, "pack_feed",
+        scalars(ctx_index), upward_weight, downward_weight.T,
+    )
+    few = n_dp <= 4
+    if few:
+        pieces = [packed] + [shifted(packed, d) for d in range(1, n_dp)]
+    else:
+        everything = exchange_dp(jnp.broadcast_to(packed[None], (n_dp,) + packed.shape))
+        tail = everything[:, share:]
         tail = jnp.concatenate(
             [
                 tail[:, :7, :share].transpose(1, 0, 2).reshape(7, model),
@@ -334,16 +378,19 @@
             ],
             axis=0,
         )
-        attention_all = jnp.concatenate(
-            [attention_all[:, :share].reshape(model, columns), tail], axis=0
-        )[None]
+        pieces = [
+            jnp.concatenate([everything[:, :share].reshape(model, columns), tail], axis=0)
+        ]
+    shares = len(pieces)
+    feed_block, hidden_all = lax.optimization_barrier((feed_block, hidden_all))
+    feed_all = exchange_dp(feed_block)
+    if not few:
         feed_all = feed_all.reshape(n_dp, 2, share, half_units).transpose(1, 0, 2, 3)
         feed_all = feed_all.reshape(1, 2 * model, half_units)
 
     hidden_rows = hidden_in[0]
     grad_rows = cotangent[0]
-    grad_source, _ = lax.optimization_barrier((grad_rows, hidden_first))
-    grad_all, _ = gather_tokens(grad_source)
+    grad_all = gather_tokens(grad_rows, False)
     tokens = hidden_all.shape[0]
 
     source = hidden_all.astype(f32)
@@ -353,31 +400,38 @@
 
     frequency = 10000.0 ** (-2.0 * jnp.arange(HALF, dtype=f32) / ROT)
     angles = frequency[:, None] * jnp.arange(tokens, dtype=f32)[None, :]
-    ctx_scalar = ctx_index.reshape(1).astype(jnp.int32)
     segments = segment_ids[0]
-    vectors, mixed, grad_normed, grad_attention, attention_sums, project_bias_grad = call(
-        attention_kernel,
+    vectors, mixed, grad_normed, attention_sums, project_bias_grad, *attention_parts = call(
+        functools.partial(attention_kernel, shares),
         [
             ((8, model), f32), ((tokens, model), bf16), ((tokens, model), bf16),
-            ((model, 2 * width), bf16), ((2, model), f32), ((16, HD), f32),
-        ],
+            ((2, model), f32), ((16, HD), f32),
+        ]
+        + [((model // shares, 2 * width), bf16)] * shares,
         [
-            ((model, columns), bf16), ((tokens, model), bf16), ((3 * width, tokens), f32),
-            ((width, tokens), bf16), ((columns, tokens), bf16),
+            ((model, columns), bf16), ((shares, 8, columns), f32), ((tokens, model), bf16),
+            ((3 * width, tokens), f32), ((width, tokens), bf16), ((columns, tokens), bf16),
+            ((model, 2 * width), bf16),
             ((HD, tokens), f32), ((HD, tokens), f32), ((HD, tokens), f32),
         ],
         tokens * model * columns * 8,
         "attention_part",
-        ctx_scalar, attention_all, normed, grad_all, jnp.cos(angles), jnp.sin(angles),
-        segments[None, :], segments[:, None],
-    )
-    attention_parts = exchange_dp(grad_attention.reshape(n_dp, share, 2 * width))
-
-    mixed, grad_normed, grad_feed, feed_sums, upward_bias_grad = call(
+        scalars(ctx_index, dp_index if few else 0), *pieces, normed, grad_all,
+        jnp.cos(angles), jnp.sin(angles), segments[None, :], segments[:, None],
+    )
+    if few:
+        attention_parts = attention_parts[:1] + [
+            shifted(attention_parts[d], d) for d in range(1, n_dp)
+        ]
+    else:
+        exchanged = exchange_dp(attention_parts[0].reshape(n_dp, share, 2 * width))
+        attention_parts = [exchanged[i] for i in range(n_dp)]
+
+    kept, away, grad_feed, feed_sums, upward_bias_grad = call(
         feed_kernel,
         [
-            ((tokens, model), bf16), ((tokens, model), bf16), (feed_all.shape, bf16),
-            ((2, model), f32), ((1, half_units), f32),
+            ((2, tokens // 2, model), bf16), ((2, tokens // 2, model), bf16),
+            (feed_all.shape, bf16), ((2, model), f32), ((1, half_units), f32),
         ],
         [
             ((model, half_units), bf16), ((model, half_units), bf16), ((tokens, model), bf16),
@@ -385,18 +439,19 @@
         ],
         tokens * model * half_units * 12,
         "feed_part",
-        ctx_scalar, feed_all, normed, grad_all, vectors, mixed, grad_normed,
-    )
-    if share % 32:
+        scalars(ctx_index, tensor_index % 2),
+        feed_all, normed, grad_all, vectors, mixed, grad_normed,
+    )
+    kept, away, grad_feed, feed_sums, upward_bias_grad, attention_parts = (
+        lax.optimization_barrier(
+            (kept, away, grad_feed, feed_sums, upward_bias_grad, attention_parts)
+        )
+    )
+    if not few:
         grad_feed = grad_feed.reshape(2, n_dp, share, half_units).transpose(1, 0, 2, 3)
         grad_feed = grad_feed.reshape(n_dp, 2 * share, half_units)
-    grad_feed, attention_parts = lax.optimization_barrier((grad_feed, attention_parts))
     feed_parts = exchange_dp(grad_feed)
 
-    mixed = halve_rows(mixed)
-    grad_normed = halve_rows(grad_normed)
-
-    tensor_index = lax.axis_index("tensor")
     project_row = 0.5 * project_bias_grad[: 3 * heads].reshape(1, 3 * width)
     project_row = jnp.pad(project_row, ((0, 0), (0, model - 3 * width)))
     unit_row = jnp.where(
@@ -415,7 +470,37 @@
         ],
         axis=0,
     )
-    sums = total_over(sums, ("tensor", "ctx", "dp"))
+    def added(values, axis, bit):
+        return values + flipped(values, axis, bit)
+
+    high_bit = tensor_index // 2
+    quarter = ((tokens // 4, model), bf16)
+    away, sums = lax.optimization_barrier(
+        (flipped(away, "tensor", 1), added(sums, "tensor", 1))
+    )
+    mixed_kept, mixed_away, grad_kept, grad_away = call(
+        split_kernel, [quarter] * 4, [], 0, "split",
+        scalars(high_bit, ctx_index), kept, away,
+    )
+    sums = added(added(sums, "tensor", 2), "ctx", 1)
+    grad_away, sums = lax.optimization_barrier((flipped(grad_away, "ctx", 1), sums))
+    eighths = [((tokens // 8, model), f32), ((tokens // 8, model), bf16)]
+    grad_normed, grad_away = call(
+        halve_kernel, eighths, [], 0, "halve_grad", scalars(high_bit), grad_kept, grad_away
+    )
+    mixed, mixed_away = call(
+        halve_kernel, eighths, [], 0, "halve_mixed",
+        scalars(ctx_index), mixed_kept, flipped(mixed_away, "tensor", 2),
+    )
+    bit = 1
+    while bit < n_dp:
+        sums = added(sums, "dp", bit)
+        bit *= 2
+    mixed = mixed + flipped(mixed_away, "ctx", 1).astype(f32)
+    grad_normed = grad_normed + flipped(grad_away, "tensor", 2).astype(f32)
+    mixed, grad_normed, sums, feed_parts = lax.optimization_barrier(
+        (mixed, grad_normed, sums, feed_parts)
+    )
     shared = lax.dynamic_slice_in_dim(sums[:5], dp_index * share, share, 1)
     project_sum = lax.dynamic_index_in_dim(sums, 5 + tensor_index, 0, keepdims=False)
     project_bias_grad = lax.dynamic_slice_in_dim(
@@ -439,7 +524,7 @@
     )
     hidden_grad = (grad_rows.astype(f32) + grad_inner).astype(bf16)[None]
 
-    attention_sum = jnp.sum(attention_parts.astype(f32), axis=0)
+    attention_sum = sum(part.astype(f32) for part in attention_parts)
     attention_own = lax.reduce_precision(attention_sum, 8, 7).astype(bf16)
     attention_both = joined(attention_own, flipped(attention_own, "ctx", 1), second).astype(f32)
 

time: 168 us -> 142 us (0.85)
  waiting for transfers between devices: 45.7 us -> 29.6 us
  local copies, waits for them, and re-layouts: 25.3 us -> 11.8 us
  Pallas kernels: 31 us -> 43 us
  other arithmetic: 25.1 us -> 16.4 us
    pallas_call x2 -> x7, Pallas kernels: 31 us -> 43 us  [call(): pl.pallas_call(kernel, out_shape=[jax.ShapeDtypeStruct(shape, dtype) for...]
    ppermute x0 -> x6, starting transfers between devices: none -> 11.4 us  [shifted(): lax.ppermute(block, 'dp', [(i, (i + distance) % count) for i in range(cou...]
    all_to_all x2, waiting for transfers between devices: 10.3 us -> 0.01 us  [exchange_dp(): return lax.all_to_all(blocks, 'dp', 0, 0)]
    all_to_all x2 -> x0, starting transfers between devices: 9.88 us -> none  [gather_dp(): lax.all_to_all(jnp.broadcast_to(block[None], (count,) + block.shape), 'dp...]
    convert_element_type x6 -> x0, other arithmetic: 6.63 us -> none  [the longest x4 5.41 us: halve_rows(): rows = rows.astype(f32 if last else bf16).reshape(-1, rows.shape[-1])]
    squeeze x6 -> x0, local copies, waits for them, and re-layouts: 4.76 us -> none  [halve_rows(): away = lax.dynamic_index_in_dim(view, 1 - mine, 1, keepdims=False)]
    ppermute x19 -> x18, waiting for transfers between devices: 34.1 us -> 29.6 us  [flipped(): lax.ppermute(block, axis, [(i, i ^ bit) for i in range(lax.axis_size(axis...]
    pad x8 -> x0, local copies, waits for them, and re-layouts: 3.99 us -> none  [the longest x7 3.97 us: body(): jnp.pad(vector, (0, columns - share))[None, :]]
  transfers between devices with their start and end apart: 23 -> 26, of which waited for: 11 -> 8; matrix products, arithmetic and copies ran while one was open for 27% -> 17% of each run, Pallas kernels for 13% -> 30%
where the time goes in v3:
time: 142 us
  Pallas kernels  43 us (30%)
  starting transfers between devices  39.7 us (28%)
  waiting for transfers between devices  29.6 us (21%)
  other arithmetic  16.4 us (12%)
  local copies, waits for them, and re-layouts  11.8 us (8%)
    pallas_call x7, Pallas kernels, call(): pl.pallas_call(kernel, out_shape=[jax.ShapeDtypeStruct(shape, dtype) for...  43 us
    ppermute x18, waiting for transfers between devices, flipped(): lax.ppermute(block, axis, [(i, i ^ bit) for i in range(lax.axis_size(axis...  29.6 us
    ppermute x18, starting transfers between devices, flipped(): lax.ppermute(block, axis, [(i, i ^ bit) for i in range(lax.axis_size(axis...  18.9 us
    ppermute x6, starting transfers between devices, shifted(): lax.ppermute(block, 'dp', [(i, (i + distance) % count) for i in range(cou...  11.4 us
    all_to_all x2, starting transfers between devices, exchange_dp(): return lax.all_to_all(blocks, 'dp', 0, 0)  9.37 us
    select_n x10, other arithmetic, ordered(): jnp.where(second, jnp.stack([other, own], axis=dim), jnp.stack([own, othe...  4.48 us
    unnamed x35, local copies, waits for them, and re-layouts  4.46 us
  transfers between devices with their start and end apart: 26, of which 8 were waited for; matrix products, arithmetic and copies ran while one was open for 17% of the time, Pallas kernels for 30%

profile of v3, /device:TPU:0, one launch (start us, length us, event | category | flops | bytes accessed | tf_op | source)
XLA Modules:
  0.0 141.6 jit_solution(11262391993997526892)
XLA Ops:
  0.7 3.0 %collective-permute-start = (bf16[128,768]{1,0:T(8,128)(2,1)}, bf16[128,768]{1,0:T(8,128)(2,1)S(1)}, u32[]{:S(2)}, u32[]{:S(2)}) collective-permute-start(bf16[128,768]{1,0:T(8,128)(2,1)} %bitcast.65), channel_id=1, source_target_pairs={{0,4},{4,0},{1,5},{5,1},{2,6},{6,2},{3,7},{7,3},{8,12},{12,8},{9,1... | collective-permute-start | bytes 589832 | tf_op jit(solution)/shard_map/ppermute | solution.py:23
  4.9 2.0 %pack_attention.1.refs_0_ = bf16[200,768]{1,0:T(8,128)(2,1)} custom-call(s32[1]{0:T(128)} %bitcast.24.dp_ref, bf16[3,192,192]{2,1,0:T(8,128)(2,1)} %bitcast.85, bf16[192,192]{1,0:T(8,128)(2,1)} %output_ref.1, bf16[3,3,16]{2,1,0:T(4,128)(2,1)} %bias_ref.1, bf16[192]{0:T(256)(128)(2,1)} %refs_0_.1, bf16[192]{0:T(256)(128)(2,1)} %refs_1_.1, ...), custom_call_target="tpu_custom_call" | custom-call | bytes 297892 | tf_op jit(solution)/shard_map/pack_attention/pallas_call | solution.py:325
  8.5 2.6 %collective-permute-start.7 = (bf16[200,768]{1,0:T(8,128)(2,1)}, bf16[200,768]{1,0:T(8,128)(2,1)}, u32[]{:S(2)}, u32[]{:S(2)}) collective-permute-start(bf16[200,768]{1,0:T(8,128)(2,1)} %pack_attention.1.refs_0_), channel_id=1, source_target_pairs={{0,16},{8,24},{16,0},{24,8},{1,17},{9,25},{17,1},{25,9},{2,18},{10... | collective-permute-start | bytes 921608 | tf_op jit(solution)/shard_map/ppermute | solution.py:49
  15.6 4.8 %collective-permute-done.3 = bf16[128,768]{1,0:T(8,128)(2,1)S(1)} collective-permute-done((bf16[128,768]{1,0:T(8,128)(2,1)}, bf16[128,768]{1,0:T(8,128)(2,1)S(1)}, u32[]{:S(2)}, u32[]{:S(2)}) %collective-permute-start.3) | collective-permute-done | bytes 196640 | tf_op jit(solution)/shard_map/ppermute | solution.py:23
  22.0 4.7 %collective-permute-done.1 = bf16[2,128,768]{2,1,0:T(8,128)(2,1)S(1)} collective-permute-done((bf16[2,128,768]{2,1,0:T(8,128)(2,1)S(1)}, bf16[2,128,768]{2,1,0:T(8,128)(2,1)S(1)}, u32[]{:S(2)}, u32[]{:S(2)}) %collective-permute-start.1) | collective-permute-done | bytes 393248 | tf_op jit(solution)/shard_map/ppermute | solution.py:23
  30.1 2.2 %pack_feed.1 = bf16[4,384,384]{2,1,0:T(8,128)(2,1)} custom-call(s32[1]{0:T(128)} %bitcast.1.ctx_ref.bit_ref, bf16[192,768]{1,0:T(8,128)(2,1)} %up_ref.1, bf16[192,768]{1,0:T(8,128)(2,1)} %bitcast.86), custom_call_target="tpu_custom_call" | custom-call | bytes 589828 | tf_op jit(solution)/shard_map/pack_feed/pallas_call | solution.py:325
  34.9 4.3 %all-to-all-start = ((bf16[4,384,384]{2,1,0:T(8,128)(2,1)}), bf16[4,384,384]{2,1,0:T(8,128)(2,1)}, u32[]{:S(2)}, u32[]{:S(2)}) async-start(bf16[4,384,384]{2,1,0:T(8,128)(2,1)} %pack_feed.1), calls=%async_computation | async-start | bytes 2359296 | tf_op jit(solution)/shard_map/all_to_all | solution.py:53
  39.2 1.6 %maximum_select_fusion.1 = bf16[2,2,2,128,768]{4,3,1,2,0:T(8,128)(2,1)S(1)} fusion(bf16[2,2,1,128,768]{4,3,1,2,0:T(8,128)(2,1)S(1)} %maximum_select_fusion.5, bf16[2,2,1,128,768]{4,3,1,2,0:T(8,128)(2,1)} %bitcast.20, pred[]{:T(512)S(6)} %gt.15), kind=kLoop, calls=%fused_computation.7 | loop fusion | flops 2359296 | bytes 3145729 | tf_op jit(solution)/shard_map/jit(_where)/select_n | solution.py:27
  43.0 2.1 %fusion.refs_4_.normed_ref = f32[1024,768]{1,0:T(8,128)} fusion(bf16[1024,768]{1,0:T(8,128)(2,1)S(1)} %bitcast.64, f32[1024]{0:T(1024)S(1)} %add_rsqrt_fusion, f32[1024]{0:T(1024)S(1)} %broadcast_multiply_fusion), kind=kLoop, calls=%fused_computation.2 | loop fusion | flops 2359296 | bytes 4726784 | tf_op jit(solution)/shard_map/mul | solution.py:399
  45.1 21.8 %attention_part.1 = (f32[8,768]{1,0:T(8,128)}, bf16[1024,768]{1,0:T(8,128)(2,1)}, bf16[1024,768]{1,0:T(8,128)(2,1)}, f32[2,768]{1,0:T(2,128)}, f32[16,64]{1,0:T(...) custom-call(s32[2]{0:T(128)} %pad_add_fusion.2.place_ref, ...), custom_call_target="tpu_custom_call" | custom-call | flops 4831838208 | bytes 6021128 | tf_op jit(solution)/shard_map/attention_part/pallas_call | solution.py:325
  66.9 2.0 %collective-permute-start.9 = (bf16[192,384]{1,0:T(8,128)(2,1)}, bf16[192,384]{1,0:T(8,128)(2,1)S(1)}, u32[]{:S(2)}, u32[]{:S(2)}) collective-permute-start(bf16[192,384]{1,0:T(8,128)(2,1)} %get-tuple-element.66), channel_id=1, source_target_pairs={{0,8},{8,16},{16,24},{24,0},{1,9},{9,17},{17,25},{25,1},{2,10},{10... | collective-permute-start | bytes 442376 | tf_op jit(solution)/shard_map/ppermute | solution.py:49
  68.9 2.4 %collective-permute-start.10 = (bf16[192,384]{1,0:T(8,128)(2,1)}, bf16[192,384]{1,0:T(8,128)(2,1)S(1)}, u32[]{:S(2)}, u32[]{:S(2)}) collective-permute-start(bf16[192,384]{1,0:T(8,128)(2,1)} %get-tuple-element.67), channel_id=1, source_target_pairs={{0,16},{8,24},{16,0},{24,8},{1,17},{9,25},{17,1},{25,9},{2,18},{10... | collective-permute-start | bytes 442376 | tf_op jit(solution)/shard_map/ppermute | solution.py:49
  72.7 9.7 %feed_part.1 = (bf16[2,512,768]{2,1,0:T(8,128)(2,1)}, bf16[2,512,768]{2,1,0:T(8,128)(2,1)}, bf16[4,384,384]{2,1,0:T(8,128)(2,1)}, f32[2,768]{1,0:T(2,128)}, f32[1,384]{1,0:T(1,128)}) custom-call(s32[2]{0:T(128)} %pad_add_fusion.1.ctx_ref, bf16[4,384,384]{2,1,0:T(8,128)(2,1)} %all-to-all-done.all_ref, f32[1024,768]{1,0:T(8,128)} %fusion.refs_4_.normed_ref, ...), custom_call_target="tpu_custom_call" | custom-call | flops 3623878656 | bytes 9068552 | tf_op jit(solution)/shard_map/feed_part/pallas_call | solution.py:325
  83.2 5.1 %all-to-all-start.1 = ((bf16[4,384,384]{2,1,0:T(8,128)(2,1)}), bf16[4,384,384]{2,1,0:T(8,128)(2,1)S(1)}, u32[]{:S(2)}, u32[]{:S(2)}) async-start(bf16[4,384,384]{2,1,0:T(8,128)(2,1)} %get-tuple-element.87), calls=%async_computation.1 | async-start | bytes 2359296 | tf_op jit(solution)/shard_map/all_to_all | solution.py:53
  91.1 3.3 %split.1 = (bf16[256,768]{1,0:T(8,128)(2,1)}, bf16[256,768]{1,0:T(8,128)(2,1)}, bf16[256,768]{1,0:T(8,128)(2,1)}, bf16[256,768]{1,0:T(8,128)(2,1)}) custom-call(s32[2]{0:T(128)} %pad_add_fusion.bits_ref, bf16[2,512,768]{2,1,0:T(8,128)(2,1)} %get-tuple-element.69.kept_ref, bf16[2,512,768]{2,1,0:T(8,128)(2,1)} %copy-done.2), custom_call_target="tpu_custom_call" | custom-call | bytes 3145736 | tf_op jit(solution)/shard_map/split/pallas_call | solution.py:325
  97.6 1.6 %collective-permute-start.14 = (bf16[256,768]{1,0:T(8,128)(2,1)}, bf16[256,768]{1,0:T(8,128)(2,1)S(1)}, u32[]{:S(2)}, u32[]{:S(2)}) collective-permute-start(bf16[256,768]{1,0:T(8,128)(2,1)} %get-tuple-element.77), channel_id=1, source_target_pairs={{0,2},{1,3},{2,0},{3,1},{4,6},{5,7},{6,4},{7,5},{8,10},{9,11},{10,... | collective-permute-start | bytes 1179656 | tf_op jit(solution)/shard_map/ppermute | solution.py:23
  99.7 9.9 %collective-permute-done.17 = f32[13,768]{1,0:T(8,128)S(1)} collective-permute-done((f32[13,768]{1,0:T(8,128)S(1)}, f32[13,768]{1,0:T(8,128)S(1)}, u32[]{:S(2)}, u32[]{:S(2)}) %collective-permute-start.17) | collective-permute-done | bytes 39968 | tf_op jit(solution)/shard_map/ppermute | solution.py:23
  110.9 2.7 %collective-permute-done.18 = f32[13,768]{1,0:T(8,128)S(1)} collective-permute-done((f32[13,768]{1,0:T(8,128)S(1)}, f32[13,768]{1,0:T(8,128)S(1)}, u32[]{:S(2)}, u32[]{:S(2)}) %collective-permute-start.18) | collective-permute-done | bytes 39968 | tf_op jit(solution)/shard_map/ppermute | solution.py:23
  113.7 2.1 %collective-permute-start.20 = (f32[13,768]{1,0:T(8,128)S(1)}, f32[13,768]{1,0:T(8,128)S(1)}, u32[]{:S(2)}, u32[]{:S(2)}) collective-permute-start(f32[13,768]{1,0:T(8,128)S(1)} %add.107), channel_id=1, source_target_pairs={{0,8},{8,0},{16,24},{24,16},{1,9},{9,1},{17,25},{25,17},{2,10},{10... | collective-permute-start | bytes 119816 | tf_op jit(solution)/shard_map/ppermute | solution.py:23
  116.6 2.0 %halve_mixed.1 = (f32[128,768]{1,0:T(8,128)}, bf16[128,768]{1,0:T(8,128)(2,1)}) custom-call(s32[1]{0:T(128)} %bitcast.1.ctx_ref.bit_ref, bf16[256,768]{1,0:T(8,128)(2,1)} %get-tuple-element.76.kept_ref, bf16[256,768]{1,0:T(8,128)(2,1)} %copy-done.4), custom_call_target="tpu_custom_call" | custom-call | bytes 786436 | tf_op jit(solution)/shard_map/halve_mixed/pallas_call | solution.py:325
  119.1 2.4 %collective-permute-start.21 = (f32[13,768]{1,0:T(8,128)S(1)}, f32[13,768]{1,0:T(8,128)S(1)}, u32[]{:S(2)}, u32[]{:S(2)}) collective-permute-start(f32[13,768]{1,0:T(8,128)S(1)} %add.109), channel_id=1, source_target_pairs={{0,16},{8,24},{16,0},{24,8},{1,17},{9,25},{17,1},{25,9},{2,18},{10... | collective-permute-start | bytes 119816 | tf_op jit(solution)/shard_map/ppermute | solution.py:23
  123.8 2.0 %halve_grad.1 = (f32[128,768]{1,0:T(8,128)}, bf16[128,768]{1,0:T(8,128)(2,1)}) custom-call(s32[1]{0:T(128)} %bitcast.2.bit_ref, bf16[256,768]{1,0:T(8,128)(2,1)} %get-tuple-element.80.kept_ref, bf16[256,768]{1,0:T(8,128)(2,1)} %copy-done.3), custom_call_target="tpu_custom_call" | custom-call | bytes 786436 | tf_op jit(solution)/shard_map/halve_grad/pallas_call | solution.py:325
  127.4 4.2 %collective-permute-done.19 = bf16[128,768]{1,0:T(8,128)(2,1)S(1)} collective-permute-done((bf16[128,768]{1,0:T(8,128)(2,1)}, bf16[128,768]{1,0:T(8,128)(2,1)S(1)}, u32[]{:S(2)}, u32[]{:S(2)}) %collective-permute-start.19) | collective-permute-done | bytes 196640 | tf_op jit(solution)/shard_map/ppermute | solution.py:23
  137.7 2.2 %collective-permute-done.23 = bf16[384,384]{1,0:T(8,128)(2,1)S(1)} collective-permute-done((bf16[384,384]{1,0:T(8,128)(2,1)S(1)}, bf16[384,384]{1,0:T(8,128)(2,1)S(1)}, u32[]{:S(2)}, u32[]{:S(2)}) %collective-permute-start.23) | collective-permute-done | bytes 294944 | tf_op jit(solution)/shard_map/ppermute | solution.py:23
  (136 shorter events, 39.8 us)
Async XLA Ops:
  0.7 13.3 %collective-permute-start = (bf16[128,768]{1,0:T(8,128)(2,1)}, bf16[128,768]{1,0:T(8,128)(2,1)S(1)}, u32[]{:S(2)}, u32[]{:S(2)}) collective-permute-start(bf16[128,768]{1,0:T(8,128)(2,1)} %bitcast.65), channel_id=1, source_target_pairs={{0,4},{4,0},{1,5},{5,1},{2,6},{6,2},{3,7},{7,3},{8,12},{12,8},{9,1... | collective-permute-start | bytes 589832 | tf_op jit(solution)/shard_map/ppermute | solution.py:23
  6.9 38.2 %collective-permute-start.6 = (bf16[200,768]{1,0:T(8,128)(2,1)}, bf16[200,768]{1,0:T(8,128)(2,1)}, u32[]{:S(2)}, u32[]{:S(2)}) collective-permute-start(bf16[200,768]{1,0:T(8,128)(2,1)} %pack_attention.1.refs_0_), channel_id=1, source_target_pairs={{0,8},{8,16},{16,24},{24,0},{1,9},{9,17},{17,25},{25,1},{2,10},{10... | collective-permute-start | bytes 921608 | tf_op jit(solution)/shard_map/ppermute | solution.py:49
  8.5 36.6 %collective-permute-start.7 = (bf16[200,768]{1,0:T(8,128)(2,1)}, bf16[200,768]{1,0:T(8,128)(2,1)}, u32[]{:S(2)}, u32[]{:S(2)}) collective-permute-start(bf16[200,768]{1,0:T(8,128)(2,1)} %pack_attention.1.refs_0_), channel_id=1, source_target_pairs={{0,16},{8,24},{16,0},{24,8},{1,17},{9,25},{17,1},{25,9},{2,18},{10... | collective-permute-start | bytes 921608 | tf_op jit(solution)/shard_map/ppermute | solution.py:49
  11.1 34.1 %collective-permute-start.8 = (bf16[200,768]{1,0:T(8,128)(2,1)}, bf16[200,768]{1,0:T(8,128)(2,1)}, u32[]{:S(2)}, u32[]{:S(2)}) collective-permute-start(bf16[200,768]{1,0:T(8,128)(2,1)} %pack_attention.1.refs_0_), channel_id=1, source_target_pairs={{0,24},{8,0},{16,8},{24,16},{1,25},{9,1},{17,9},{25,17},{2,26},{10... | collective-permute-start | bytes 921608 | tf_op jit(solution)/shard_map/ppermute | solution.py:49
  12.4 8.0 %collective-permute-start.3 = (bf16[128,768]{1,0:T(8,128)(2,1)}, bf16[128,768]{1,0:T(8,128)(2,1)S(1)}, u32[]{:S(2)}, u32[]{:S(2)}) collective-permute-start(bf16[128,768]{1,0:T(8,128)(2,1)} %bitcast.68), channel_id=1, source_target_pairs={{0,2},{1,3},{2,0},{3,1},{4,6},{5,7},{6,4},{7,5},{8,10},{9,11},{10,... | collective-permute-start | bytes 589832 | tf_op jit(solution)/shard_map/ppermute | solution.py:23
  15.0 11.6 %collective-permute-start.1 = (bf16[2,128,768]{2,1,0:T(8,128)(2,1)S(1)}, bf16[2,128,768]{2,1,0:T(8,128)(2,1)S(1)}, u32[]{:S(2)}, u32[]{:S(2)}) collective-permute-start(bf16[2,128,768]{2,1,0:T(8,128)(2,1)S(1)} %maximum_select_fusion.7), channel_id=1, source_target_pairs={{0,2},{1,3},{2,0},{3,1},{4,6},{5,7},{6,4},{7,5},{8,10},{9,11},{10,... | collective-permute-start | bytes 1179656 | tf_op jit(solution)/shard_map/ppermute | solution.py:23
  20.5 7.8 %collective-permute-start.4 = (bf16[2,128,768]{2,1,0:T(8,128)(2,1)S(1)}, bf16[2,128,768]{2,1,0:T(8,128)(2,1)S(1)}, u32[]{:S(2)}, u32[]{:S(2)}) collective-permute-start(bf16[2,128,768]{2,1,0:T(8,128)(2,1)S(1)} %maximum_select_fusion.8), channel_id=1, source_target_pairs={{0,4},{4,0},{1,5},{5,1},{2,6},{6,2},{3,7},{7,3},{8,12},{12,8},{9,1... | collective-permute-start | bytes 1179656 | tf_op jit(solution)/shard_map/ppermute | solution.py:23
  27.7 5.6 %collective-permute-start.2 = (bf16[2,2,128,768]{3,2,0,1:T(8,128)(2,1)}, bf16[2,2,128,768]{3,2,0,1:T(8,128)(2,1)}, u32[]{:S(2)}, u32[]{:S(2)}) collective-permute-start(bf16[2,2,128,768]{3,2,0,1:T(8,128)(2,1)} %maximum_select_fusion.2), channel_id=1, source_target_pairs={{0,1},{1,0},{2,3},{3,2},{4,5},{5,4},{6,7},{7,6},{8,9},{9,8},{10,11... | collective-permute-start | bytes 2359304 | tf_op jit(solution)/shard_map/ppermute | solution.py:23
  28.4 10.7 %collective-permute-start.5 = (bf16[2,2,128,768]{3,2,1,0:T(8,128)(2,1)S(1)}, bf16[2,2,128,768]{3,2,1,0:T(8,128)(2,1)}, u32[]{:S(2)}, u32[]{:S(2)}) collective-permute-start(bf16[2,2,128,768]{3,2,1,0:T(8,128)(2,1)S(1)} %maximum_select_fusion.4), channel_id=1, source_target_pairs={{0,1},{1,0},{2,3},{3,2},{4,5},{5,4},{6,7},{7,6},{8,9},{9,8},{10,11... | collective-permute-start | bytes 2359304 | tf_op jit(solution)/shard_map/ppermute | solution.py:23
  34.9 37.8 %all-to-all-start = ((bf16[4,384,384]{2,1,0:T(8,128)(2,1)}), bf16[4,384,384]{2,1,0:T(8,128)(2,1)}, u32[]{:S(2)}, u32[]{:S(2)}) async-start(bf16[4,384,384]{2,1,0:T(8,128)(2,1)} %pack_feed.1), calls=%async_computation | async-start | bytes 2359296 | tf_op jit(solution)/shard_map/all_to_all | solution.py:53
  66.9 15.6 %collective-permute-start.9 = (bf16[192,384]{1,0:T(8,128)(2,1)}, bf16[192,384]{1,0:T(8,128)(2,1)S(1)}, u32[]{:S(2)}, u32[]{:S(2)}) collective-permute-start(bf16[192,384]{1,0:T(8,128)(2,1)} %get-tuple-element.66), channel_id=1, source_target_pairs={{0,8},{8,16},{16,24},{24,0},{1,9},{9,17},{17,25},{25,1},{2,10},{10... | collective-permute-start | bytes 442376 | tf_op jit(solution)/shard_map/ppermute | solution.py:49
  68.9 13.6 %collective-permute-start.10 = (bf16[192,384]{1,0:T(8,128)(2,1)}, bf16[192,384]{1,0:T(8,128)(2,1)S(1)}, u32[]{:S(2)}, u32[]{:S(2)}) collective-permute-start(bf16[192,384]{1,0:T(8,128)(2,1)} %get-tuple-element.67), channel_id=1, source_target_pairs={{0,16},{8,24},{16,0},{24,8},{1,17},{9,25},{17,1},{25,9},{2,18},{10... | collective-permute-start | bytes 442376 | tf_op jit(solution)/shard_map/ppermute | solution.py:49
  71.3 11.3 %collective-permute-start.11 = (bf16[192,384]{1,0:T(8,128)(2,1)}, bf16[192,384]{1,0:T(8,128)(2,1)S(1)}, u32[]{:S(2)}, u32[]{:S(2)}) collective-permute-start(bf16[192,384]{1,0:T(8,128)(2,1)} %get-tuple-element.68), channel_id=1, source_target_pairs={{0,24},{8,0},{16,8},{24,16},{1,25},{9,1},{17,9},{25,17},{2,26},{10... | collective-permute-start | bytes 442376 | tf_op jit(solution)/shard_map/ppermute | solution.py:49
  82.5 7.4 %collective-permute-start.12 = (bf16[2,512,768]{2,1,0:T(8,128)(2,1)}, bf16[2,512,768]{2,1,0:T(8,128)(2,1)S(1)}, u32[]{:S(2)}, u32[]{:S(2)}) collective-permute-start(bf16[2,512,768]{2,1,0:T(8,128)(2,1)} %get-tuple-element.70), channel_id=1, source_target_pairs={{0,1},{1,0},{2,3},{3,2},{4,5},{5,4},{6,7},{7,6},{8,9},{9,8},{10,11... | collective-permute-start | bytes 4718600 | tf_op jit(solution)/shard_map/ppermute | solution.py:23
  83.2 49.5 %all-to-all-start.1 = ((bf16[4,384,384]{2,1,0:T(8,128)(2,1)}), bf16[4,384,384]{2,1,0:T(8,128)(2,1)S(1)}, u32[]{:S(2)}, u32[]{:S(2)}) async-start(bf16[4,384,384]{2,1,0:T(8,128)(2,1)} %get-tuple-element.87), calls=%async_computation.1 | async-start | bytes 2359296 | tf_op jit(solution)/shard_map/all_to_all | solution.py:53
  94.4 19.3 %collective-permute-start.16 = (bf16[256,768]{1,0:T(8,128)(2,1)}, bf16[256,768]{1,0:T(8,128)(2,1)S(1)}, u32[]{:S(2)}, u32[]{:S(2)}) collective-permute-start(bf16[256,768]{1,0:T(8,128)(2,1)} %get-tuple-element.81), channel_id=1, source_target_pairs={{0,4},{4,0},{1,5},{5,1},{2,6},{6,2},{3,7},{7,3},{8,12},{12,8},{9,1... | collective-permute-start | bytes 1179656 | tf_op jit(solution)/shard_map/ppermute | solution.py:23
  96.1 19.7 %collective-permute-start.22 = (bf16[192,384]{1,0:T(8,128)(2,1)S(1)}, bf16[192,384]{1,0:T(8,128)(2,1)S(1)}, u32[]{:S(2)}, u32[]{:S(2)}) collective-permute-start(bf16[192,384]{1,0:T(8,128)(2,1)S(1)} %reduce-precision_convert_fusion.1), channel_id=1, source_target_pairs={{0,4},{4,0},{1,5},{5,1},{2,6},{6,2},{3,7},{7,3},{8,12},{12,8},{9,1... | collective-permute-start | bytes 442376 | tf_op jit(solution)/shard_map/ppermute | solution.py:23
  97.6 18.3 %collective-permute-start.14 = (bf16[256,768]{1,0:T(8,128)(2,1)}, bf16[256,768]{1,0:T(8,128)(2,1)S(1)}, u32[]{:S(2)}, u32[]{:S(2)}) collective-permute-start(bf16[256,768]{1,0:T(8,128)(2,1)} %get-tuple-element.77), channel_id=1, source_target_pairs={{0,2},{1,3},{2,0},{3,1},{4,6},{5,7},{6,4},{7,5},{8,10},{9,11},{10,... | collective-permute-start | bytes 1179656 | tf_op jit(solution)/shard_map/ppermute | solution.py:23
  99.2 10.3 %collective-permute-start.17 = (f32[13,768]{1,0:T(8,128)S(1)}, f32[13,768]{1,0:T(8,128)S(1)}, u32[]{:S(2)}, u32[]{:S(2)}) collective-permute-start(f32[13,768]{1,0:T(8,128)S(1)} %add.104), channel_id=1, source_target_pairs={{0,2},{1,3},{2,0},{3,1},{4,6},{5,7},{6,4},{7,5},{8,10},{9,11},{10,... | collective-permute-start | bytes 119816 | tf_op jit(solution)/shard_map/ppermute | solution.py:23
  113.7 5.4 %collective-permute-start.20 = (f32[13,768]{1,0:T(8,128)S(1)}, f32[13,768]{1,0:T(8,128)S(1)}, u32[]{:S(2)}, u32[]{:S(2)}) collective-permute-start(f32[13,768]{1,0:T(8,128)S(1)} %add.107), channel_id=1, source_target_pairs={{0,8},{8,0},{16,24},{24,16},{1,9},{9,1},{17,25},{25,17},{2,10},{10... | collective-permute-start | bytes 119816 | tf_op jit(solution)/shard_map/ppermute | solution.py:23
  118.6 8.8 %collective-permute-start.15 = (bf16[128,768]{1,0:T(8,128)(2,1)}, bf16[128,768]{1,0:T(8,128)(2,1)S(1)}, u32[]{:S(2)}, u32[]{:S(2)}) collective-permute-start(bf16[128,768]{1,0:T(8,128)(2,1)} %get-tuple-element.79), channel_id=1, source_target_pairs={{0,4},{4,0},{1,5},{5,1},{2,6},{6,2},{3,7},{7,3},{8,12},{12,8},{9,1... | collective-permute-start | bytes 589832 | tf_op jit(solution)/shard_map/ppermute | solution.py:23
  119.1 8.2 %collective-permute-start.21 = (f32[13,768]{1,0:T(8,128)S(1)}, f32[13,768]{1,0:T(8,128)S(1)}, u32[]{:S(2)}, u32[]{:S(2)}) collective-permute-start(f32[13,768]{1,0:T(8,128)S(1)} %add.109), channel_id=1, source_target_pairs={{0,16},{8,24},{16,0},{24,8},{1,17},{9,25},{17,1},{25,9},{2,18},{10... | collective-permute-start | bytes 119816 | tf_op jit(solution)/shard_map/ppermute | solution.py:23
  125.8 5.9 %collective-permute-start.19 = (bf16[128,768]{1,0:T(8,128)(2,1)}, bf16[128,768]{1,0:T(8,128)(2,1)S(1)}, u32[]{:S(2)}, u32[]{:S(2)}) collective-permute-start(bf16[128,768]{1,0:T(8,128)(2,1)} %get-tuple-element.85), channel_id=1, source_target_pairs={{0,2},{1,3},{2,0},{3,1},{4,6},{5,7},{6,4},{7,5},{8,10},{9,11},{10,... | collective-permute-start | bytes 589832 | tf_op jit(solution)/shard_map/ppermute | solution.py:23
  133.0 6.8 %collective-permute-start.23 = (bf16[384,384]{1,0:T(8,128)(2,1)S(1)}, bf16[384,384]{1,0:T(8,128)(2,1)S(1)}, u32[]{:S(2)}, u32[]{:S(2)}) collective-permute-start(bf16[384,384]{1,0:T(8,128)(2,1)S(1)} %reduce-precision_convert_fusion), channel_id=1, source_target_pairs={{0,4},{4,0},{1,5},{5,1},{2,6},{6,2},{3,7},{7,3},{8,12},{12,8},{9,1... | collective-permute-start | bytes 884744 | tf_op jit(solution)/shard_map/ppermute | solution.py:23
  (18 other events, 104.4 us)

commit v4 on v3

--- a/solution.py
+++ b/solution.py
@@ -103,10 +103,10 @@
 
 
 def split_kernel(
-    bits_ref, kept_ref, got_ref, mixed_kept_ref, mixed_away_ref, grad_kept_ref, grad_away_ref
+    high_ref, ctx_ref, kept_ref, got_ref, mixed_kept_ref, mixed_away_ref, grad_kept_ref, grad_away_ref
 ):
     size = kept_ref.shape[1] // 4
-    high, ctx = bits_ref[0], bits_ref[1]
+    high, ctx = high_ref[0], ctx_ref[0]
 
     def total(which, c, h):
         rows = rows_at(c * 2 + h, size)
@@ -132,21 +132,21 @@
     away_out_ref[...] = total(1 - bit_ref[0]).astype(bf16)
 
 
-def attention_kernel(shares, place_ref, *refs):
+def attention_kernel(shares, ctx_ref, dp_ref, *refs):
     piece_refs, refs = refs[:shares], refs[shares:]
-    normed_ref, cot_ref, cos_ref, sin_ref, seg_row_ref, seg_col_ref = refs[:6]
-    refs = refs[6:]
+    normed_ref, cot_ref, cos_ref, sin_ref, seg_row_ref = refs[:5]
+    refs = refs[5:]
     vectors_ref, mixed_ref, grad_normed_ref, sums_ref, bias_grad_ref = refs[:5]
     part_refs, refs = refs[5 : 5 + shares], refs[5 + shares :]
     (
         weights_ref, small_ref, first_ref, qkv_ref, grad_ref, feature_ref, grad_weights_ref,
-        dq_ref, dk_ref, dv_ref,
+        dq_ref, dk_ref, dv_ref, seg_col_ref,
     ) = refs
     tokens, model = normed_ref.shape
     share = piece_refs[0].shape[0] - 8
     width = grad_ref.shape[0]
     scale = HD**-0.5
-    ctx, dp = place_ref[0], place_ref[1]
+    ctx, dp = ctx_ref[0], dp_ref[0]
     for d, ref in enumerate(piece_refs):
         source = lax.rem(dp + (shares - d), shares)
         weights_ref[rows_at(source, share), :] = ref[:share, :]
@@ -164,6 +164,7 @@
         first_ref[rows, :] = first
         qkv_ref[:, rows] = (dot(first, project, ((1,), (0,))) + bias).T
         grad_ref[:, rows] = dot(cot_ref[rows, :], output, ((1,), (0,))).astype(bf16).T
+    seg_col_ref[...] = jnp.broadcast_to(seg_row_ref[...], (8, tokens)).T
     cosine = cos_ref[...]
     sine = sin_ref[...]
     ones = jnp.ones((8, tokens), bf16)
@@ -202,7 +203,7 @@
             scores = dot(key_rows[low:end], query, ((1,), (0,)))
             key_at = lax.broadcasted_iota(jnp.int32, scores.shape, 0) + low
             query_at = lax.broadcasted_iota(jnp.int32, scores.shape, 1) + begin
-            allowed = (seg_col_ref[low:end, :] == seg_row_ref[:, begin:end]) & (
+            allowed = (seg_col_ref[low:end, 0:1] == seg_row_ref[:, begin:end]) & (
                 key_at <= query_at
             )
             scores = jnp.where(allowed, scores, masked_score)
@@ -264,8 +265,8 @@
 
 
 def feed_kernel(
-    ctx_ref, all_ref, normed_ref, cot_ref, vectors_ref, mixed_in_ref, grad_in_ref,
-    kept_ref, away_ref, grad_weights_ref, sums_ref, bias_grad_ref,
+    ctx_ref, low_ref, all_ref, normed_ref, cot_ref, vectors_ref, mixed_in_ref, grad_in_ref,
+    sums_in_ref, bias_in_ref, kept_ref, away_ref, grad_weights_ref, sums_ref,
     up_ref, down_ref, second_ref, act_ref, pre_ref,
 ):
     tokens, model = normed_ref.shape
@@ -278,7 +279,7 @@
         ctx_ref[0] > 0, vectors_ref[6:7, units : 2 * units], vectors_ref[6:7, :units]
     )
     up, down = up_ref[...], down_ref[...]
-    low = ctx_ref[1] > 0
+    low = low_ref[0] > 0
 
     def divide(which, start, block):
         first, last = block[: ROWS // 2], block[ROWS // 2 :]
@@ -289,6 +290,7 @@
     total_one = jnp.zeros((1, model), f32)
     total_two = jnp.zeros((1, model), f32)
     total_bias = jnp.zeros((1, units), f32)
+    total_cot = jnp.zeros((1, model), f32)
     for i in range(0, tokens, ROWS):
         rows = slice(i, i + ROWS)
         second = (normed_ref[rows, :] * gain + shift).astype(bf16)
@@ -299,6 +301,7 @@
         act_ref[:, rows] = act.T
         grad_pre = dot(cot_ref[rows, :], down, ((1,), (0,))) * slope
         total_bias += jnp.sum(grad_pre, axis=0, keepdims=True)
+        total_cot += jnp.sum(cot_ref[rows, :].astype(f32), axis=0, keepdims=True)
         pre = grad_pre.astype(bf16)
         pre_ref[:, rows] = pre.T
         mixed = dot(act, down, ((1,), (1,))) + mixed_in_ref[rows, :].astype(f32)
@@ -308,29 +311,57 @@
         total_two += jnp.sum(grad_second, axis=0, keepdims=True)
         grad_normed = grad_second * gain + grad_in_ref[rows, :].astype(f32)
         divide(1, i, grad_normed.astype(bf16))
-    sums_ref[0:1, :] = total_one
-    sums_ref[1:2, :] = total_two
-    bias_grad_ref[...] = total_bias
+    total_cot = 0.125 * total_cot
     up_part = dot(pre_ref[...], second_ref[...], ((1,), (0,))).astype(bf16).T
     down_part = dot(act_ref[...], cot_ref[...], ((1,), (0,))).astype(bf16).T
     for s in range(shares):
-        grad_weights_ref[s, :share, :] = up_part[s * share : (s + 1) * share]
-        grad_weights_ref[s, share:, :] = down_part[s * share : (s + 1) * share]
-
-
-def call(kernel, out_shape, scratch, flops, name, *args):
+        lanes = slice(s * share, (s + 1) * share)
+        grad_weights_ref[s, :share, :] = up_part[lanes]
+        grad_weights_ref[s, share : 2 * share, :] = down_part[lanes]
+    sums_ref[0:2, :] = sums_in_ref[...]
+    sums_ref[2:3, :] = total_one
+    sums_ref[3:4, :] = total_two
+    sums_ref[4:5, :] = total_cot
+    sums_ref[5:6, :units] = total_bias
+    if shares == 1:
+        return
+    bias = bias_in_ref[...]
+    part = HD // shares
+    heads = 3 * (model // HD) // 4
+    for s in range(shares):
+        lanes = slice(s * share, (s + 1) * share)
+        slices = [bias[i : i + 1, s * part : (s + 1) * part] for i in range(heads)]
+        slices.append(jnp.zeros((1, share - heads * part), f32))
+        one, two = sums_in_ref[0:1, lanes], sums_in_ref[1:2, lanes]
+        values = jnp.concatenate(
+            [
+                jnp.concatenate([one, two], axis=1),
+                jnp.concatenate([total_one[:, lanes], total_two[:, lanes]], axis=1),
+                jnp.concatenate([total_cot[:, lanes]] + slices, axis=1),
+                total_bias,
+            ],
+            axis=0,
+        )
+        high = values.astype(bf16)
+        rest = (values - high.astype(f32)).astype(bf16)
+        grad_weights_ref[s, 2 * share :, :] = jnp.concatenate(
+            [high.astype(f32), rest.astype(f32)], axis=0
+        ).astype(bf16)
+
+
+def call(kernel, out_shape, scratch, flops, name, scalars, *args):
     whole = pl.BlockSpec(memory_space=pltpu.VMEM)
     scalar = pl.BlockSpec(memory_space=pltpu.SMEM)
     moved = sum(a.size * a.dtype.itemsize for a in args)
     return pl.pallas_call(
         kernel,
         out_shape=[jax.ShapeDtypeStruct(shape, dtype) for shape, dtype in out_shape],
-        in_specs=[scalar] + [whole] * (len(args) - 1),
+        in_specs=[scalar] * len(scalars) + [whole] * len(args),
         out_specs=[whole] * len(out_shape),
         scratch_shapes=[pltpu.VMEM(shape, dtype) for shape, dtype in scratch],
         cost_estimate=pl.CostEstimate(flops=flops, transcendentals=0, bytes_accessed=moved),
         name=name,
-    )(*args)
+    )(*[jnp.asarray(s, jnp.int32).reshape(1) for s in scalars], *args)
 
 
 def body(
@@ -352,20 +383,17 @@
     bias_share = HD // n_dp
     tensor_index = lax.axis_index("tensor")
 
-    def scalars(*values):
-        return jnp.stack([jnp.asarray(v, jnp.int32) for v in values])
-
     (packed,) = call(
         pack_kernel, [((share + 8, columns), bf16)], [], 0, "pack_attention",
-        scalars(dp_index), project_weight.transpose(1, 0, 2), output_weight, project_bias,
+        [dp_index], project_weight.transpose(1, 0, 2), output_weight, project_bias,
         attend_gain, attend_shift, feed_gain, feed_shift, output_bias, downward_bias,
-        upward_bias[0],
+        upward_bias,
     )
     (feed_block,) = call(
         pack_feed_kernel, [((n_dp, 2 * share, half_units), bf16)], [], 0, "pack_feed",
-        scalars(ctx_index), upward_weight, downward_weight.T,
-    )
-    few = n_dp <= 4
+        [ctx_index], upward_weight, downward_weight.T,
+    )
+    few = n_dp == 4
     if few:
         pieces = [packed] + [shifted(packed, d) for d in range(1, n_dp)]
     else:
@@ -400,7 +428,6 @@
 
     frequency = 10000.0 ** (-2.0 * jnp.arange(HALF, dtype=f32) / ROT)
     angles = frequency[:, None] * jnp.arange(tokens, dtype=f32)[None, :]
-    segments = segment_ids[0]
     vectors, mixed, grad_normed, attention_sums, project_bias_grad, *attention_parts = call(
         functools.partial(attention_kernel, shares),
         [
@@ -413,11 +440,12 @@
             ((3 * width, tokens), f32), ((width, tokens), bf16), ((columns, tokens), bf16),
             ((model, 2 * width), bf16),
             ((HD, tokens), f32), ((HD, tokens), f32), ((HD, tokens), f32),
+            ((tokens, 8), jnp.int32),
         ],
         tokens * model * columns * 8,
         "attention_part",
-        scalars(ctx_index, dp_index if few else 0), *pieces, normed, grad_all,
-        jnp.cos(angles), jnp.sin(angles), segments[None, :], segments[:, None],
+        [ctx_index, dp_index if few else 0], *pieces, normed, grad_all,
+        jnp.cos(angles), jnp.sin(angles), segment_ids,
     )
     if few:
         attention_parts = attention_parts[:1] + [
@@ -427,11 +455,12 @@
         exchanged = exchange_dp(attention_parts[0].reshape(n_dp, share, 2 * width))
         attention_parts = [exchanged[i] for i in range(n_dp)]
 
-    kept, away, grad_feed, feed_sums, upward_bias_grad = call(
+    kept, away, grad_feed, sums = call(
         feed_kernel,
         [
             ((2, tokens // 2, model), bf16), ((2, tokens // 2, model), bf16),
-            (feed_all.shape, bf16), ((2, model), f32), ((1, half_units), f32),
+            ((shares, feed_all.shape[1] + (8 if few else 0), half_units), bf16),
+            ((8, model), f32),
         ],
         [
             ((model, half_units), bf16), ((model, half_units), bf16), ((tokens, model), bf16),
@@ -439,76 +468,71 @@
         ],
         tokens * model * half_units * 12,
         "feed_part",
-        scalars(ctx_index, tensor_index % 2),
-        feed_all, normed, grad_all, vectors, mixed, grad_normed,
-    )
-    kept, away, grad_feed, feed_sums, upward_bias_grad, attention_parts = (
-        lax.optimization_barrier(
-            (kept, away, grad_feed, feed_sums, upward_bias_grad, attention_parts)
-        )
+        [ctx_index, tensor_index % 2],
+        feed_all, normed, grad_all, vectors, mixed, grad_normed, attention_sums,
+        project_bias_grad,
+    )
+    kept, away, grad_feed, attention_parts = lax.optimization_barrier(
+        (kept, away, grad_feed, attention_parts)
     )
     if not few:
         grad_feed = grad_feed.reshape(2, n_dp, share, half_units).transpose(1, 0, 2, 3)
         grad_feed = grad_feed.reshape(n_dp, 2 * share, half_units)
     feed_parts = exchange_dp(grad_feed)
 
-    project_row = 0.5 * project_bias_grad[: 3 * heads].reshape(1, 3 * width)
-    project_row = jnp.pad(project_row, ((0, 0), (0, model - 3 * width)))
-    unit_row = jnp.where(
-        second,
-        jnp.pad(upward_bias_grad, ((0, 0), (half_units, 0))),
-        jnp.pad(upward_bias_grad, ((0, 0), (0, half_units))),
-    )
-    slot = lax.broadcasted_iota(jnp.int32, (n_tensor, 1), 0) == tensor_index
-    sums = jnp.concatenate(
-        [
-            attention_sums,
-            feed_sums,
-            jnp.sum(grad_rows.astype(f32), axis=0, keepdims=True),
-            jnp.where(slot, project_row, 0.0),
-            jnp.where(slot, unit_row, 0.0),
-        ],
-        axis=0,
-    )
-    def added(values, axis, bit):
-        return values + flipped(values, axis, bit)
-
     high_bit = tensor_index // 2
     quarter = ((tokens // 4, model), bf16)
-    away, sums = lax.optimization_barrier(
-        (flipped(away, "tensor", 1), added(sums, "tensor", 1))
-    )
     mixed_kept, mixed_away, grad_kept, grad_away = call(
         split_kernel, [quarter] * 4, [], 0, "split",
-        scalars(high_bit, ctx_index), kept, away,
-    )
-    sums = added(added(sums, "tensor", 2), "ctx", 1)
-    grad_away, sums = lax.optimization_barrier((flipped(grad_away, "ctx", 1), sums))
+        [high_bit, ctx_index], kept, flipped(away, "tensor", 1),
+    )
+    grad_away = flipped(grad_away, "ctx", 1)
     eighths = [((tokens // 8, model), f32), ((tokens // 8, model), bf16)]
     grad_normed, grad_away = call(
-        halve_kernel, eighths, [], 0, "halve_grad", scalars(high_bit), grad_kept, grad_away
+        halve_kernel, eighths, [], 0, "halve_grad", [high_bit], grad_kept, grad_away
     )
     mixed, mixed_away = call(
         halve_kernel, eighths, [], 0, "halve_mixed",
-        scalars(ctx_index), mixed_kept, flipped(mixed_away, "tensor", 2),
-    )
-    bit = 1
-    while bit < n_dp:
-        sums = added(sums, "dp", bit)
-        bit *= 2
+        [ctx_index], mixed_kept, flipped(mixed_away, "tensor", 2),
+    )
     mixed = mixed + flipped(mixed_away, "ctx", 1).astype(f32)
     grad_normed = grad_normed + flipped(grad_away, "tensor", 2).astype(f32)
-    mixed, grad_normed, sums, feed_parts = lax.optimization_barrier(
-        (mixed, grad_normed, sums, feed_parts)
-    )
-    shared = lax.dynamic_slice_in_dim(sums[:5], dp_index * share, share, 1)
-    project_sum = lax.dynamic_index_in_dim(sums, 5 + tensor_index, 0, keepdims=False)
-    project_bias_grad = lax.dynamic_slice_in_dim(
-        project_sum[: 3 * width].reshape(3, heads, HD), dp_index * bias_share, bias_share, 2
-    )
-    upward_bias_grad = lax.dynamic_slice(
-        sums, (5 + n_tensor + tensor_index, dp_index * (units // n_dp)), (1, units // n_dp)
-    )
+    mixed, grad_normed, feed_parts = lax.optimization_barrier((mixed, grad_normed, feed_parts))
+    feed_sum = jnp.sum(feed_parts.astype(f32), axis=0)
+
+    if few:
+        small = feed_sum[2 * share : 2 * share + 4] + feed_sum[2 * share + 4 :]
+    else:
+        bias_rows = project_bias_grad[: 3 * heads].reshape(3 * heads, n_dp, bias_share)
+        bias_rows = bias_rows.transpose(1, 0, 2).reshape(n_dp, 3 * heads * bias_share)
+        small = jnp.concatenate([sums[:5], sums[5:6]], axis=0)
+        bit = 1
+        while bit < n_dp:
+            small = small + flipped(small, "dp", bit)
+            bias_rows = bias_rows + flipped(bias_rows, "dp", bit)
+            bit *= 2
+        units_row = small[5:6, :half_units]
+        small = lax.dynamic_slice_in_dim(small[:5], dp_index * share, share, 1)
+        bias_row = lax.dynamic_index_in_dim(bias_rows, dp_index, 0, keepdims=False)
+    if few:
+        units_row = small[3:4]
+        bias_row = small[2, share : share + 3 * heads * bias_share]
+        small = small[:3]
+    small = small + flipped(small, "tensor", 1)
+    small = small + flipped(small, "tensor", 2)
+    small = small + flipped(small, "ctx", 1)
+    if few:
+        shared = [
+            small[0, :share], small[0, share:], small[1, :share], small[1, share:],
+            small[2, :share],
+        ]
+    else:
+        shared = [small[i] for i in range(5)]
+    units_row = joined(units_row, flipped(units_row, "ctx", 1), second)
+    upward_bias_grad = lax.dynamic_slice_in_dim(
+        units_row, dp_index * (units // n_dp), units // n_dp, 1
+    )
+    project_bias_grad = bias_row.reshape(3, heads, bias_share)
 
     own_source = hidden_rows.astype(f32)
     hidden_out = own_source + mixed
@@ -528,7 +552,7 @@
     attention_own = lax.reduce_precision(attention_sum, 8, 7).astype(bf16)
     attention_both = joined(attention_own, flipped(attention_own, "ctx", 1), second).astype(f32)
 
-    feed_sum = jnp.sum(feed_parts.astype(f32), axis=0)
+    feed_sum = feed_sum[: 2 * share]
     feed_own = lax.reduce_precision(feed_sum, 8, 7).astype(bf16)
     feed_both = joined(feed_own, flipped(feed_own, "ctx", 1), second).astype(f32)
 

time: 142 us -> 129 us (0.908)
  waiting for transfers between devices: 29.6 us -> 23.4 us
  other arithmetic: 16.4 us -> 13.1 us
  local copies, waits for them, and re-layouts: 11.8 us -> 8.52 us
    ppermute x18 -> x17, waiting for transfers between devices: 29.6 us -> 23.4 us  [flipped(): lax.ppermute(block, axis, [(i, i ^ bit) for i in range(lax.axis_size(axis...]
    ppermute x18 -> x17, starting transfers between devices: 18.9 us -> 14.1 us  [flipped(): lax.ppermute(block, axis, [(i, i ^ bit) for i in range(lax.axis_size(axis...]
    ppermute x6, starting transfers between devices: 11.4 us -> 16.1 us  [shifted(): lax.ppermute(block, 'dp', [(i, (i + distance) % count) for i in range(cou...]
    another operation x3 -> x0, other arithmetic: 1.75 us -> none  [scalars(): return jnp.stack([jnp.asarray(v, jnp.int32) for v in values])]
    unnamed x35 -> x19, local copies, waits for them, and re-layouts: 4.46 us -> 4.24 us
  transfers between devices with their start and end apart: 26 -> 25, of which waited for: 8 -> 8; matrix products, arithmetic and copies ran while one was open for 17% -> 14% of each run, Pallas kernels for 30% -> 33%
where the time goes in v4:
time: 129 us; the launch traced here: 128 us
  Pallas kernels  42.8 us (33%)
  starting transfers between devices  39.4 us (31%)
  waiting for transfers between devices  23.4 us (18%)
  other arithmetic  13.1 us (10%)
  local copies, waits for them, and re-layouts  8.52 us (7%)
    pallas_call x7, Pallas kernels, call(): pl.pallas_call(kernel, out_shape=[jax.ShapeDtypeStruct(shape, dtype) for...  42.8 us
    ppermute x17, waiting for transfers between devices, flipped(): lax.ppermute(block, axis, [(i, i ^ bit) for i in range(lax.axis_size(axis...  23.4 us
    ppermute x6, starting transfers between devices, shifted(): lax.ppermute(block, 'dp', [(i, (i + distance) % count) for i in range(cou...  16.1 us
    ppermute x17, starting transfers between devices, flipped(): lax.ppermute(block, axis, [(i, i ^ bit) for i in range(lax.axis_size(axis...  14.1 us
    all_to_all x2, starting transfers between devices, exchange_dp(): return lax.all_to_all(blocks, 'dp', 0, 0)  9.31 us
    unnamed x19, local copies, waits for them, and re-layouts  4.24 us
    select_n x10, other arithmetic, ordered(): jnp.where(second, jnp.stack([other, own], axis=dim), jnp.stack([own, othe...  3.64 us
  transfers between devices with their start and end apart: 25, of which 8 were waited for; matrix products, arithmetic and copies ran while one was open for 14% of the time, Pallas kernels for 33%

profile of v4, /device:TPU:0, one launch (start us, length us, event | category | flops | bytes accessed | tf_op | source)
XLA Modules:
  0.0 128.4 jit_solution(18137175792066330652)
XLA Ops:
  0.7 3.0 %collective-permute-start = (bf16[128,768]{1,0:T(8,128)(2,1)}, bf16[128,768]{1,0:T(8,128)(2,1)S(1)}, u32[]{:S(2)}, u32[]{:S(2)}) collective-permute-start(bf16[128,768]{1,0:T(8,128)(2,1)} %bitcast.64), channel_id=1, source_target_pairs={{0,4},{4,0},{1,5},{5,1},{2,6},{6,2},{3,7},{7,3},{8,12},{12,8},{9,1... | collective-permute-start | bytes 589832 | tf_op jit(solution)/shard_map/ppermute | solution.py:23
  3.7 1.5 %collective-permute-start.3 = (bf16[128,768]{1,0:T(8,128)(2,1)}, bf16[128,768]{1,0:T(8,128)(2,1)S(1)}, u32[]{:S(2)}, u32[]{:S(2)}) collective-permute-start(bf16[128,768]{1,0:T(8,128)(2,1)} %bitcast.67), channel_id=1, source_target_pairs={{0,2},{1,3},{2,0},{3,1},{4,6},{5,7},{6,4},{7,5},{8,10},{9,11},{10,... | collective-permute-start | bytes 589832 | tf_op jit(solution)/shard_map/ppermute | solution.py:23
  5.2 2.0 %pack_attention.1.refs_0_ = bf16[200,768]{1,0:T(8,128)(2,1)} custom-call(s32[1]{0:T(128)} %bitcast.24.dp_ref, bf16[3,192,192]{2,1,0:T(8,128)(2,1)} %bitcast.84, bf16[192,192]{1,0:T(8,128)(2,1)} %output_ref.1, bf16[3,3,16]{2,1,0:T(4,128)(2,1)} %bias_ref.1, bf16[192]{0:T(256)(128)(2,1)} %refs_0_.1, bf16[192]{0:T(256)(128)(2,1)} %refs_1_.1, ...), custom_call_target="tpu_custom_call" | custom-call | bytes 297888 | tf_op jit(solution)/shard_map/pack_attention/pallas_call | solution.py:356
  7.2 1.6 %collective-permute-start.6 = (bf16[200,768]{1,0:T(8,128)(2,1)}, bf16[200,768]{1,0:T(8,128)(2,1)}, u32[]{:S(2)}, u32[]{:S(2)}) collective-permute-start(bf16[200,768]{1,0:T(8,128)(2,1)} %pack_attention.1.refs_0_), channel_id=1, source_target_pairs={{0,8},{8,16},{16,24},{24,0},{1,9},{9,17},{17,25},{25,1},{2,10},{10... | collective-permute-start | bytes 921608 | tf_op jit(solution)/shard_map/ppermute | solution.py:49
  8.8 2.6 %collective-permute-start.7 = (bf16[200,768]{1,0:T(8,128)(2,1)}, bf16[200,768]{1,0:T(8,128)(2,1)}, u32[]{:S(2)}, u32[]{:S(2)}) collective-permute-start(bf16[200,768]{1,0:T(8,128)(2,1)} %pack_attention.1.refs_0_), channel_id=1, source_target_pairs={{0,16},{8,24},{16,0},{24,8},{1,17},{9,25},{17,1},{25,9},{2,18},{10... | collective-permute-start | bytes 921608 | tf_op jit(solution)/shard_map/ppermute | solution.py:49
  15.1 2.3 %pack_feed.1 = bf16[4,384,384]{2,1,0:T(8,128)(2,1)} custom-call(s32[1]{0:T(128)} %bitcast.1.ctx_ref.bit_ref, bf16[192,768]{1,0:T(8,128)(2,1)} %up_ref.1, bf16[192,768]{1,0:T(8,128)(2,1)} %bitcast.85), custom_call_target="tpu_custom_call" | custom-call | bytes 589824 | tf_op jit(solution)/shard_map/pack_feed/pallas_call | solution.py:356
  17.5 5.9 %collective-permute-done.1 = bf16[2,128,768]{2,1,0:T(8,128)(2,1)S(1)} collective-permute-done((bf16[2,128,768]{2,1,0:T(8,128)(2,1)S(1)}, bf16[2,128,768]{2,1,0:T(8,128)(2,1)S(1)}, u32[]{:S(2)}, u32[]{:S(2)}) %collective-permute-start.1) | collective-permute-done | bytes 393248 | tf_op jit(solution)/shard_map/ppermute | solution.py:23
  26.3 4.3 %all-to-all-start = ((bf16[4,384,384]{2,1,0:T(8,128)(2,1)}), bf16[4,384,384]{2,1,0:T(8,128)(2,1)}, u32[]{:S(2)}, u32[]{:S(2)}) async-start(bf16[4,384,384]{2,1,0:T(8,128)(2,1)} %pack_feed.1), calls=%async_computation | async-start | bytes 2359296 | tf_op jit(solution)/shard_map/all_to_all | solution.py:53
  30.6 1.6 %maximum_select_fusion.1 = bf16[2,2,2,128,768]{4,3,1,2,0:T(8,128)(2,1)S(1)} fusion(bf16[2,2,1,128,768]{4,3,1,2,0:T(8,128)(2,1)S(1)} %maximum_select_fusion.5, bf16[2,2,1,128,768]{4,3,1,2,0:T(8,128)(2,1)} %bitcast.20, pred[]{:T(512)S(6)} %gt.15), kind=kLoop, calls=%fused_computation.7 | loop fusion | flops 2359296 | bytes 3145729 | tf_op jit(solution)/shard_map/jit(_where)/select_n | solution.py:27
  34.4 2.1 %fusion.refs_4_.normed_ref = f32[1024,768]{1,0:T(8,128)} fusion(bf16[1024,768]{1,0:T(8,128)(2,1)S(1)} %bitcast.63, f32[1024]{0:T(1024)S(1)} %add_rsqrt_fusion, f32[1024]{0:T(1024)S(1)} %broadcast_multiply_fusion), kind=kLoop, calls=%fused_computation.2 | loop fusion | flops 2359296 | bytes 4726784 | tf_op jit(solution)/shard_map/mul | solution.py:427
  36.5 21.6 %attention_part.1 = (f32[8,768]{1,0:T(8,128)}, bf16[1024,768]{1,0:T(8,128)(2,1)}, bf16[1024,768]{1,0:T(8,128)(2,1)}, f32[2,768]{1,0:T(2,128)}, f32[16,64]{1,0:T(...) custom-call(s32[1]{0:T(128)} %bitcast.1.ctx_ref.bit_ref, ...), custom_call_target="tpu_custom_call" | custom-call | flops 4831838208 | bytes 6017024 | tf_op jit(solution)/shard_map/attention_part/pallas_call | solution.py:356
  58.1 8.1 %collective-permute-start.9 = (bf16[192,384]{1,0:T(8,128)(2,1)}, bf16[192,384]{1,0:T(8,128)(2,1)}, u32[]{:S(2)}, u32[]{:S(2)}) collective-permute-start(bf16[192,384]{1,0:T(8,128)(2,1)} %get-tuple-element.57), channel_id=1, source_target_pairs={{0,8},{8,16},{16,24},{24,0},{1,9},{9,17},{17,25},{25,1},{2,10},{10... | collective-permute-start | bytes 442376 | tf_op jit(solution)/shard_map/ppermute | solution.py:49
  66.2 2.4 %collective-permute-start.11 = (bf16[192,384]{1,0:T(8,128)(2,1)}, bf16[192,384]{1,0:T(8,128)(2,1)S(1)}, u32[]{:S(2)}, u32[]{:S(2)}) collective-permute-start(bf16[192,384]{1,0:T(8,128)(2,1)} %get-tuple-element.59), channel_id=1, source_target_pairs={{0,24},{8,0},{16,8},{24,16},{1,25},{9,1},{17,9},{25,17},{2,26},{10... | collective-permute-start | bytes 442376 | tf_op jit(solution)/shard_map/ppermute | solution.py:49
  68.7 9.8 %feed_part.1 = (bf16[2,512,768]{2,1,0:T(8,128)(2,1)}, bf16[2,512,768]{2,1,0:T(8,128)(2,1)}, bf16[4,392,384]{2,1,0:T(8,128)(2,1)}, f32[8,768]{1,0:T(8,128)}) custom-call(s32[1]{0:T(128)} %bitcast.1.ctx_ref.bit_ref, s32[1]{0:T(128)} %bitcast.3.low_ref, bf16[4,384,384]{2,1,0:T(8,128)(2,1)} %all-to-all-done.all_ref, f32[1024,768]{1,0:T(8,128)} %fusion.refs_4_.normed_ref, ...), custom_call_target="tpu_custom_call" | custom-call | flops 3623878656 | bytes 9078784 | tf_op jit(solution)/shard_map/feed_part/pallas_call | solution.py:356
  79.2 5.0 %all-to-all-start.1 = ((bf16[4,392,384]{2,1,0:T(8,128)(2,1)}), bf16[4,392,384]{2,1,0:T(8,128)(2,1)S(1)}, u32[]{:S(2)}, u32[]{:S(2)}) async-start(bf16[4,392,384]{2,1,0:T(8,128)(2,1)} %get-tuple-element.70), calls=%async_computation.1 | async-start | bytes 2408448 | tf_op jit(solution)/shard_map/all_to_all | solution.py:53
  87.4 3.3 %split.1 = (bf16[256,768]{1,0:T(8,128)(2,1)}, bf16[256,768]{1,0:T(8,128)(2,1)}, bf16[256,768]{1,0:T(8,128)(2,1)}, bf16[256,768]{1,0:T(8,128)(2,1)}) custom-call(s32[1]{0:T(128)} %bitcast.2.high_ref.bit_ref, s32[1]{0:T(128)} %bitcast.1.ctx_ref.bit_ref, bf16[2,512,768]{2,1,0:T(8,128)(2,1)} %get-tuple-element.60.kept_ref, bf16[2,512,768]{2,1,0:T(8,128)(2,1)} %copy-done.2), custom_call_target="tpu_custom_call" | custom-call | bytes 3145728 | tf_op jit(solution)/shard_map/split/pallas_call | solution.py:356
  91.3 1.5 %collective-permute-start.15 = (bf16[256,768]{1,0:T(8,128)(2,1)}, bf16[256,768]{1,0:T(8,128)(2,1)}, u32[]{:S(2)}, u32[]{:S(2)}) collective-permute-start(bf16[256,768]{1,0:T(8,128)(2,1)} %get-tuple-element.67), channel_id=1, source_target_pairs={{0,4},{4,0},{1,5},{5,1},{2,6},{6,2},{3,7},{7,3},{8,12},{12,8},{9,1... | collective-permute-start | bytes 1179656 | tf_op jit(solution)/shard_map/ppermute | solution.py:23
  95.0 6.4 %collective-permute-done.13.got_ref = bf16[256,768]{1,0:T(8,128)(2,1)} collective-permute-done((bf16[256,768]{1,0:T(8,128)(2,1)}, bf16[256,768]{1,0:T(8,128)(2,1)}, u32[]{:S(2)}, u32[]{:S(2)}) %collective-permute-start.13) | collective-permute-done | bytes 393248 | tf_op jit(solution)/shard_map/ppermute | solution.py:23
  101.4 2.0 %halve_mixed.1 = (f32[128,768]{1,0:T(8,128)}, bf16[128,768]{1,0:T(8,128)(2,1)}) custom-call(s32[1]{0:T(128)} %bitcast.1.ctx_ref.bit_ref, bf16[256,768]{1,0:T(8,128)(2,1)} %get-tuple-element.62.kept_ref, bf16[256,768]{1,0:T(8,128)(2,1)} %collective-permute-done.13.got_ref), custom_call_target="tpu_custom_call" | custom-call | bytes 786432 | tf_op jit(solution)/shard_map/halve_mixed/pallas_call | solution.py:356
  105.8 2.0 %halve_grad.1 = (f32[128,768]{1,0:T(8,128)}, bf16[128,768]{1,0:T(8,128)(2,1)}) custom-call(s32[1]{0:T(128)} %bitcast.2.high_ref.bit_ref, bf16[256,768]{1,0:T(8,128)(2,1)} %get-tuple-element.66.kept_ref, bf16[256,768]{1,0:T(8,128)(2,1)} %collective-permute-done.15.got_ref), custom_call_target="tpu_custom_call" | custom-call | bytes 786432 | tf_op jit(solution)/shard_map/halve_grad/pallas_call | solution.py:356
  109.3 4.3 %collective-permute-done.16 = bf16[128,768]{1,0:T(8,128)(2,1)S(1)} collective-permute-done((bf16[128,768]{1,0:T(8,128)(2,1)}, bf16[128,768]{1,0:T(8,128)(2,1)S(1)}, u32[]{:S(2)}, u32[]{:S(2)}) %collective-permute-start.16) | collective-permute-done | bytes 196640 | tf_op jit(solution)/shard_map/ppermute | solution.py:23
  116.3 1.5 %collective-permute-start.22 = (f32[1,384]{1,0:T(1,128)S(1)}, f32[1,384]{1,0:T(1,128)S(1)}, u32[]{:S(2)}, u32[]{:S(2)}) collective-permute-start(f32[1,384]{1,0:T(1,128)S(1)} %slice.81), channel_id=1, source_target_pairs={{0,4},{4,0},{1,5},{5,1},{2,6},{6,2},{3,7},{7,3},{8,12},{12,8},{9,1... | collective-permute-start | bytes 4616 | tf_op jit(solution)/shard_map/ppermute | solution.py:23
  119.5 2.2 %collective-permute-done.18 = f32[3,384]{1,0:T(4,128)S(1)} collective-permute-done((f32[3,384]{1,0:T(4,128)S(1)}, f32[3,384]{1,0:T(4,128)S(1)}, u32[]{:S(2)}, u32[]{:S(2)}) %collective-permute-start.18) | collective-permute-done | bytes 4640 | tf_op jit(solution)/shard_map/ppermute | solution.py:23
  122.3 3.0 %collective-permute-done.22 = f32[1,384]{1,0:T(1,128)S(1)} collective-permute-done((f32[1,384]{1,0:T(1,128)S(1)}, f32[1,384]{1,0:T(1,128)S(1)}, u32[]{:S(2)}, u32[]{:S(2)}) %collective-permute-start.22) | collective-permute-done | bytes 1568 | tf_op jit(solution)/shard_map/ppermute | solution.py:23
  (102 shorter events, 27.4 us)
Async XLA Ops:
  0.7 12.1 %collective-permute-start = (bf16[128,768]{1,0:T(8,128)(2,1)}, bf16[128,768]{1,0:T(8,128)(2,1)S(1)}, u32[]{:S(2)}, u32[]{:S(2)}) collective-permute-start(bf16[128,768]{1,0:T(8,128)(2,1)} %bitcast.64), channel_id=1, source_target_pairs={{0,4},{4,0},{1,5},{5,1},{2,6},{6,2},{3,7},{7,3},{8,12},{12,8},{9,1... | collective-permute-start | bytes 589832 | tf_op jit(solution)/shard_map/ppermute | solution.py:23
  3.7 10.8 %collective-permute-start.3 = (bf16[128,768]{1,0:T(8,128)(2,1)}, bf16[128,768]{1,0:T(8,128)(2,1)S(1)}, u32[]{:S(2)}, u32[]{:S(2)}) collective-permute-start(bf16[128,768]{1,0:T(8,128)(2,1)} %bitcast.67), channel_id=1, source_target_pairs={{0,2},{1,3},{2,0},{3,1},{4,6},{5,7},{6,4},{7,5},{8,10},{9,11},{10,... | collective-permute-start | bytes 589832 | tf_op jit(solution)/shard_map/ppermute | solution.py:23
  7.2 29.3 %collective-permute-start.6 = (bf16[200,768]{1,0:T(8,128)(2,1)}, bf16[200,768]{1,0:T(8,128)(2,1)}, u32[]{:S(2)}, u32[]{:S(2)}) collective-permute-start(bf16[200,768]{1,0:T(8,128)(2,1)} %pack_attention.1.refs_0_), channel_id=1, source_target_pairs={{0,8},{8,16},{16,24},{24,0},{1,9},{9,17},{17,25},{25,1},{2,10},{10... | collective-permute-start | bytes 921608 | tf_op jit(solution)/shard_map/ppermute | solution.py:49
  8.8 27.7 %collective-permute-start.7 = (bf16[200,768]{1,0:T(8,128)(2,1)}, bf16[200,768]{1,0:T(8,128)(2,1)}, u32[]{:S(2)}, u32[]{:S(2)}) collective-permute-start(bf16[200,768]{1,0:T(8,128)(2,1)} %pack_attention.1.refs_0_), channel_id=1, source_target_pairs={{0,16},{8,24},{16,0},{24,8},{1,17},{9,25},{17,1},{25,9},{2,18},{10... | collective-permute-start | bytes 921608 | tf_op jit(solution)/shard_map/ppermute | solution.py:49
  11.4 25.2 %collective-permute-start.8 = (bf16[200,768]{1,0:T(8,128)(2,1)}, bf16[200,768]{1,0:T(8,128)(2,1)}, u32[]{:S(2)}, u32[]{:S(2)}) collective-permute-start(bf16[200,768]{1,0:T(8,128)(2,1)} %pack_attention.1.refs_0_), channel_id=1, source_target_pairs={{0,24},{8,0},{16,8},{24,16},{1,25},{9,1},{17,9},{25,17},{2,26},{10... | collective-permute-start | bytes 921608 | tf_op jit(solution)/shard_map/ppermute | solution.py:49
  13.9 9.5 %collective-permute-start.1 = (bf16[2,128,768]{2,1,0:T(8,128)(2,1)S(1)}, bf16[2,128,768]{2,1,0:T(8,128)(2,1)S(1)}, u32[]{:S(2)}, u32[]{:S(2)}) collective-permute-start(bf16[2,128,768]{2,1,0:T(8,128)(2,1)S(1)} %maximum_select_fusion.7), channel_id=1, source_target_pairs={{0,2},{1,3},{2,0},{3,1},{4,6},{5,7},{6,4},{7,5},{8,10},{9,11},{10,... | collective-permute-start | bytes 1179656 | tf_op jit(solution)/shard_map/ppermute | solution.py:23
  14.5 9.2 %collective-permute-start.4 = (bf16[2,128,768]{2,1,0:T(8,128)(2,1)S(1)}, bf16[2,128,768]{2,1,0:T(8,128)(2,1)S(1)}, u32[]{:S(2)}, u32[]{:S(2)}) collective-permute-start(bf16[2,128,768]{2,1,0:T(8,128)(2,1)S(1)} %maximum_select_fusion.8), channel_id=1, source_target_pairs={{0,4},{4,0},{1,5},{5,1},{2,6},{6,2},{3,7},{7,3},{8,12},{12,8},{9,1... | collective-permute-start | bytes 1179656 | tf_op jit(solution)/shard_map/ppermute | solution.py:23
  23.9 6.7 %collective-permute-start.5 = (bf16[2,2,128,768]{3,2,1,0:T(8,128)(2,1)S(1)}, bf16[2,2,128,768]{3,2,1,0:T(8,128)(2,1)}, u32[]{:S(2)}, u32[]{:S(2)}) collective-permute-start(bf16[2,2,128,768]{3,2,1,0:T(8,128)(2,1)S(1)} %maximum_select_fusion.4), channel_id=1, source_target_pairs={{0,1},{1,0},{2,3},{3,2},{4,5},{5,4},{6,7},{7,6},{8,9},{9,8},{10,11... | collective-permute-start | bytes 2359304 | tf_op jit(solution)/shard_map/ppermute | solution.py:23
  26.3 42.4 %all-to-all-start = ((bf16[4,384,384]{2,1,0:T(8,128)(2,1)}), bf16[4,384,384]{2,1,0:T(8,128)(2,1)}, u32[]{:S(2)}, u32[]{:S(2)}) async-start(bf16[4,384,384]{2,1,0:T(8,128)(2,1)} %pack_feed.1), calls=%async_computation | async-start | bytes 2359296 | tf_op jit(solution)/shard_map/all_to_all | solution.py:53
  58.1 20.3 %collective-permute-start.9 = (bf16[192,384]{1,0:T(8,128)(2,1)}, bf16[192,384]{1,0:T(8,128)(2,1)}, u32[]{:S(2)}, u32[]{:S(2)}) collective-permute-start(bf16[192,384]{1,0:T(8,128)(2,1)} %get-tuple-element.57), channel_id=1, source_target_pairs={{0,8},{8,16},{16,24},{24,0},{1,9},{9,17},{17,25},{25,1},{2,10},{10... | collective-permute-start | bytes 442376 | tf_op jit(solution)/shard_map/ppermute | solution.py:49
  66.2 12.2 %collective-permute-start.10 = (bf16[192,384]{1,0:T(8,128)(2,1)}, bf16[192,384]{1,0:T(8,128)(2,1)S(1)}, u32[]{:S(2)}, u32[]{:S(2)}) collective-permute-start(bf16[192,384]{1,0:T(8,128)(2,1)} %get-tuple-element.58), channel_id=1, source_target_pairs={{0,16},{8,24},{16,0},{24,8},{1,17},{9,25},{17,1},{25,9},{2,18},{10... | collective-permute-start | bytes 442376 | tf_op jit(solution)/shard_map/ppermute | solution.py:49
  66.2 12.2 %collective-permute-start.11 = (bf16[192,384]{1,0:T(8,128)(2,1)}, bf16[192,384]{1,0:T(8,128)(2,1)S(1)}, u32[]{:S(2)}, u32[]{:S(2)}) collective-permute-start(bf16[192,384]{1,0:T(8,128)(2,1)} %get-tuple-element.59), channel_id=1, source_target_pairs={{0,24},{8,0},{16,8},{24,16},{1,25},{9,1},{17,9},{25,17},{2,26},{10... | collective-permute-start | bytes 442376 | tf_op jit(solution)/shard_map/ppermute | solution.py:49
  78.5 7.8 %collective-permute-start.12 = (bf16[2,512,768]{2,1,0:T(8,128)(2,1)}, bf16[2,512,768]{2,1,0:T(8,128)(2,1)S(1)}, u32[]{:S(2)}, u32[]{:S(2)}) collective-permute-start(bf16[2,512,768]{2,1,0:T(8,128)(2,1)} %get-tuple-element.61), channel_id=1, source_target_pairs={{0,1},{1,0},{2,3},{3,2},{4,5},{5,4},{6,7},{7,6},{8,9},{9,8},{10,11... | collective-permute-start | bytes 4718600 | tf_op jit(solution)/shard_map/ppermute | solution.py:23
  79.2 35.5 %all-to-all-start.1 = ((bf16[4,392,384]{2,1,0:T(8,128)(2,1)}), bf16[4,392,384]{2,1,0:T(8,128)(2,1)S(1)}, u32[]{:S(2)}, u32[]{:S(2)}) async-start(bf16[4,392,384]{2,1,0:T(8,128)(2,1)} %get-tuple-element.70), calls=%async_computation.1 | async-start | bytes 2408448 | tf_op jit(solution)/shard_map/all_to_all | solution.py:53
  85.7 7.9 %collective-permute-start.20 = (bf16[192,384]{1,0:T(8,128)(2,1)S(1)}, bf16[192,384]{1,0:T(8,128)(2,1)S(1)}, u32[]{:S(2)}, u32[]{:S(2)}) collective-permute-start(bf16[192,384]{1,0:T(8,128)(2,1)S(1)} %reduce-precision_convert_fusion), channel_id=1, source_target_pairs={{0,4},{4,0},{1,5},{5,1},{2,6},{6,2},{3,7},{7,3},{8,12},{12,8},{9,1... | collective-permute-start | bytes 442376 | tf_op jit(solution)/shard_map/ppermute | solution.py:23
  90.7 10.7 %collective-permute-start.13 = (bf16[256,768]{1,0:T(8,128)(2,1)}, bf16[256,768]{1,0:T(8,128)(2,1)}, u32[]{:S(2)}, u32[]{:S(2)}) collective-permute-start(bf16[256,768]{1,0:T(8,128)(2,1)} %get-tuple-element.63), channel_id=1, source_target_pairs={{0,2},{1,3},{2,0},{3,1},{4,6},{5,7},{6,4},{7,5},{8,10},{9,11},{10,... | collective-permute-start | bytes 1179656 | tf_op jit(solution)/shard_map/ppermute | solution.py:23
  91.3 14.5 %collective-permute-start.15 = (bf16[256,768]{1,0:T(8,128)(2,1)}, bf16[256,768]{1,0:T(8,128)(2,1)}, u32[]{:S(2)}, u32[]{:S(2)}) collective-permute-start(bf16[256,768]{1,0:T(8,128)(2,1)} %get-tuple-element.67), channel_id=1, source_target_pairs={{0,4},{4,0},{1,5},{5,1},{2,6},{6,2},{3,7},{7,3},{8,12},{12,8},{9,1... | collective-permute-start | bytes 1179656 | tf_op jit(solution)/shard_map/ppermute | solution.py:23
  103.4 5.9 %collective-permute-start.14 = (bf16[128,768]{1,0:T(8,128)(2,1)}, bf16[128,768]{1,0:T(8,128)(2,1)S(1)}, u32[]{:S(2)}, u32[]{:S(2)}) collective-permute-start(bf16[128,768]{1,0:T(8,128)(2,1)} %get-tuple-element.65), channel_id=1, source_target_pairs={{0,4},{4,0},{1,5},{5,1},{2,6},{6,2},{3,7},{7,3},{8,12},{12,8},{9,1... | collective-permute-start | bytes 589832 | tf_op jit(solution)/shard_map/ppermute | solution.py:23
  107.7 5.9 %collective-permute-start.16 = (bf16[128,768]{1,0:T(8,128)(2,1)}, bf16[128,768]{1,0:T(8,128)(2,1)S(1)}, u32[]{:S(2)}, u32[]{:S(2)}) collective-permute-start(bf16[128,768]{1,0:T(8,128)(2,1)} %get-tuple-element.69), channel_id=1, source_target_pairs={{0,2},{1,3},{2,0},{3,1},{4,6},{5,7},{6,4},{7,5},{8,10},{9,11},{10,... | collective-permute-start | bytes 589832 | tf_op jit(solution)/shard_map/ppermute | solution.py:23
  115.0 3.0 %collective-permute-start.17 = (f32[3,384]{1,0:T(4,128)S(1)}, f32[3,384]{1,0:T(4,128)S(1)}, u32[]{:S(2)}, u32[]{:S(2)}) collective-permute-start(f32[3,384]{1,0:T(4,128)S(1)} %bitcast.86), channel_id=1, source_target_pairs={{0,1},{1,0},{2,3},{3,2},{4,5},{5,4},{6,7},{7,6},{8,9},{9,8},{10,11... | collective-permute-start | bytes 13832 | tf_op jit(solution)/shard_map/ppermute | solution.py:23
  115.8 10.8 %collective-permute-start.21 = (bf16[384,384]{1,0:T(8,128)(2,1)S(1)}, bf16[384,384]{1,0:T(8,128)(2,1)S(1)}, u32[]{:S(2)}, u32[]{:S(2)}) collective-permute-start(bf16[384,384]{1,0:T(8,128)(2,1)S(1)} %fusion.3), channel_id=1, source_target_pairs={{0,4},{4,0},{1,5},{5,1},{2,6},{6,2},{3,7},{7,3},{8,12},{12,8},{9,1... | collective-permute-start | bytes 884744 | tf_op jit(solution)/shard_map/ppermute | solution.py:23
  116.3 9.0 %collective-permute-start.22 = (f32[1,384]{1,0:T(1,128)S(1)}, f32[1,384]{1,0:T(1,128)S(1)}, u32[]{:S(2)}, u32[]{:S(2)}) collective-permute-start(f32[1,384]{1,0:T(1,128)S(1)} %slice.81), channel_id=1, source_target_pairs={{0,4},{4,0},{1,5},{5,1},{2,6},{6,2},{3,7},{7,3},{8,12},{12,8},{9,1... | collective-permute-start | bytes 4616 | tf_op jit(solution)/shard_map/ppermute | solution.py:23
  118.0 3.7 %collective-permute-start.18 = (f32[3,384]{1,0:T(4,128)S(1)}, f32[3,384]{1,0:T(4,128)S(1)}, u32[]{:S(2)}, u32[]{:S(2)}) collective-permute-start(f32[3,384]{1,0:T(4,128)S(1)} %slice_add_fusion.1), channel_id=1, source_target_pairs={{0,2},{1,3},{2,0},{3,1},{4,6},{5,7},{6,4},{7,5},{8,10},{9,11},{10,... | collective-permute-start | bytes 13832 | tf_op jit(solution)/shard_map/ppermute | solution.py:23
  121.7 4.2 %collective-permute-start.19 = (f32[3,384]{1,0:T(4,128)S(1)}, f32[3,384]{1,0:T(4,128)S(1)}, u32[]{:S(2)}, u32[]{:S(2)}) collective-permute-start(f32[3,384]{1,0:T(4,128)S(1)} %add.92), channel_id=1, source_target_pairs={{0,4},{4,0},{1,5},{5,1},{2,6},{6,2},{3,7},{7,3},{8,12},{12,8},{9,1... | collective-permute-start | bytes 13832 | tf_op jit(solution)/shard_map/ppermute | solution.py:23
  (9 other events, 36.5 us)

commit v5 on v4

--- a/solution.py
+++ b/solution.py
@@ -136,11 +136,10 @@
     piece_refs, refs = refs[:shares], refs[shares:]
     normed_ref, cot_ref, cos_ref, sin_ref, seg_row_ref = refs[:5]
     refs = refs[5:]
-    vectors_ref, mixed_ref, grad_normed_ref, sums_ref, bias_grad_ref = refs[:5]
-    part_refs, refs = refs[5 : 5 + shares], refs[5 + shares :]
+    vectors_ref, weights_ref, feature_ref, bias_grad_ref = refs[:4]
+    part_refs, refs = refs[4 : 4 + shares], refs[4 + shares :]
     (
-        weights_ref, small_ref, first_ref, qkv_ref, grad_ref, feature_ref, grad_weights_ref,
-        dq_ref, dk_ref, dv_ref, seg_col_ref,
+        small_ref, first_ref, qkv_ref, grad_ref, grad_weights_ref, dq_ref, dk_ref, dv_ref, seg_col_ref,
     ) = refs
     tokens, model = normed_ref.shape
     share = piece_refs[0].shape[0] - 8
@@ -251,29 +250,44 @@
     for d, ref in enumerate(part_refs):
         ref[...] = grad_weights_ref[rows_at(lax.rem(dp + d, shares), share), :]
 
-    total_one = jnp.zeros((1, model), f32)
-    total_two = jnp.zeros((1, model), f32)
-    for rows in chunks:
-        attended = feature_ref[3 * width :, rows].T
-        mixed_ref[rows, :] = (0.5 * dot(attended, output, ((1,), (1,)))).astype(bf16)
-        grad_first = 0.5 * dot(feature_ref[: 3 * width, rows].T, project, ((1,), (1,)))
-        total_one += jnp.sum(grad_first * normed_ref[rows, :], axis=0, keepdims=True)
-        total_two += jnp.sum(grad_first, axis=0, keepdims=True)
-        grad_normed_ref[rows, :] = (grad_first * gain).astype(bf16)
-    sums_ref[0:1, :] = total_one
-    sums_ref[1:2, :] = total_two
-
 
 def feed_kernel(
-    ctx_ref, low_ref, all_ref, normed_ref, cot_ref, vectors_ref, mixed_in_ref, grad_in_ref,
-    sums_in_ref, bias_in_ref, kept_ref, away_ref, grad_weights_ref, sums_ref,
-    up_ref, down_ref, second_ref, act_ref, pre_ref,
+    ctx_ref, low_ref, all_ref, normed_ref, cot_ref, vectors_ref, weights_ref, feature_ref,
+    bias_in_ref, kept_ref, away_ref, grad_weights_ref, sums_ref,
+    up_ref, down_ref, second_ref, act_ref, pre_ref, mixed_in_ref, grad_in_ref, sums_in_ref,
 ):
     tokens, model = normed_ref.shape
     shares, share, units = all_ref.shape[0], all_ref.shape[1] // 2, all_ref.shape[2]
     for s in range(shares):
         up_ref[s * share : (s + 1) * share, :] = all_ref[s, :share, :]
         down_ref[s * share : (s + 1) * share, :] = all_ref[s, share:, :]
+    width = HD * (model // HD) // 4
+    project = weights_ref[:, : 3 * width]
+    output = weights_ref[:, 3 * width :]
+    chunks = [slice(i, i + ROWS) for i in range(0, tokens, ROWS)]
+    for half in range(2):
+        own = chunks[half * (len(chunks) // 2) : (half + 1) * (len(chunks) // 2)]
+
+        @pl.when(ctx_ref[0] == half)
+        def _():
+            total_one = jnp.zeros((1, model), f32)
+            total_two = jnp.zeros((1, model), f32)
+            for rows in own:
+                attended = feature_ref[3 * width :, rows].T
+                mixed_in_ref[rows, :] = dot(attended, output, ((1,), (1,))).astype(bf16)
+                grad_first = dot(feature_ref[: 3 * width, rows].T, project, ((1,), (1,)))
+                total_one += jnp.sum(grad_first * normed_ref[rows, :], axis=0, keepdims=True)
+                total_two += jnp.sum(grad_first, axis=0, keepdims=True)
+                grad_in_ref[rows, :] = (grad_first * vectors_ref[0:1, :]).astype(bf16)
+            sums_in_ref[0:1, :] = total_one
+            sums_in_ref[1:2, :] = total_two
+
+        @pl.when(ctx_ref[0] != half)
+        def _():
+            for rows in own:
+                mixed_in_ref[rows, :] = jnp.zeros((ROWS, model), bf16)
+                grad_in_ref[rows, :] = jnp.zeros((ROWS, model), bf16)
+
     gain, shift = vectors_ref[2:3, :], vectors_ref[3:4, :]
     bias = jnp.where(
         ctx_ref[0] > 0, vectors_ref[6:7, units : 2 * units], vectors_ref[6:7, :units]
@@ -395,7 +409,9 @@
     )
     few = n_dp == 4
     if few:
-        pieces = [packed] + [shifted(packed, d) for d in range(1, n_dp)]
+        near, far = shifted(packed, 1), shifted(packed, 3)
+        near, far = lax.optimization_barrier((near, far))
+        pieces = [packed, near, shifted(near, 1), far]
     else:
         everything = exchange_dp(jnp.broadcast_to(packed[None], (n_dp,) + packed.shape))
         tail = everything[:, share:]
@@ -428,16 +444,16 @@
 
     frequency = 10000.0 ** (-2.0 * jnp.arange(HALF, dtype=f32) / ROT)
     angles = frequency[:, None] * jnp.arange(tokens, dtype=f32)[None, :]
-    vectors, mixed, grad_normed, attention_sums, project_bias_grad, *attention_parts = call(
+    vectors, weights, feature, project_bias_grad, *attention_parts = call(
         functools.partial(attention_kernel, shares),
         [
-            ((8, model), f32), ((tokens, model), bf16), ((tokens, model), bf16),
-            ((2, model), f32), ((16, HD), f32),
+            ((8, model), f32), ((model, columns), bf16), ((columns, tokens), bf16),
+            ((16, HD), f32),
         ]
         + [((model // shares, 2 * width), bf16)] * shares,
         [
-            ((model, columns), bf16), ((shares, 8, columns), f32), ((tokens, model), bf16),
-            ((3 * width, tokens), f32), ((width, tokens), bf16), ((columns, tokens), bf16),
+            ((shares, 8, columns), f32), ((tokens, model), bf16),
+            ((3 * width, tokens), f32), ((width, tokens), bf16),
             ((model, 2 * width), bf16),
             ((HD, tokens), f32), ((HD, tokens), f32), ((HD, tokens), f32),
             ((tokens, 8), jnp.int32),
@@ -465,12 +481,12 @@
         [
             ((model, half_units), bf16), ((model, half_units), bf16), ((tokens, model), bf16),
             ((half_units, tokens), bf16), ((half_units, tokens), bf16),
+            ((tokens, model), bf16), ((tokens, model), bf16), ((2, model), f32),
         ],
         tokens * model * half_units * 12,
         "feed_part",
         [ctx_index, tensor_index % 2],
-        feed_all, normed, grad_all, vectors, mixed, grad_normed, attention_sums,
-        project_bias_grad,
+        feed_all, normed, grad_all, vectors, weights, feature, project_bias_grad,
     )
     kept, away, grad_feed, attention_parts = lax.optimization_barrier(
         (kept, away, grad_feed, attention_parts)
@@ -520,7 +536,15 @@
         small = small[:3]
     small = small + flipped(small, "tensor", 1)
     small = small + flipped(small, "tensor", 2)
-    small = small + flipped(small, "ctx", 1)
+    if few:
+        small = jnp.concatenate([small, units_row])
+        small_got = flipped(small, "ctx", 1)
+        units_got = small_got[3:]
+    else:
+        small_got = flipped(small, "ctx", 1)
+        units_got = flipped(units_row, "ctx", 1)
+    units_row = joined(units_row, units_got, second)
+    small = small + small_got
     if few:
         shared = [
             small[0, :share], small[0, share:], small[1, :share], small[1, share:],
@@ -528,7 +552,6 @@
         ]
     else:
         shared = [small[i] for i in range(5)]
-    units_row = joined(units_row, flipped(units_row, "ctx", 1), second)
     upward_bias_grad = lax.dynamic_slice_in_dim(
         units_row, dp_index * (units // n_dp), units // n_dp, 1
     )

time: 129 us -> 126 us (0.977)
  starting transfers between devices: 39.4 us -> 32.3 us
  waiting for transfers between devices: 23.4 us -> 25.5 us
  local copies, waits for them, and re-layouts: 8.52 us -> 10.2 us
    ppermute x6, starting transfers between devices: 16.1 us -> 9.74 us  [shifted(): lax.ppermute(block, 'dp', [(i, (i + distance) % count) for i in range(cou...]
    ppermute x17 -> x16, waiting for transfers between devices: 23.4 us -> 25.4 us  [flipped(): lax.ppermute(block, axis, [(i, i ^ bit) for i in range(lax.axis_size(axis...]
    unnamed x19 -> x21, local copies, waits for them, and re-layouts: 4.24 us -> 4.78 us
    ppermute x17 -> x16, starting transfers between devices: 14.1 us -> 14.5 us  [flipped(): lax.ppermute(block, axis, [(i, i ^ bit) for i in range(lax.axis_size(axis...]
  transfers between devices with their start and end apart: 25 -> 24, of which waited for: 8 -> 6; matrix products, arithmetic and copies ran while one was open for 14% -> 16% of each run, Pallas kernels for 33% -> 34%
where the time goes in v5:
time: 126 us; the launch traced here: 125 us
  Pallas kernels  42.3 us (34%)
  starting transfers between devices  32.3 us (26%)
  waiting for transfers between devices  25.5 us (20%)
  other arithmetic  14 us (11%)
  local copies, waits for them, and re-layouts  10.2 us (8%)
    pallas_call x7, Pallas kernels, call(): pl.pallas_call(kernel, out_shape=[jax.ShapeDtypeStruct(shape, dtype) for...  42.3 us
    ppermute x16, waiting for transfers between devices, flipped(): lax.ppermute(block, axis, [(i, i ^ bit) for i in range(lax.axis_size(axis...  25.4 us
    ppermute x16, starting transfers between devices, flipped(): lax.ppermute(block, axis, [(i, i ^ bit) for i in range(lax.axis_size(axis...  14.5 us
    ppermute x6, starting transfers between devices, shifted(): lax.ppermute(block, 'dp', [(i, (i + distance) % count) for i in range(cou...  9.74 us
    all_to_all x2, starting transfers between devices, exchange_dp(): return lax.all_to_all(blocks, 'dp', 0, 0)  8.09 us
    unnamed x21, local copies, waits for them, and re-layouts  4.78 us
    select_n x10, other arithmetic, ordered(): jnp.where(second, jnp.stack([other, own], axis=dim), jnp.stack([own, othe...  4.52 us
  transfers between devices with their start and end apart: 24, of which 6 were waited for; matrix products, arithmetic and copies ran while one was open for 16% of the time, Pallas kernels for 34%

profile of v5, /device:TPU:0, one launch (start us, length us, event | category | flops | bytes accessed | tf_op | source)
XLA Modules:
  0.0 125.3 jit_solution(6676439866738138671)
XLA Ops:
  0.7 3.0 %collective-permute-start = (bf16[128,768]{1,0:T(8,128)(2,1)}, bf16[128,768]{1,0:T(8,128)(2,1)S(1)}, u32[]{:S(2)}, u32[]{:S(2)}) collective-permute-start(bf16[128,768]{1,0:T(8,128)(2,1)} %bitcast.64), channel_id=1, source_target_pairs={{0,4},{4,0},{1,5},{5,1},{2,6},{6,2},{3,7},{7,3},{8,12},{12,8},{9,1... | collective-permute-start | bytes 589832 | tf_op jit(solution)/shard_map/ppermute | solution.py:23
  3.7 1.5 %collective-permute-start.3 = (bf16[128,768]{1,0:T(8,128)(2,1)}, bf16[128,768]{1,0:T(8,128)(2,1)S(1)}, u32[]{:S(2)}, u32[]{:S(2)}) collective-permute-start(bf16[128,768]{1,0:T(8,128)(2,1)} %bitcast.67), channel_id=1, source_target_pairs={{0,2},{1,3},{2,0},{3,1},{4,6},{5,7},{6,4},{7,5},{8,10},{9,11},{10,... | collective-permute-start | bytes 589832 | tf_op jit(solution)/shard_map/ppermute | solution.py:23
  5.2 2.0 %pack_attention.1.refs_0_ = bf16[200,768]{1,0:T(8,128)(2,1)} custom-call(s32[1]{0:T(128)} %bitcast.24.dp_ref, bf16[3,192,192]{2,1,0:T(8,128)(2,1)} %bitcast.84, bf16[192,192]{1,0:T(8,128)(2,1)} %output_ref.1, bf16[3,3,16]{2,1,0:T(4,128)(2,1)} %bias_ref.1, bf16[192]{0:T(256)(128)(2,1)} %refs_0_.1, bf16[192]{0:T(256)(128)(2,1)} %refs_1_.1, ...), custom_call_target="tpu_custom_call" | custom-call | bytes 297888 | tf_op jit(solution)/shard_map/pack_attention/pallas_call | solution.py:370
  7.2 1.6 %collective-permute-start.6 = (bf16[200,768]{1,0:T(8,128)(2,1)}, bf16[200,768]{1,0:T(8,128)(2,1)}, u32[]{:S(2)}, u32[]{:S(2)}) collective-permute-start(bf16[200,768]{1,0:T(8,128)(2,1)} %pack_attention.1.refs_0_), channel_id=1, source_target_pairs={{0,8},{8,16},{16,24},{24,0},{1,9},{9,17},{17,25},{25,1},{2,10},{10... | collective-permute-start | bytes 921608 | tf_op jit(solution)/shard_map/ppermute | solution.py:49
  8.8 2.2 %collective-permute-start.7 = (bf16[200,768]{1,0:T(8,128)(2,1)}, bf16[200,768]{1,0:T(8,128)(2,1)S(1)}, u32[]{:S(2)}, u32[]{:S(2)}) collective-permute-start(bf16[200,768]{1,0:T(8,128)(2,1)} %pack_attention.1.refs_0_), channel_id=1, source_target_pairs={{0,24},{8,0},{16,8},{24,16},{1,25},{9,1},{17,9},{25,17},{2,26},{10... | collective-permute-start | bytes 921608 | tf_op jit(solution)/shard_map/ppermute | solution.py:49
  13.4 8.5 %collective-permute-done.1 = bf16[2,128,768]{2,1,0:T(8,128)(2,1)S(1)} collective-permute-done((bf16[2,128,768]{2,1,0:T(8,128)(2,1)S(1)}, bf16[2,128,768]{2,1,0:T(8,128)(2,1)S(1)}, u32[]{:S(2)}, u32[]{:S(2)}) %collective-permute-start.1) | collective-permute-done | bytes 393248 | tf_op jit(solution)/shard_map/ppermute | solution.py:23
  24.5 2.2 %pack_feed.1 = bf16[4,384,384]{2,1,0:T(8,128)(2,1)} custom-call(s32[1]{0:T(128)} %bitcast.1.ctx_ref.bit_ref, bf16[192,768]{1,0:T(8,128)(2,1)} %up_ref.1, bf16[192,768]{1,0:T(8,128)(2,1)} %bitcast.85), custom_call_target="tpu_custom_call" | custom-call | bytes 589824 | tf_op jit(solution)/shard_map/pack_feed/pallas_call | solution.py:370
  29.3 4.6 %all-to-all-start = ((bf16[4,384,384]{2,1,0:T(8,128)(2,1)}), bf16[4,384,384]{2,1,0:T(8,128)(2,1)}, u32[]{:S(2)}, u32[]{:S(2)}) async-start(bf16[4,384,384]{2,1,0:T(8,128)(2,1)} %pack_feed.1), calls=%async_computation | async-start | bytes 2359296 | tf_op jit(solution)/shard_map/all_to_all | solution.py:53
  33.8 1.7 %maximum_select_fusion.1 = bf16[2,2,2,128,768]{4,3,1,2,0:T(8,128)(2,1)S(1)} fusion(bf16[2,2,1,128,768]{4,3,1,2,0:T(8,128)(2,1)S(1)} %maximum_select_fusion.5, bf16[2,2,1,128,768]{4,3,1,2,0:T(8,128)(2,1)} %bitcast.20, pred[]{:T(512)S(6)} %gt.15), kind=kLoop, calls=%fused_computation.7 | loop fusion | flops 2359296 | bytes 3145729 | tf_op jit(solution)/shard_map/jit(_where)/select_n | solution.py:27
  37.7 2.1 %fusion.refs_4_.normed_ref = f32[1024,768]{1,0:T(8,128)} fusion(bf16[1024,768]{1,0:T(8,128)(2,1)S(1)} %bitcast.63, f32[1024]{0:T(1024)S(1)} %add_rsqrt_fusion, f32[1024]{0:T(1024)S(1)} %broadcast_multiply_fusion), kind=kLoop, calls=%fused_computation.2 | loop fusion | flops 2359296 | bytes 4726784 | tf_op jit(solution)/shard_map/mul | solution.py:443
  39.8 19.6 %attention_part.1 = (f32[8,768]{1,0:T(8,128)}, bf16[768,768]{1,0:T(8,128)(2,1)}, bf16[768,1024]{1,0:T(8,128)(2,1)}, f32[16,64]{1,0:T(8,128)}, bf16[192,384]{1,0:...) custom-call(s32[1]{0:T(128)} %bitcast.1.ctx_ref.bit_ref, ...), custom_call_target="tpu_custom_call" | custom-call | flops 4831838208 | bytes 6017024 | tf_op jit(solution)/shard_map/attention_part/pallas_call | solution.py:370
  59.4 2.0 %collective-permute-start.9 = (bf16[192,384]{1,0:T(8,128)(2,1)}, bf16[192,384]{1,0:T(8,128)(2,1)}, u32[]{:S(2)}, u32[]{:S(2)}) collective-permute-start(bf16[192,384]{1,0:T(8,128)(2,1)} %get-tuple-element.59), channel_id=1, source_target_pairs={{0,8},{8,16},{16,24},{24,0},{1,9},{9,17},{17,25},{25,1},{2,10},{10... | collective-permute-start | bytes 442376 | tf_op jit(solution)/shard_map/ppermute | solution.py:49
  61.4 2.4 %collective-permute-start.10 = (bf16[192,384]{1,0:T(8,128)(2,1)}, bf16[192,384]{1,0:T(8,128)(2,1)S(1)}, u32[]{:S(2)}, u32[]{:S(2)}) collective-permute-start(bf16[192,384]{1,0:T(8,128)(2,1)} %get-tuple-element.60), channel_id=1, source_target_pairs={{0,16},{8,24},{16,0},{24,8},{1,17},{9,25},{17,1},{25,9},{2,18},{10... | collective-permute-start | bytes 442376 | tf_op jit(solution)/shard_map/ppermute | solution.py:49
  65.3 11.3 %feed_part.1 = (bf16[2,512,768]{2,1,0:T(8,128)(2,1)}, bf16[2,512,768]{2,1,0:T(8,128)(2,1)}, bf16[4,392,384]{2,1,0:T(8,128)(2,1)}, f32[8,768]{1,0:T(8,128)}) custom-call(s32[1]{0:T(128)} %bitcast.1.ctx_ref.bit_ref, s32[1]{0:T(128)} %bitcast.3.low_ref, bf16[4,384,384]{2,1,0:T(8,128)(2,1)} %all-to-all-done.all_ref, f32[1024,768]{1,0:T(8,128)} %fusion.refs_4_.normed_ref, ...), custom_call_target="tpu_custom_call" | custom-call | flops 3623878656 | bytes 8679424 | tf_op jit(solution)/shard_map/feed_part/pallas_call | solution.py:370
  77.3 3.5 %all-to-all-start.1 = ((bf16[4,392,384]{2,1,0:T(8,128)(2,1)}), bf16[4,392,384]{2,1,0:T(8,128)(2,1)S(1)}, u32[]{:S(2)}, u32[]{:S(2)}) async-start(bf16[4,392,384]{2,1,0:T(8,128)(2,1)} %get-tuple-element.72), calls=%async_computation.1 | async-start | bytes 2408448 | tf_op jit(solution)/shard_map/all_to_all | solution.py:53
  84.1 3.3 %split.1 = (bf16[256,768]{1,0:T(8,128)(2,1)}, bf16[256,768]{1,0:T(8,128)(2,1)}, bf16[256,768]{1,0:T(8,128)(2,1)}, bf16[256,768]{1,0:T(8,128)(2,1)}) custom-call(s32[1]{0:T(128)} %bitcast.2.high_ref.bit_ref, s32[1]{0:T(128)} %bitcast.1.ctx_ref.bit_ref, bf16[2,512,768]{2,1,0:T(8,128)(2,1)} %get-tuple-element.62.kept_ref, bf16[2,512,768]{2,1,0:T(8,128)(2,1)} %copy-done.2), custom_call_target="tpu_custom_call" | custom-call | bytes 3145728 | tf_op jit(solution)/shard_map/split/pallas_call | solution.py:370
  91.7 6.7 %collective-permute-done.13.got_ref = bf16[256,768]{1,0:T(8,128)(2,1)} collective-permute-done((bf16[256,768]{1,0:T(8,128)(2,1)}, bf16[256,768]{1,0:T(8,128)(2,1)}, u32[]{:S(2)}, u32[]{:S(2)}) %collective-permute-start.13) | collective-permute-done | bytes 393248 | tf_op jit(solution)/shard_map/ppermute | solution.py:23
  98.4 2.0 %halve_mixed.1 = (f32[128,768]{1,0:T(8,128)}, bf16[128,768]{1,0:T(8,128)(2,1)}) custom-call(s32[1]{0:T(128)} %bitcast.1.ctx_ref.bit_ref, bf16[256,768]{1,0:T(8,128)(2,1)} %get-tuple-element.64.kept_ref, bf16[256,768]{1,0:T(8,128)(2,1)} %collective-permute-done.13.got_ref), custom_call_target="tpu_custom_call" | custom-call | bytes 786432 | tf_op jit(solution)/shard_map/halve_mixed/pallas_call | solution.py:370
  100.3 1.5 %collective-permute-start.14 = (bf16[128,768]{1,0:T(8,128)(2,1)}, bf16[128,768]{1,0:T(8,128)(2,1)S(1)}, u32[]{:S(2)}, u32[]{:S(2)}) collective-permute-start(bf16[128,768]{1,0:T(8,128)(2,1)} %get-tuple-element.67), channel_id=1, source_target_pairs={{0,4},{4,0},{1,5},{5,1},{2,6},{6,2},{3,7},{7,3},{8,12},{12,8},{9,1... | collective-permute-start | bytes 589832 | tf_op jit(solution)/shard_map/ppermute | solution.py:23
  102.7 2.0 %halve_grad.1 = (f32[128,768]{1,0:T(8,128)}, bf16[128,768]{1,0:T(8,128)(2,1)}) custom-call(s32[1]{0:T(128)} %bitcast.2.high_ref.bit_ref, bf16[256,768]{1,0:T(8,128)(2,1)} %get-tuple-element.68.kept_ref, bf16[256,768]{1,0:T(8,128)(2,1)} %collective-permute-done.15.got_ref), custom_call_target="tpu_custom_call" | custom-call | bytes 786432 | tf_op jit(solution)/shard_map/halve_grad/pallas_call | solution.py:370
  106.3 4.3 %collective-permute-done.16 = bf16[128,768]{1,0:T(8,128)(2,1)S(1)} collective-permute-done((bf16[128,768]{1,0:T(8,128)(2,1)}, bf16[128,768]{1,0:T(8,128)(2,1)S(1)}, u32[]{:S(2)}, u32[]{:S(2)}) %collective-permute-start.16) | collective-permute-done | bytes 196640 | tf_op jit(solution)/shard_map/ppermute | solution.py:23
  114.9 2.2 %collective-permute-done.18 = f32[3,384]{1,0:T(4,128)S(1)} collective-permute-done((f32[3,384]{1,0:T(4,128)S(1)}, f32[3,384]{1,0:T(4,128)S(1)}, u32[]{:S(2)}, u32[]{:S(2)}) %collective-permute-start.18) | collective-permute-done | bytes 4640 | tf_op jit(solution)/shard_map/ppermute | solution.py:23
  117.2 1.5 %collective-permute-start.19 = (f32[4,384]{1,0:T(4,128)S(1)}, f32[4,384]{1,0:T(4,128)S(1)}, u32[]{:S(2)}, u32[]{:S(2)}) collective-permute-start(f32[4,384]{1,0:T(4,128)S(1)} %pad_maximum_fusion), channel_id=1, source_target_pairs={{0,4},{4,0},{1,5},{5,1},{2,6},{6,2},{3,7},{7,3},{8,12},{12,8},{9,1... | collective-permute-start | bytes 18440 | tf_op jit(solution)/shard_map/ppermute | solution.py:23
  119.6 2.6 %collective-permute-done.19 = f32[4,384]{1,0:T(4,128)S(1)} collective-permute-done((f32[4,384]{1,0:T(4,128)S(1)}, f32[4,384]{1,0:T(4,128)S(1)}, u32[]{:S(2)}, u32[]{:S(2)}) %collective-permute-start.19) | collective-permute-done | bytes 6176 | tf_op jit(solution)/shard_map/ppermute | solution.py:23
  (104 shorter events, 30.0 us)
Async XLA Ops:
  0.7 10.4 %collective-permute-start = (bf16[128,768]{1,0:T(8,128)(2,1)}, bf16[128,768]{1,0:T(8,128)(2,1)S(1)}, u32[]{:S(2)}, u32[]{:S(2)}) collective-permute-start(bf16[128,768]{1,0:T(8,128)(2,1)} %bitcast.64), channel_id=1, source_target_pairs={{0,4},{4,0},{1,5},{5,1},{2,6},{6,2},{3,7},{7,3},{8,12},{12,8},{9,1... | collective-permute-start | bytes 589832 | tf_op jit(solution)/shard_map/ppermute | solution.py:23
  3.7 9.0 %collective-permute-start.3 = (bf16[128,768]{1,0:T(8,128)(2,1)}, bf16[128,768]{1,0:T(8,128)(2,1)S(1)}, u32[]{:S(2)}, u32[]{:S(2)}) collective-permute-start(bf16[128,768]{1,0:T(8,128)(2,1)} %bitcast.67), channel_id=1, source_target_pairs={{0,2},{1,3},{2,0},{3,1},{4,6},{5,7},{6,4},{7,5},{8,10},{9,11},{10,... | collective-permute-start | bytes 589832 | tf_op jit(solution)/shard_map/ppermute | solution.py:23
  7.2 19.6 %collective-permute-start.6 = (bf16[200,768]{1,0:T(8,128)(2,1)}, bf16[200,768]{1,0:T(8,128)(2,1)}, u32[]{:S(2)}, u32[]{:S(2)}) collective-permute-start(bf16[200,768]{1,0:T(8,128)(2,1)} %pack_attention.1.refs_0_), channel_id=1, source_target_pairs={{0,8},{8,16},{16,24},{24,0},{1,9},{9,17},{17,25},{25,1},{2,10},{10... | collective-permute-start | bytes 921608 | tf_op jit(solution)/shard_map/ppermute | solution.py:49
  8.8 18.0 %collective-permute-start.7 = (bf16[200,768]{1,0:T(8,128)(2,1)}, bf16[200,768]{1,0:T(8,128)(2,1)S(1)}, u32[]{:S(2)}, u32[]{:S(2)}) collective-permute-start(bf16[200,768]{1,0:T(8,128)(2,1)} %pack_attention.1.refs_0_), channel_id=1, source_target_pairs={{0,24},{8,0},{16,8},{24,16},{1,25},{9,1},{17,9},{25,17},{2,26},{10... | collective-permute-start | bytes 921608 | tf_op jit(solution)/shard_map/ppermute | solution.py:49
  12.1 9.9 %collective-permute-start.1 = (bf16[2,128,768]{2,1,0:T(8,128)(2,1)S(1)}, bf16[2,128,768]{2,1,0:T(8,128)(2,1)S(1)}, u32[]{:S(2)}, u32[]{:S(2)}) collective-permute-start(bf16[2,128,768]{2,1,0:T(8,128)(2,1)S(1)} %maximum_select_fusion.7), channel_id=1, source_target_pairs={{0,2},{1,3},{2,0},{3,1},{4,6},{5,7},{6,4},{7,5},{8,10},{9,11},{10,... | collective-permute-start | bytes 1179656 | tf_op jit(solution)/shard_map/ppermute | solution.py:23
  12.8 10.2 %collective-permute-start.4 = (bf16[2,128,768]{2,1,0:T(8,128)(2,1)S(1)}, bf16[2,128,768]{2,1,0:T(8,128)(2,1)S(1)}, u32[]{:S(2)}, u32[]{:S(2)}) collective-permute-start(bf16[2,128,768]{2,1,0:T(8,128)(2,1)S(1)} %maximum_select_fusion.8), channel_id=1, source_target_pairs={{0,4},{4,0},{1,5},{5,1},{2,6},{6,2},{3,7},{7,3},{8,12},{12,8},{9,1... | collective-permute-start | bytes 1179656 | tf_op jit(solution)/shard_map/ppermute | solution.py:23
  23.0 4.7 %collective-permute-start.2 = (bf16[2,2,128,768]{3,2,0,1:T(8,128)(2,1)}, bf16[2,2,128,768]{3,2,0,1:T(8,128)(2,1)}, u32[]{:S(2)}, u32[]{:S(2)}) collective-permute-start(bf16[2,2,128,768]{3,2,0,1:T(8,128)(2,1)} %maximum_select_fusion.2), channel_id=1, source_target_pairs={{0,1},{1,0},{2,3},{3,2},{4,5},{5,4},{6,7},{7,6},{8,9},{9,8},{10,11... | collective-permute-start | bytes 2359304 | tf_op jit(solution)/shard_map/ppermute | solution.py:23
  23.1 10.7 %collective-permute-start.5 = (bf16[2,2,128,768]{3,2,1,0:T(8,128)(2,1)S(1)}, bf16[2,2,128,768]{3,2,1,0:T(8,128)(2,1)}, u32[]{:S(2)}, u32[]{:S(2)}) collective-permute-start(bf16[2,2,128,768]{3,2,1,0:T(8,128)(2,1)S(1)} %maximum_select_fusion.4), channel_id=1, source_target_pairs={{0,1},{1,0},{2,3},{3,2},{4,5},{5,4},{6,7},{7,6},{8,9},{9,8},{10,11... | collective-permute-start | bytes 2359304 | tf_op jit(solution)/shard_map/ppermute | solution.py:23
  26.8 13.0 %collective-permute-start.8 = (bf16[200,768]{1,0:T(8,128)(2,1)}, bf16[200,768]{1,0:T(8,128)(2,1)}, u32[]{:S(2)}, u32[]{:S(2)}) collective-permute-start(bf16[200,768]{1,0:T(8,128)(2,1)} %collective-permute-done.6.refs_1_), channel_id=1, source_target_pairs={{0,8},{8,16},{16,24},{24,0},{1,9},{9,17},{17,25},{25,1},{2,10},{10... | collective-permute-start | bytes 921608 | tf_op jit(solution)/shard_map/ppermute | solution.py:49
  29.3 36.0 %all-to-all-start = ((bf16[4,384,384]{2,1,0:T(8,128)(2,1)}), bf16[4,384,384]{2,1,0:T(8,128)(2,1)}, u32[]{:S(2)}, u32[]{:S(2)}) async-start(bf16[4,384,384]{2,1,0:T(8,128)(2,1)} %pack_feed.1), calls=%async_computation | async-start | bytes 2359296 | tf_op jit(solution)/shard_map/all_to_all | solution.py:53
  59.4 17.1 %collective-permute-start.9 = (bf16[192,384]{1,0:T(8,128)(2,1)}, bf16[192,384]{1,0:T(8,128)(2,1)}, u32[]{:S(2)}, u32[]{:S(2)}) collective-permute-start(bf16[192,384]{1,0:T(8,128)(2,1)} %get-tuple-element.59), channel_id=1, source_target_pairs={{0,8},{8,16},{16,24},{24,0},{1,9},{9,17},{17,25},{25,1},{2,10},{10... | collective-permute-start | bytes 442376 | tf_op jit(solution)/shard_map/ppermute | solution.py:49
  61.4 15.1 %collective-permute-start.10 = (bf16[192,384]{1,0:T(8,128)(2,1)}, bf16[192,384]{1,0:T(8,128)(2,1)S(1)}, u32[]{:S(2)}, u32[]{:S(2)}) collective-permute-start(bf16[192,384]{1,0:T(8,128)(2,1)} %get-tuple-element.60), channel_id=1, source_target_pairs={{0,16},{8,24},{16,0},{24,8},{1,17},{9,25},{17,1},{25,9},{2,18},{10... | collective-permute-start | bytes 442376 | tf_op jit(solution)/shard_map/ppermute | solution.py:49
  63.8 12.8 %collective-permute-start.11 = (bf16[192,384]{1,0:T(8,128)(2,1)}, bf16[192,384]{1,0:T(8,128)(2,1)S(1)}, u32[]{:S(2)}, u32[]{:S(2)}) collective-permute-start(bf16[192,384]{1,0:T(8,128)(2,1)} %get-tuple-element.61), channel_id=1, source_target_pairs={{0,24},{8,0},{16,8},{24,16},{1,25},{9,1},{17,9},{25,17},{2,26},{10... | collective-permute-start | bytes 442376 | tf_op jit(solution)/shard_map/ppermute | solution.py:49
  76.6 6.3 %collective-permute-start.12 = (bf16[2,512,768]{2,1,0:T(8,128)(2,1)}, bf16[2,512,768]{2,1,0:T(8,128)(2,1)S(1)}, u32[]{:S(2)}, u32[]{:S(2)}) collective-permute-start(bf16[2,512,768]{2,1,0:T(8,128)(2,1)} %get-tuple-element.63), channel_id=1, source_target_pairs={{0,1},{1,0},{2,3},{3,2},{4,5},{5,4},{6,7},{7,6},{8,9},{9,8},{10,11... | collective-permute-start | bytes 4718600 | tf_op jit(solution)/shard_map/ppermute | solution.py:23
  77.3 34.3 %all-to-all-start.1 = ((bf16[4,392,384]{2,1,0:T(8,128)(2,1)}), bf16[4,392,384]{2,1,0:T(8,128)(2,1)S(1)}, u32[]{:S(2)}, u32[]{:S(2)}) async-start(bf16[4,392,384]{2,1,0:T(8,128)(2,1)} %get-tuple-element.72), calls=%async_computation.1 | async-start | bytes 2408448 | tf_op jit(solution)/shard_map/all_to_all | solution.py:53
  82.3 7.9 %collective-permute-start.20 = (bf16[192,384]{1,0:T(8,128)(2,1)S(1)}, bf16[192,384]{1,0:T(8,128)(2,1)S(1)}, u32[]{:S(2)}, u32[]{:S(2)}) collective-permute-start(bf16[192,384]{1,0:T(8,128)(2,1)S(1)} %reduce-precision_convert_fusion), channel_id=1, source_target_pairs={{0,4},{4,0},{1,5},{5,1},{2,6},{6,2},{3,7},{7,3},{8,12},{12,8},{9,1... | collective-permute-start | bytes 442376 | tf_op jit(solution)/shard_map/ppermute | solution.py:23
  87.4 11.0 %collective-permute-start.13 = (bf16[256,768]{1,0:T(8,128)(2,1)}, bf16[256,768]{1,0:T(8,128)(2,1)}, u32[]{:S(2)}, u32[]{:S(2)}) collective-permute-start(bf16[256,768]{1,0:T(8,128)(2,1)} %get-tuple-element.65), channel_id=1, source_target_pairs={{0,2},{1,3},{2,0},{3,1},{4,6},{5,7},{6,4},{7,5},{8,10},{9,11},{10,... | collective-permute-start | bytes 1179656 | tf_op jit(solution)/shard_map/ppermute | solution.py:23
  88.8 13.9 %collective-permute-start.15 = (bf16[256,768]{1,0:T(8,128)(2,1)}, bf16[256,768]{1,0:T(8,128)(2,1)}, u32[]{:S(2)}, u32[]{:S(2)}) collective-permute-start(bf16[256,768]{1,0:T(8,128)(2,1)} %get-tuple-element.69), channel_id=1, source_target_pairs={{0,4},{4,0},{1,5},{5,1},{2,6},{6,2},{3,7},{7,3},{8,12},{12,8},{9,1... | collective-permute-start | bytes 1179656 | tf_op jit(solution)/shard_map/ppermute | solution.py:23
  100.3 5.9 %collective-permute-start.14 = (bf16[128,768]{1,0:T(8,128)(2,1)}, bf16[128,768]{1,0:T(8,128)(2,1)S(1)}, u32[]{:S(2)}, u32[]{:S(2)}) collective-permute-start(bf16[128,768]{1,0:T(8,128)(2,1)} %get-tuple-element.67), channel_id=1, source_target_pairs={{0,4},{4,0},{1,5},{5,1},{2,6},{6,2},{3,7},{7,3},{8,12},{12,8},{9,1... | collective-permute-start | bytes 589832 | tf_op jit(solution)/shard_map/ppermute | solution.py:23
  104.7 5.9 %collective-permute-start.16 = (bf16[128,768]{1,0:T(8,128)(2,1)}, bf16[128,768]{1,0:T(8,128)(2,1)S(1)}, u32[]{:S(2)}, u32[]{:S(2)}) collective-permute-start(bf16[128,768]{1,0:T(8,128)(2,1)} %get-tuple-element.71), channel_id=1, source_target_pairs={{0,2},{1,3},{2,0},{3,1},{4,6},{5,7},{6,4},{7,5},{8,10},{9,11},{10,... | collective-permute-start | bytes 589832 | tf_op jit(solution)/shard_map/ppermute | solution.py:23
  111.9 1.5 %collective-permute-start.17 = (f32[3,384]{1,0:T(4,128)S(1)}, f32[3,384]{1,0:T(4,128)S(1)}, u32[]{:S(2)}, u32[]{:S(2)}) collective-permute-start(f32[3,384]{1,0:T(4,128)S(1)} %bitcast.86), channel_id=1, source_target_pairs={{0,1},{1,0},{2,3},{3,2},{4,5},{5,4},{6,7},{7,6},{8,9},{9,8},{10,11... | collective-permute-start | bytes 13832 | tf_op jit(solution)/shard_map/ppermute | solution.py:23
  112.7 10.9 %collective-permute-start.21 = (bf16[384,384]{1,0:T(8,128)(2,1)S(1)}, bf16[384,384]{1,0:T(8,128)(2,1)S(1)}, u32[]{:S(2)}, u32[]{:S(2)}) collective-permute-start(bf16[384,384]{1,0:T(8,128)(2,1)S(1)} %fusion.3), channel_id=1, source_target_pairs={{0,4},{4,0},{1,5},{5,1},{2,6},{6,2},{3,7},{7,3},{8,12},{12,8},{9,1... | collective-permute-start | bytes 884744 | tf_op jit(solution)/shard_map/ppermute | solution.py:23
  113.5 3.7 %collective-permute-start.18 = (f32[3,384]{1,0:T(4,128)S(1)}, f32[3,384]{1,0:T(4,128)S(1)}, u32[]{:S(2)}, u32[]{:S(2)}) collective-permute-start(f32[3,384]{1,0:T(4,128)S(1)} %slice_add_fusion.1), channel_id=1, source_target_pairs={{0,2},{1,3},{2,0},{3,1},{4,6},{5,7},{6,4},{7,5},{8,10},{9,11},{10,... | collective-permute-start | bytes 13832 | tf_op jit(solution)/shard_map/ppermute | solution.py:23
  117.2 5.0 %collective-permute-start.19 = (f32[4,384]{1,0:T(4,128)S(1)}, f32[4,384]{1,0:T(4,128)S(1)}, u32[]{:S(2)}, u32[]{:S(2)}) collective-permute-start(f32[4,384]{1,0:T(4,128)S(1)} %pad_maximum_fusion), channel_id=1, source_target_pairs={{0,4},{4,0},{1,5},{5,1},{2,6},{6,2},{3,7},{7,3},{8,12},{12,8},{9,1... | collective-permute-start | bytes 18440 | tf_op jit(solution)/shard_map/ppermute | solution.py:23
  (9 other events, 40.3 us)

commit v6 on v5

--- a/solution.py
+++ b/solution.py
@@ -534,8 +534,6 @@
         units_row = small[3:4]
         bias_row = small[2, share : share + 3 * heads * bias_share]
         small = small[:3]
-    small = small + flipped(small, "tensor", 1)
-    small = small + flipped(small, "tensor", 2)
     if few:
         small = jnp.concatenate([small, units_row])
         small_got = flipped(small, "ctx", 1)
@@ -545,6 +543,9 @@
         units_got = flipped(units_row, "ctx", 1)
     units_row = joined(units_row, units_got, second)
     small = small + small_got
+    small = small[:3] if few else small
+    small = small + flipped(small, "tensor", 2)
+    small = small + flipped(small, "tensor", 1)
     if few:
         shared = [
             small[0, :share], small[0, share:], small[1, :share], small[1, share:],

time: 126 us -> 124 us (0.984)
  waiting for transfers between devices: 25.5 us -> 24.1 us
    ppermute x16, waiting for transfers between devices: 25.4 us -> 24.1 us  [flipped(): lax.ppermute(block, axis, [(i, i ^ bit) for i in range(lax.axis_size(axis...]
  transfers between devices with their start and end apart: 24 -> 24, of which waited for: 6 -> 7; matrix products, arithmetic and copies ran while one was open for 16% -> 16% of each run, Pallas kernels for 34% -> 34%
where the time goes in v6:
time: 124 us; the launch traced here: 123 us
  Pallas kernels  42.3 us (34%)
  starting transfers between devices  31.3 us (25%)
  waiting for transfers between devices  24.1 us (19%)
  other arithmetic  14 us (11%)
  local copies, waits for them, and re-layouts  10.3 us (8%)
    pallas_call x7, Pallas kernels, call(): pl.pallas_call(kernel, out_shape=[jax.ShapeDtypeStruct(shape, dtype) for...  42.3 us
    ppermute x16, waiting for transfers between devices, flipped(): lax.ppermute(block, axis, [(i, i ^ bit) for i in range(lax.axis_size(axis...  24.1 us
    ppermute x16, starting transfers between devices, flipped(): lax.ppermute(block, axis, [(i, i ^ bit) for i in range(lax.axis_size(axis...  13.5 us
    ppermute x6, starting transfers between devices, shifted(): lax.ppermute(block, 'dp', [(i, (i + distance) % count) for i in range(cou...  9.74 us
    all_to_all x2, starting transfers between devices, exchange_dp(): return lax.all_to_all(blocks, 'dp', 0, 0)  8.09 us
    unnamed x21, local copies, waits for them, and re-layouts  4.78 us
    select_n x10, other arithmetic, ordered(): jnp.where(second, jnp.stack([other, own], axis=dim), jnp.stack([own, othe...  4.52 us
  transfers between devices with their start and end apart: 24, of which 7 were waited for; matrix products, arithmetic and copies ran while one was open for 16% of the time, Pallas kernels for 34%

profile of v6, /device:TPU:0, one launch (start us, length us, event | category | flops | bytes accessed | tf_op | source)
XLA Modules:
  0.0 123.0 jit_solution(8268971945849036185)
XLA Ops:
  0.7 3.0 %collective-permute-start = (bf16[128,768]{1,0:T(8,128)(2,1)}, bf16[128,768]{1,0:T(8,128)(2,1)S(1)}, u32[]{:S(2)}, u32[]{:S(2)}) collective-permute-start(bf16[128,768]{1,0:T(8,128)(2,1)} %bitcast.63), channel_id=1, source_target_pairs={{0,4},{4,0},{1,5},{5,1},{2,6},{6,2},{3,7},{7,3},{8,12},{12,8},{9,1... | collective-permute-start | bytes 589832 | tf_op jit(solution)/shard_map/ppermute | solution.py:23
  3.7 1.5 %collective-permute-start.3 = (bf16[128,768]{1,0:T(8,128)(2,1)}, bf16[128,768]{1,0:T(8,128)(2,1)S(1)}, u32[]{:S(2)}, u32[]{:S(2)}) collective-permute-start(bf16[128,768]{1,0:T(8,128)(2,1)} %bitcast.66), channel_id=1, source_target_pairs={{0,2},{1,3},{2,0},{3,1},{4,6},{5,7},{6,4},{7,5},{8,10},{9,11},{10,... | collective-permute-start | bytes 589832 | tf_op jit(solution)/shard_map/ppermute | solution.py:23
  5.2 2.0 %pack_attention.1.refs_0_ = bf16[200,768]{1,0:T(8,128)(2,1)} custom-call(s32[1]{0:T(128)} %bitcast.24.dp_ref, bf16[3,192,192]{2,1,0:T(8,128)(2,1)} %bitcast.83, bf16[192,192]{1,0:T(8,128)(2,1)} %output_ref.1, bf16[3,3,16]{2,1,0:T(4,128)(2,1)} %bias_ref.1, bf16[192]{0:T(256)(128)(2,1)} %refs_0_.1, bf16[192]{0:T(256)(128)(2,1)} %refs_1_.1, ...), custom_call_target="tpu_custom_call" | custom-call | bytes 297888 | tf_op jit(solution)/shard_map/pack_attention/pallas_call | solution.py:370
  7.2 1.6 %collective-permute-start.6 = (bf16[200,768]{1,0:T(8,128)(2,1)}, bf16[200,768]{1,0:T(8,128)(2,1)}, u32[]{:S(2)}, u32[]{:S(2)}) collective-permute-start(bf16[200,768]{1,0:T(8,128)(2,1)} %pack_attention.1.refs_0_), channel_id=1, source_target_pairs={{0,8},{8,16},{16,24},{24,0},{1,9},{9,17},{17,25},{25,1},{2,10},{10... | collective-permute-start | bytes 921608 | tf_op jit(solution)/shard_map/ppermute | solution.py:49
  8.8 2.2 %collective-permute-start.7 = (bf16[200,768]{1,0:T(8,128)(2,1)}, bf16[200,768]{1,0:T(8,128)(2,1)S(1)}, u32[]{:S(2)}, u32[]{:S(2)}) collective-permute-start(bf16[200,768]{1,0:T(8,128)(2,1)} %pack_attention.1.refs_0_), channel_id=1, source_target_pairs={{0,24},{8,0},{16,8},{24,16},{1,25},{9,1},{17,9},{25,17},{2,26},{10... | collective-permute-start | bytes 921608 | tf_op jit(solution)/shard_map/ppermute | solution.py:49
  13.4 8.5 %collective-permute-done.1 = bf16[2,128,768]{2,1,0:T(8,128)(2,1)S(1)} collective-permute-done((bf16[2,128,768]{2,1,0:T(8,128)(2,1)S(1)}, bf16[2,128,768]{2,1,0:T(8,128)(2,1)S(1)}, u32[]{:S(2)}, u32[]{:S(2)}) %collective-permute-start.1) | collective-permute-done | bytes 393248 | tf_op jit(solution)/shard_map/ppermute | solution.py:23
  24.5 2.2 %pack_feed.1 = bf16[4,384,384]{2,1,0:T(8,128)(2,1)} custom-call(s32[1]{0:T(128)} %bitcast.1.ctx_ref.bit_ref, bf16[192,768]{1,0:T(8,128)(2,1)} %up_ref.1, bf16[192,768]{1,0:T(8,128)(2,1)} %bitcast.84), custom_call_target="tpu_custom_call" | custom-call | bytes 589824 | tf_op jit(solution)/shard_map/pack_feed/pallas_call | solution.py:370
  29.3 4.6 %all-to-all-start = ((bf16[4,384,384]{2,1,0:T(8,128)(2,1)}), bf16[4,384,384]{2,1,0:T(8,128)(2,1)}, u32[]{:S(2)}, u32[]{:S(2)}) async-start(bf16[4,384,384]{2,1,0:T(8,128)(2,1)} %pack_feed.1), calls=%async_computation | async-start | bytes 2359296 | tf_op jit(solution)/shard_map/all_to_all | solution.py:53
  33.8 1.7 %maximum_select_fusion.1 = bf16[2,2,2,128,768]{4,3,1,2,0:T(8,128)(2,1)S(1)} fusion(bf16[2,2,1,128,768]{4,3,1,2,0:T(8,128)(2,1)S(1)} %maximum_select_fusion.5, bf16[2,2,1,128,768]{4,3,1,2,0:T(8,128)(2,1)} %bitcast.20, pred[]{:T(512)S(6)} %gt.15), kind=kLoop, calls=%fused_computation.7 | loop fusion | flops 2359296 | bytes 3145729 | tf_op jit(solution)/shard_map/jit(_where)/select_n | solution.py:27
  37.7 2.1 %fusion.refs_4_.normed_ref = f32[1024,768]{1,0:T(8,128)} fusion(bf16[1024,768]{1,0:T(8,128)(2,1)S(1)} %bitcast.62, f32[1024]{0:T(1024)S(1)} %add_rsqrt_fusion, f32[1024]{0:T(1024)S(1)} %broadcast_multiply_fusion), kind=kLoop, calls=%fused_computation.2 | loop fusion | flops 2359296 | bytes 4726784 | tf_op jit(solution)/shard_map/mul | solution.py:443
  39.8 19.6 %attention_part.1 = (f32[8,768]{1,0:T(8,128)}, bf16[768,768]{1,0:T(8,128)(2,1)}, bf16[768,1024]{1,0:T(8,128)(2,1)}, f32[16,64]{1,0:T(8,128)}, bf16[192,384]{1,0:...) custom-call(s32[1]{0:T(128)} %bitcast.1.ctx_ref.bit_ref, ...), custom_call_target="tpu_custom_call" | custom-call | flops 4831838208 | bytes 6017024 | tf_op jit(solution)/shard_map/attention_part/pallas_call | solution.py:370
  59.4 2.0 %collective-permute-start.9 = (bf16[192,384]{1,0:T(8,128)(2,1)}, bf16[192,384]{1,0:T(8,128)(2,1)}, u32[]{:S(2)}, u32[]{:S(2)}) collective-permute-start(bf16[192,384]{1,0:T(8,128)(2,1)} %get-tuple-element.59), channel_id=1, source_target_pairs={{0,8},{8,16},{16,24},{24,0},{1,9},{9,17},{17,25},{25,1},{2,10},{10... | collective-permute-start | bytes 442376 | tf_op jit(solution)/shard_map/ppermute | solution.py:49
  61.4 2.4 %collective-permute-start.10 = (bf16[192,384]{1,0:T(8,128)(2,1)}, bf16[192,384]{1,0:T(8,128)(2,1)S(1)}, u32[]{:S(2)}, u32[]{:S(2)}) collective-permute-start(bf16[192,384]{1,0:T(8,128)(2,1)} %get-tuple-element.60), channel_id=1, source_target_pairs={{0,16},{8,24},{16,0},{24,8},{1,17},{9,25},{17,1},{25,9},{2,18},{10... | collective-permute-start | bytes 442376 | tf_op jit(solution)/shard_map/ppermute | solution.py:49
  63.8 1.5 %collective-permute-start.11 = (bf16[192,384]{1,0:T(8,128)(2,1)}, bf16[192,384]{1,0:T(8,128)(2,1)S(1)}, u32[]{:S(2)}, u32[]{:S(2)}) collective-permute-start(bf16[192,384]{1,0:T(8,128)(2,1)} %get-tuple-element.61), channel_id=1, source_target_pairs={{0,24},{8,0},{16,8},{24,16},{1,25},{9,1},{17,9},{25,17},{2,26},{10... | collective-permute-start | bytes 442376 | tf_op jit(solution)/shard_map/ppermute | solution.py:49
  65.3 11.3 %feed_part.1 = (bf16[2,512,768]{2,1,0:T(8,128)(2,1)}, bf16[2,512,768]{2,1,0:T(8,128)(2,1)}, bf16[4,392,384]{2,1,0:T(8,128)(2,1)}, f32[8,768]{1,0:T(8,128)}) custom-call(s32[1]{0:T(128)} %bitcast.1.ctx_ref.bit_ref, s32[1]{0:T(128)} %bitcast.3.low_ref, bf16[4,384,384]{2,1,0:T(8,128)(2,1)} %all-to-all-done.all_ref, f32[1024,768]{1,0:T(8,128)} %fusion.refs_4_.normed_ref, ...), custom_call_target="tpu_custom_call" | custom-call | flops 3623878656 | bytes 8679424 | tf_op jit(solution)/shard_map/feed_part/pallas_call | solution.py:370
  77.3 3.5 %all-to-all-start.1 = ((bf16[4,392,384]{2,1,0:T(8,128)(2,1)}), bf16[4,392,384]{2,1,0:T(8,128)(2,1)S(1)}, u32[]{:S(2)}, u32[]{:S(2)}) async-start(bf16[4,392,384]{2,1,0:T(8,128)(2,1)} %get-tuple-element.72), calls=%async_computation.1 | async-start | bytes 2408448 | tf_op jit(solution)/shard_map/all_to_all | solution.py:53
  84.1 3.3 %split.1 = (bf16[256,768]{1,0:T(8,128)(2,1)}, bf16[256,768]{1,0:T(8,128)(2,1)}, bf16[256,768]{1,0:T(8,128)(2,1)}, bf16[256,768]{1,0:T(8,128)(2,1)}) custom-call(s32[1]{0:T(128)} %bitcast.2.high_ref.bit_ref, s32[1]{0:T(128)} %bitcast.1.ctx_ref.bit_ref, bf16[2,512,768]{2,1,0:T(8,128)(2,1)} %get-tuple-element.62.kept_ref, bf16[2,512,768]{2,1,0:T(8,128)(2,1)} %copy-done.2), custom_call_target="tpu_custom_call" | custom-call | bytes 3145728 | tf_op jit(solution)/shard_map/split/pallas_call | solution.py:370
  91.7 6.7 %collective-permute-done.13.got_ref = bf16[256,768]{1,0:T(8,128)(2,1)} collective-permute-done((bf16[256,768]{1,0:T(8,128)(2,1)}, bf16[256,768]{1,0:T(8,128)(2,1)}, u32[]{:S(2)}, u32[]{:S(2)}) %collective-permute-start.13) | collective-permute-done | bytes 393248 | tf_op jit(solution)/shard_map/ppermute | solution.py:23
  98.4 2.0 %halve_mixed.1 = (f32[128,768]{1,0:T(8,128)}, bf16[128,768]{1,0:T(8,128)(2,1)}) custom-call(s32[1]{0:T(128)} %bitcast.1.ctx_ref.bit_ref, bf16[256,768]{1,0:T(8,128)(2,1)} %get-tuple-element.64.kept_ref, bf16[256,768]{1,0:T(8,128)(2,1)} %collective-permute-done.13.got_ref), custom_call_target="tpu_custom_call" | custom-call | bytes 786432 | tf_op jit(solution)/shard_map/halve_mixed/pallas_call | solution.py:370
  100.3 1.5 %collective-permute-start.14 = (bf16[128,768]{1,0:T(8,128)(2,1)}, bf16[128,768]{1,0:T(8,128)(2,1)S(1)}, u32[]{:S(2)}, u32[]{:S(2)}) collective-permute-start(bf16[128,768]{1,0:T(8,128)(2,1)} %get-tuple-element.67), channel_id=1, source_target_pairs={{0,4},{4,0},{1,5},{5,1},{2,6},{6,2},{3,7},{7,3},{8,12},{12,8},{9,1... | collective-permute-start | bytes 589832 | tf_op jit(solution)/shard_map/ppermute | solution.py:23
  102.7 2.0 %halve_grad.1 = (f32[128,768]{1,0:T(8,128)}, bf16[128,768]{1,0:T(8,128)(2,1)}) custom-call(s32[1]{0:T(128)} %bitcast.2.high_ref.bit_ref, bf16[256,768]{1,0:T(8,128)(2,1)} %get-tuple-element.68.kept_ref, bf16[256,768]{1,0:T(8,128)(2,1)} %collective-permute-done.15.got_ref), custom_call_target="tpu_custom_call" | custom-call | bytes 786432 | tf_op jit(solution)/shard_map/halve_grad/pallas_call | solution.py:370
  106.3 4.3 %collective-permute-done.16 = bf16[128,768]{1,0:T(8,128)(2,1)S(1)} collective-permute-done((bf16[128,768]{1,0:T(8,128)(2,1)}, bf16[128,768]{1,0:T(8,128)(2,1)S(1)}, u32[]{:S(2)}, u32[]{:S(2)}) %collective-permute-start.16) | collective-permute-done | bytes 196640 | tf_op jit(solution)/shard_map/ppermute | solution.py:23
  113.5 1.5 %collective-permute-start.21 = (bf16[384,384]{1,0:T(8,128)(2,1)S(1)}, bf16[384,384]{1,0:T(8,128)(2,1)S(1)}, u32[]{:S(2)}, u32[]{:S(2)}) collective-permute-start(bf16[384,384]{1,0:T(8,128)(2,1)S(1)} %fusion.3), channel_id=1, source_target_pairs={{0,4},{4,0},{1,5},{5,1},{2,6},{6,2},{3,7},{7,3},{8,12},{12,8},{9,1... | collective-permute-start | bytes 884744 | tf_op jit(solution)/shard_map/ppermute | solution.py:23
  117.1 2.3 %collective-permute-done.18 = f32[3,384]{1,0:T(4,128)S(1)} collective-permute-done((f32[3,384]{1,0:T(4,128)S(1)}, f32[3,384]{1,0:T(4,128)S(1)}, u32[]{:S(2)}, u32[]{:S(2)}) %collective-permute-start.18) | collective-permute-done | bytes 4640 | tf_op jit(solution)/shard_map/ppermute | solution.py:23
  (103 shorter events, 28.8 us)
Async XLA Ops:
  0.7 10.4 %collective-permute-start = (bf16[128,768]{1,0:T(8,128)(2,1)}, bf16[128,768]{1,0:T(8,128)(2,1)S(1)}, u32[]{:S(2)}, u32[]{:S(2)}) collective-permute-start(bf16[128,768]{1,0:T(8,128)(2,1)} %bitcast.63), channel_id=1, source_target_pairs={{0,4},{4,0},{1,5},{5,1},{2,6},{6,2},{3,7},{7,3},{8,12},{12,8},{9,1... | collective-permute-start | bytes 589832 | tf_op jit(solution)/shard_map/ppermute | solution.py:23
  3.7 9.0 %collective-permute-start.3 = (bf16[128,768]{1,0:T(8,128)(2,1)}, bf16[128,768]{1,0:T(8,128)(2,1)S(1)}, u32[]{:S(2)}, u32[]{:S(2)}) collective-permute-start(bf16[128,768]{1,0:T(8,128)(2,1)} %bitcast.66), channel_id=1, source_target_pairs={{0,2},{1,3},{2,0},{3,1},{4,6},{5,7},{6,4},{7,5},{8,10},{9,11},{10,... | collective-permute-start | bytes 589832 | tf_op jit(solution)/shard_map/ppermute | solution.py:23
  7.2 19.6 %collective-permute-start.6 = (bf16[200,768]{1,0:T(8,128)(2,1)}, bf16[200,768]{1,0:T(8,128)(2,1)}, u32[]{:S(2)}, u32[]{:S(2)}) collective-permute-start(bf16[200,768]{1,0:T(8,128)(2,1)} %pack_attention.1.refs_0_), channel_id=1, source_target_pairs={{0,8},{8,16},{16,24},{24,0},{1,9},{9,17},{17,25},{25,1},{2,10},{10... | collective-permute-start | bytes 921608 | tf_op jit(solution)/shard_map/ppermute | solution.py:49
  8.8 18.0 %collective-permute-start.7 = (bf16[200,768]{1,0:T(8,128)(2,1)}, bf16[200,768]{1,0:T(8,128)(2,1)S(1)}, u32[]{:S(2)}, u32[]{:S(2)}) collective-permute-start(bf16[200,768]{1,0:T(8,128)(2,1)} %pack_attention.1.refs_0_), channel_id=1, source_target_pairs={{0,24},{8,0},{16,8},{24,16},{1,25},{9,1},{17,9},{25,17},{2,26},{10... | collective-permute-start | bytes 921608 | tf_op jit(solution)/shard_map/ppermute | solution.py:49
  12.1 9.9 %collective-permute-start.1 = (bf16[2,128,768]{2,1,0:T(8,128)(2,1)S(1)}, bf16[2,128,768]{2,1,0:T(8,128)(2,1)S(1)}, u32[]{:S(2)}, u32[]{:S(2)}) collective-permute-start(bf16[2,128,768]{2,1,0:T(8,128)(2,1)S(1)} %maximum_select_fusion.7), channel_id=1, source_target_pairs={{0,2},{1,3},{2,0},{3,1},{4,6},{5,7},{6,4},{7,5},{8,10},{9,11},{10,... | collective-permute-start | bytes 1179656 | tf_op jit(solution)/shard_map/ppermute | solution.py:23
  12.8 10.2 %collective-permute-start.4 = (bf16[2,128,768]{2,1,0:T(8,128)(2,1)S(1)}, bf16[2,128,768]{2,1,0:T(8,128)(2,1)S(1)}, u32[]{:S(2)}, u32[]{:S(2)}) collective-permute-start(bf16[2,128,768]{2,1,0:T(8,128)(2,1)S(1)} %maximum_select_fusion.8), channel_id=1, source_target_pairs={{0,4},{4,0},{1,5},{5,1},{2,6},{6,2},{3,7},{7,3},{8,12},{12,8},{9,1... | collective-permute-start | bytes 1179656 | tf_op jit(solution)/shard_map/ppermute | solution.py:23
  23.0 4.7 %collective-permute-start.2 = (bf16[2,2,128,768]{3,2,0,1:T(8,128)(2,1)}, bf16[2,2,128,768]{3,2,0,1:T(8,128)(2,1)}, u32[]{:S(2)}, u32[]{:S(2)}) collective-permute-start(bf16[2,2,128,768]{3,2,0,1:T(8,128)(2,1)} %maximum_select_fusion.2), channel_id=1, source_target_pairs={{0,1},{1,0},{2,3},{3,2},{4,5},{5,4},{6,7},{7,6},{8,9},{9,8},{10,11... | collective-permute-start | bytes 2359304 | tf_op jit(solution)/shard_map/ppermute | solution.py:23
  23.1 10.7 %collective-permute-start.5 = (bf16[2,2,128,768]{3,2,1,0:T(8,128)(2,1)S(1)}, bf16[2,2,128,768]{3,2,1,0:T(8,128)(2,1)}, u32[]{:S(2)}, u32[]{:S(2)}) collective-permute-start(bf16[2,2,128,768]{3,2,1,0:T(8,128)(2,1)S(1)} %maximum_select_fusion.4), channel_id=1, source_target_pairs={{0,1},{1,0},{2,3},{3,2},{4,5},{5,4},{6,7},{7,6},{8,9},{9,8},{10,11... | collective-permute-start | bytes 2359304 | tf_op jit(solution)/shard_map/ppermute | solution.py:23
  26.8 13.0 %collective-permute-start.8 = (bf16[200,768]{1,0:T(8,128)(2,1)}, bf16[200,768]{1,0:T(8,128)(2,1)}, u32[]{:S(2)}, u32[]{:S(2)}) collective-permute-start(bf16[200,768]{1,0:T(8,128)(2,1)} %collective-permute-done.6.refs_1_), channel_id=1, source_target_pairs={{0,8},{8,16},{16,24},{24,0},{1,9},{9,17},{17,25},{25,1},{2,10},{10... | collective-permute-start | bytes 921608 | tf_op jit(solution)/shard_map/ppermute | solution.py:49
  29.3 36.0 %all-to-all-start = ((bf16[4,384,384]{2,1,0:T(8,128)(2,1)}), bf16[4,384,384]{2,1,0:T(8,128)(2,1)}, u32[]{:S(2)}, u32[]{:S(2)}) async-start(bf16[4,384,384]{2,1,0:T(8,128)(2,1)} %pack_feed.1), calls=%async_computation | async-start | bytes 2359296 | tf_op jit(solution)/shard_map/all_to_all | solution.py:53
  59.4 17.1 %collective-permute-start.9 = (bf16[192,384]{1,0:T(8,128)(2,1)}, bf16[192,384]{1,0:T(8,128)(2,1)}, u32[]{:S(2)}, u32[]{:S(2)}) collective-permute-start(bf16[192,384]{1,0:T(8,128)(2,1)} %get-tuple-element.59), channel_id=1, source_target_pairs={{0,8},{8,16},{16,24},{24,0},{1,9},{9,17},{17,25},{25,1},{2,10},{10... | collective-permute-start | bytes 442376 | tf_op jit(solution)/shard_map/ppermute | solution.py:49
  61.4 15.1 %collective-permute-start.10 = (bf16[192,384]{1,0:T(8,128)(2,1)}, bf16[192,384]{1,0:T(8,128)(2,1)S(1)}, u32[]{:S(2)}, u32[]{:S(2)}) collective-permute-start(bf16[192,384]{1,0:T(8,128)(2,1)} %get-tuple-element.60), channel_id=1, source_target_pairs={{0,16},{8,24},{16,0},{24,8},{1,17},{9,25},{17,1},{25,9},{2,18},{10... | collective-permute-start | bytes 442376 | tf_op jit(solution)/shard_map/ppermute | solution.py:49
  63.8 12.8 %collective-permute-start.11 = (bf16[192,384]{1,0:T(8,128)(2,1)}, bf16[192,384]{1,0:T(8,128)(2,1)S(1)}, u32[]{:S(2)}, u32[]{:S(2)}) collective-permute-start(bf16[192,384]{1,0:T(8,128)(2,1)} %get-tuple-element.61), channel_id=1, source_target_pairs={{0,24},{8,0},{16,8},{24,16},{1,25},{9,1},{17,9},{25,17},{2,26},{10... | collective-permute-start | bytes 442376 | tf_op jit(solution)/shard_map/ppermute | solution.py:49
  76.6 6.3 %collective-permute-start.12 = (bf16[2,512,768]{2,1,0:T(8,128)(2,1)}, bf16[2,512,768]{2,1,0:T(8,128)(2,1)S(1)}, u32[]{:S(2)}, u32[]{:S(2)}) collective-permute-start(bf16[2,512,768]{2,1,0:T(8,128)(2,1)} %get-tuple-element.63), channel_id=1, source_target_pairs={{0,1},{1,0},{2,3},{3,2},{4,5},{5,4},{6,7},{7,6},{8,9},{9,8},{10,11... | collective-permute-start | bytes 4718600 | tf_op jit(solution)/shard_map/ppermute | solution.py:23
  77.3 34.3 %all-to-all-start.1 = ((bf16[4,392,384]{2,1,0:T(8,128)(2,1)}), bf16[4,392,384]{2,1,0:T(8,128)(2,1)S(1)}, u32[]{:S(2)}, u32[]{:S(2)}) async-start(bf16[4,392,384]{2,1,0:T(8,128)(2,1)} %get-tuple-element.72), calls=%async_computation.1 | async-start | bytes 2408448 | tf_op jit(solution)/shard_map/all_to_all | solution.py:53
  82.3 7.9 %collective-permute-start.20 = (bf16[192,384]{1,0:T(8,128)(2,1)S(1)}, bf16[192,384]{1,0:T(8,128)(2,1)S(1)}, u32[]{:S(2)}, u32[]{:S(2)}) collective-permute-start(bf16[192,384]{1,0:T(8,128)(2,1)S(1)} %reduce-precision_convert_fusion), channel_id=1, source_target_pairs={{0,4},{4,0},{1,5},{5,1},{2,6},{6,2},{3,7},{7,3},{8,12},{12,8},{9,1... | collective-permute-start | bytes 442376 | tf_op jit(solution)/shard_map/ppermute | solution.py:23
  87.4 11.0 %collective-permute-start.13 = (bf16[256,768]{1,0:T(8,128)(2,1)}, bf16[256,768]{1,0:T(8,128)(2,1)}, u32[]{:S(2)}, u32[]{:S(2)}) collective-permute-start(bf16[256,768]{1,0:T(8,128)(2,1)} %get-tuple-element.65), channel_id=1, source_target_pairs={{0,2},{1,3},{2,0},{3,1},{4,6},{5,7},{6,4},{7,5},{8,10},{9,11},{10,... | collective-permute-start | bytes 1179656 | tf_op jit(solution)/shard_map/ppermute | solution.py:23
  88.8 13.9 %collective-permute-start.15 = (bf16[256,768]{1,0:T(8,128)(2,1)}, bf16[256,768]{1,0:T(8,128)(2,1)}, u32[]{:S(2)}, u32[]{:S(2)}) collective-permute-start(bf16[256,768]{1,0:T(8,128)(2,1)} %get-tuple-element.69), channel_id=1, source_target_pairs={{0,4},{4,0},{1,5},{5,1},{2,6},{6,2},{3,7},{7,3},{8,12},{12,8},{9,1... | collective-permute-start | bytes 1179656 | tf_op jit(solution)/shard_map/ppermute | solution.py:23
  100.3 5.9 %collective-permute-start.14 = (bf16[128,768]{1,0:T(8,128)(2,1)}, bf16[128,768]{1,0:T(8,128)(2,1)S(1)}, u32[]{:S(2)}, u32[]{:S(2)}) collective-permute-start(bf16[128,768]{1,0:T(8,128)(2,1)} %get-tuple-element.67), channel_id=1, source_target_pairs={{0,4},{4,0},{1,5},{5,1},{2,6},{6,2},{3,7},{7,3},{8,12},{12,8},{9,1... | collective-permute-start | bytes 589832 | tf_op jit(solution)/shard_map/ppermute | solution.py:23
  104.7 5.9 %collective-permute-start.16 = (bf16[128,768]{1,0:T(8,128)(2,1)}, bf16[128,768]{1,0:T(8,128)(2,1)S(1)}, u32[]{:S(2)}, u32[]{:S(2)}) collective-permute-start(bf16[128,768]{1,0:T(8,128)(2,1)} %get-tuple-element.71), channel_id=1, source_target_pairs={{0,2},{1,3},{2,0},{3,1},{4,6},{5,7},{6,4},{7,5},{8,10},{9,11},{10,... | collective-permute-start | bytes 589832 | tf_op jit(solution)/shard_map/ppermute | solution.py:23
  111.9 3.8 %collective-permute-start.17 = (f32[4,384]{1,0:T(4,128)S(1)}, f32[4,384]{1,0:T(4,128)S(1)}, u32[]{:S(2)}, u32[]{:S(2)}) collective-permute-start(f32[4,384]{1,0:T(4,128)S(1)} %slice_add_fusion.1), channel_id=1, source_target_pairs={{0,4},{4,0},{1,5},{5,1},{2,6},{6,2},{3,7},{7,3},{8,12},{12,8},{9,1... | collective-permute-start | bytes 18440 | tf_op jit(solution)/shard_map/ppermute | solution.py:23
  113.5 7.7 %collective-permute-start.21 = (bf16[384,384]{1,0:T(8,128)(2,1)S(1)}, bf16[384,384]{1,0:T(8,128)(2,1)S(1)}, u32[]{:S(2)}, u32[]{:S(2)}) collective-permute-start(bf16[384,384]{1,0:T(8,128)(2,1)S(1)} %fusion.3), channel_id=1, source_target_pairs={{0,4},{4,0},{1,5},{5,1},{2,6},{6,2},{3,7},{7,3},{8,12},{12,8},{9,1... | collective-permute-start | bytes 884744 | tf_op jit(solution)/shard_map/ppermute | solution.py:23
  115.7 3.6 %collective-permute-start.18 = (f32[3,384]{1,0:T(4,128)S(1)}, f32[3,384]{1,0:T(4,128)S(1)}, u32[]{:S(2)}, u32[]{:S(2)}) collective-permute-start(f32[3,384]{1,0:T(4,128)S(1)} %slice_add_fusion), channel_id=1, source_target_pairs={{0,2},{1,3},{2,0},{3,1},{4,6},{5,7},{6,4},{7,5},{8,10},{9,11},{10,... | collective-permute-start | bytes 13832 | tf_op jit(solution)/shard_map/ppermute | solution.py:23
  119.3 1.2 collective-permute-start.19
  (9 other events, 39.7 us)
